TPU v7x, 32 devices: a whole 2x2x4 slice. The times are simulated.
32 devices in a mesh: dp: 8 (over y, x, core), mp: 4 (over z).
Axes of the slice: x: 2, y: 2, z: 4, core: 2. Of those that a mesh axis runs over, the one named last changes fastest.
Arguments:
- tokens: bfloat16 [16384, 768], P(('dp', 'mp')), may hold values from -6 to 6
- segment_ids: int32 [32, 512], P('dp'), may hold values from 0 to 7, never falling along the last dimension, each value on 1 to 128 neighbouring positions
- query_weight: bfloat16 [768, 768], P(None, 'mp'), may hold values from -0.21875 to 0.21875
- query_bias: bfloat16 [768], P('mp'), may hold values from -3 to 3
- key_weight: bfloat16 [768, 768], P(None, 'mp'), may hold values from -0.21875 to 0.21875
- value_weight: bfloat16 [768, 768], P(None, 'mp'), may hold values from -0.21875 to 0.21875
- value_bias: bfloat16 [768], P('mp'), may hold values from -3 to 3
- output_weight: bfloat16 [768, 768], P('mp'), may hold values from -0.875 to 0.875
- output_bias: bfloat16 [768], replicated, may hold values from -3 to 3
- first_gain: bfloat16 [768], replicated, may hold values from 0.25 to 1.75
- first_shift: bfloat16 [768], replicated, may hold values from -3 to 3
- up_weight: bfloat16 [768, 3072], P(None, 'mp'), may hold values from -0.21875 to 0.21875
- up_bias: bfloat16 [3072], P('mp'), may hold values from -3 to 3
- down_weight: bfloat16 [3072, 768], P('mp'), may hold values from -0.21875 to 0.21875
- down_bias: bfloat16 [768], replicated, may hold values from -3 to 3
- second_gain: bfloat16 [768], replicated, may hold values from 0.25 to 1.75
- second_shift: bfloat16 [768], replicated, may hold values from -3 to 3
- cotangent: bfloat16 [16384, 768], P(('dp', 'mp')), may hold values from -6 to 6
Outputs:
- output: bfloat16 [16384, 768], P(('dp', 'mp'))
- input_grad: bfloat16 [16384, 768], P(('dp', 'mp'))
- query_weight_grad: float32 [768, 768], P(None, 'mp')
- query_bias_grad: float32 [768], P('mp')
- key_weight_grad: float32 [768, 768], P(None, 'mp')
- value_weight_grad: float32 [768, 768], P(None, 'mp')
- value_bias_grad: float32 [768], P('mp')
- output_weight_grad: float32 [768, 768], P('mp')
- output_bias_grad: float32 [768], replicated
- first_gain_grad: float32 [768], replicated
- first_shift_grad: float32 [768], replicated
- up_weight_grad: float32 [768, 3072], P(None, 'mp')
- up_bias_grad: float32 [3072], P('mp')
- down_weight_grad: float32 [3072, 768], P('mp')
- down_bias_grad: float32 [768], replicated
- second_gain_grad: float32 [768], replicated
- second_shift_grad: float32 [768], replicated
Inputs may be any that keep to these rules, and one draw needn't show every extreme that they name: `segment_ids`: along each row of 512 tokens the ids never fall; each passage holds 1 to 128 tokens, and some passage holds exactly 128.
All inputs are finite; a program needn't handle non-finite values.
Results may differ from a plain program's by a relative error of at most 0.023.
Values may be sent and summed in bfloat16 or wider, within the bound.
No kernel may reach another device: no remote copies, remote signals or barrier semaphores. Data moves between devices by JAX's collectives and lax.ppermute only.
A program may use at most 128 MiB of HBM per device.

v0:
```python
import math

import jax
import jax.numpy as jnp
from jax import lax
from jax.sharding import PartitionSpec as P

HEAD_DIM = 64


epsilon = 1e-05


def inner_rows(left, right):
    return lax.dot_general(
        left, right, (((0,), (0,)), ((), ())), preferred_element_type=jnp.float32
    )


def outer_cols(left, right):
    return lax.dot_general(
        left, right, (((1,), (1,)), ((), ())), preferred_element_type=jnp.float32
    )


def norm_forward(total, norm_gain, norm_shift):
    average = jnp.mean(total, axis=-1, keepdims=True)
    centred = total - average
    inverse = lax.rsqrt(jnp.mean(centred * centred, axis=-1, keepdims=True) + epsilon)
    normal = centred * inverse
    return (normal * norm_gain + norm_shift, normal, inverse)


def norm_backward(grad_out, normal, inverse, norm_gain):
    scaled = grad_out * norm_gain
    return inverse * (
        scaled
        - jnp.mean(scaled, axis=-1, keepdims=True)
        - normal * jnp.mean(scaled * normal, axis=-1, keepdims=True)
    )


def gelu_slope(hidden):
    cumulative = 0.5 * (1.0 + lax.erf(hidden * 0.7071067811865476))
    density = jnp.exp(-0.5 * hidden * hidden) * 0.3989422804014327
    return cumulative + hidden * density


def masked_scores(queries, key_vecs, segment_row):
    scale_factor = 1.0 / math.sqrt(queries.shape[-1])
    scores = (
        jnp.einsum("qhd,khd->hqk", queries, key_vecs, preferred_element_type=jnp.float32)
        * scale_factor
    )
    allowed = segment_row[:, None] == segment_row[None, :]
    return jnp.where(allowed[None], scores, -1e30)


def row_forward(pieces):
    queries, key_vecs, values, segment_row = pieces
    masked = masked_scores(queries, key_vecs, segment_row)
    highest_score = jnp.max(masked, axis=-1, keepdims=True)
    expo = jnp.exp(masked - highest_score)
    denominator = jnp.sum(expo, axis=-1, keepdims=True)
    probs = (expo / denominator).astype(jnp.bfloat16)
    context = jnp.einsum("hqk,khd->qhd", probs, values, preferred_element_type=jnp.float32)
    log_total = highest_score[..., 0] + jnp.log(denominator[..., 0])
    return (context.astype(jnp.bfloat16), log_total)


def row_backward(pieces):
    queries, key_vecs, values, segment_row, log_total, grad_context = pieces
    scale_factor = 1.0 / math.sqrt(queries.shape[-1])
    masked = masked_scores(queries, key_vecs, segment_row)
    probs = jnp.exp(masked - log_total[..., None])
    grad_probs = jnp.einsum(
        "qhd,khd->hqk", grad_context, values, preferred_element_type=jnp.float32
    )
    grad_values = jnp.einsum(
        "hqk,qhd->khd", probs.astype(jnp.bfloat16), grad_context, preferred_element_type=jnp.float32
    )
    inner = jnp.sum(grad_probs * probs, axis=-1, keepdims=True)
    grad_scores = (probs * (grad_probs - inner)).astype(jnp.bfloat16)
    grad_queries = (
        jnp.einsum("hqk,khd->qhd", grad_scores, key_vecs, preferred_element_type=jnp.float32)
        * scale_factor
    )
    grad_keys = (
        jnp.einsum("hqk,qhd->khd", grad_scores, queries, preferred_element_type=jnp.float32)
        * scale_factor
    )
    return (
        grad_queries.astype(jnp.bfloat16),
        grad_keys.astype(jnp.bfloat16),
        grad_values.astype(jnp.bfloat16),
    )


def shards(
    tokens,
    segment_ids,
    query_weight,
    query_bias,
    key_weight,
    value_weight,
    value_bias,
    output_weight,
    output_bias,
    first_gain,
    first_shift,
    up_weight,
    up_bias,
    down_weight,
    down_bias,
    second_gain,
    second_shift,
    cotangent,
):
    row_count, row_length = segment_ids.shape
    head_width = query_weight.shape[1]
    local_heads = head_width // HEAD_DIM

    def by_heads(array):
        return array.reshape(row_count, row_length, local_heads, HEAD_DIM)

    def flat(array):
        return array.reshape(row_count * row_length, head_width)

    group_tokens = lax.all_gather(tokens, "mp", axis=0, tiled=True)
    queries = (
        jnp.dot(group_tokens, query_weight, preferred_element_type=jnp.float32) + query_bias
    ).astype(jnp.bfloat16)
    key_vecs = jnp.dot(group_tokens, key_weight, preferred_element_type=jnp.float32).astype(
        jnp.bfloat16
    )
    values = (
        jnp.dot(group_tokens, value_weight, preferred_element_type=jnp.float32) + value_bias
    ).astype(jnp.bfloat16)
    contexts, log_totals = lax.map(
        row_forward, (by_heads(queries), by_heads(key_vecs), by_heads(values), segment_ids)
    )
    contexts = flat(contexts)
    rows = contexts
    attended = (
        lax.psum_scatter(
            jnp.dot(rows, output_weight, preferred_element_type=jnp.float32).astype(jnp.bfloat16),
            "mp",
            scatter_dimension=0,
            tiled=True,
        ).astype(jnp.float32)
        + output_bias
    )
    gain_one = first_gain.astype(jnp.float32)
    gain_two = second_gain.astype(jnp.float32)
    normed_one, normal_one, inverse_one = norm_forward(
        tokens.astype(jnp.float32) + attended, gain_one, first_shift.astype(jnp.float32)
    )
    group_normed = lax.all_gather(normed_one.astype(jnp.bfloat16), "mp", axis=0, tiled=True)
    hidden = jnp.dot(group_normed, up_weight, preferred_element_type=jnp.float32) + up_bias
    activated = jax.nn.gelu(hidden, approximate=False).astype(jnp.bfloat16)
    rows = activated
    mixed = (
        lax.psum_scatter(
            jnp.dot(rows, down_weight, preferred_element_type=jnp.float32).astype(jnp.bfloat16),
            "mp",
            scatter_dimension=0,
            tiled=True,
        ).astype(jnp.float32)
        + down_bias
    )
    result, normal_two, inverse_two = norm_forward(
        normed_one + mixed, gain_two, second_shift.astype(jnp.float32)
    )
    grad_out = cotangent.astype(jnp.float32)
    grad_second_gain = jnp.sum(grad_out * normal_two, axis=0)
    grad_second_shift = jnp.sum(grad_out, axis=0)
    grad_two = norm_backward(grad_out, normal_two, inverse_two, gain_two)
    grad_mixed = grad_two.astype(jnp.bfloat16)
    grad_down_bias = jnp.sum(grad_mixed.astype(jnp.float32), axis=0)
    group_grad_mixed = lax.all_gather(grad_mixed, "mp", axis=0, tiled=True)
    grad_down = inner_rows(activated, group_grad_mixed)
    grad_active = outer_cols(group_grad_mixed, down_weight)
    grad_hidden = (grad_active * gelu_slope(hidden)).astype(jnp.bfloat16)
    grad_up_bias = jnp.sum(grad_hidden.astype(jnp.float32), axis=0)
    grad_up = inner_rows(group_normed, grad_hidden)
    rows = grad_hidden
    grad_normed = (
        lax.psum_scatter(
            outer_cols(rows, up_weight).astype(jnp.bfloat16), "mp", scatter_dimension=0, tiled=True
        ).astype(jnp.float32)
        + grad_two
    )
    grad_first_gain = jnp.sum(grad_normed * normal_one, axis=0)
    grad_first_shift = jnp.sum(grad_normed, axis=0)
    grad_one = norm_backward(grad_normed, normal_one, inverse_one, gain_one)
    grad_attended = grad_one.astype(jnp.bfloat16)
    grad_output_bias = jnp.sum(grad_attended.astype(jnp.float32), axis=0)
    group_grad_att = lax.all_gather(grad_attended, "mp", axis=0, tiled=True)
    grad_output = inner_rows(contexts, group_grad_att)
    grad_contexts = outer_cols(group_grad_att, output_weight).astype(jnp.bfloat16)
    grad_queries, grad_keys, grad_values = lax.map(
        row_backward,
        (
            by_heads(queries),
            by_heads(key_vecs),
            by_heads(values),
            segment_ids,
            log_totals,
            by_heads(grad_contexts),
        ),
    )
    grad_queries = flat(grad_queries)
    grad_keys = flat(grad_keys)
    grad_values = flat(grad_values)
    grad_query_bias = jnp.sum(grad_queries.astype(jnp.float32), axis=0)
    grad_value_bias = jnp.sum(grad_values.astype(jnp.float32), axis=0)
    grad_query = inner_rows(group_tokens, grad_queries)
    grad_key = inner_rows(group_tokens, grad_keys)
    grad_value = inner_rows(group_tokens, grad_values)
    part_query = outer_cols(grad_queries, query_weight)
    part_key = outer_cols(grad_keys, key_weight)
    part_value = outer_cols(grad_values, value_weight)
    grad_tokens = (
        lax.psum_scatter(
            (part_query + part_key + part_value).astype(jnp.bfloat16),
            "mp",
            scatter_dimension=0,
            tiled=True,
        ).astype(jnp.float32)
        + grad_one
    )
    (
        grad_query,
        grad_query_bias,
        grad_key,
        grad_value,
        grad_value_bias,
        grad_output,
        grad_up,
        grad_up_bias,
        grad_down,
    ) = lax.psum(
        (
            grad_query,
            grad_query_bias,
            grad_key,
            grad_value,
            grad_value_bias,
            grad_output,
            grad_up,
            grad_up_bias,
            grad_down,
        ),
        "dp",
    )
    (
        grad_output_bias,
        grad_first_gain,
        grad_first_shift,
        grad_down_bias,
        grad_second_gain,
        grad_second_shift,
    ) = lax.psum(
        (
            grad_output_bias,
            grad_first_gain,
            grad_first_shift,
            grad_down_bias,
            grad_second_gain,
            grad_second_shift,
        ),
        ("dp", "mp"),
    )
    return (
        result.astype(jnp.bfloat16),
        grad_tokens.astype(jnp.bfloat16),
        grad_query,
        grad_query_bias,
        grad_key,
        grad_value,
        grad_value_bias,
        grad_output,
        grad_output_bias,
        grad_first_gain,
        grad_first_shift,
        grad_up,
        grad_up_bias,
        grad_down,
        grad_down_bias,
        grad_second_gain,
        grad_second_shift,
    )


def solution(mesh):
    in_specs = (
        P(("dp", "mp"), None),
        P("dp", None),
        P(None, "mp"),
        P("mp"),
        P(None, "mp"),
        P(None, "mp"),
        P("mp"),
        P("mp", None),
        P(),
        P(),
        P(),
        P(None, "mp"),
        P("mp"),
        P("mp", None),
        P(),
        P(),
        P(),
        P(("dp", "mp"), None),
    )
    out_specs = (
        P(("dp", "mp"), None),
        P(("dp", "mp"), None),
        P(None, "mp"),
        P("mp"),
        P(None, "mp"),
        P(None, "mp"),
        P("mp"),
        P("mp", None),
        P(),
        P(),
        P(),
        P(None, "mp"),
        P("mp"),
        P("mp", None),
        P(),
        P(),
        P(),
    )
    return jax.shard_map(shards, mesh=mesh, in_specs=in_specs, out_specs=out_specs, check_vma=False)
```

profile of v0, /device:TPU:9, one launch (start us, length us, event | category | flops | bytes accessed | tf_op | source)
XLA Modules:
  0.0 787.0 jit_solution(2633334808695440258)
XLA Ops:
  9.3 62.5 %all-gather.5.cloned.1.call-done = bf16[2048,768]{1,0:T(8,128)(2,1)} async-done(((bf16[512,768]{1,0:T(8,128)(2,1)}), bf16[2048,768]{1,0:T(8,128)(2,1)}) %all-gather.5.cloned.1.call-update) | async-done | bytes 3145744 | tf_op jit(solution)/shard_map/all_gather | solution.py:129
  71.9 3.1 fusion.70
  76.6 3.1 fusion.71
  80.4 3.1 convolution_convert_fusion.4
  85.1 22.9 %while.26 = (s32[]{:T(128)}, bf16[4,512,3,64]{1,3,2,0:T(8,128)(2,1)}, f32[4,3,512]{2,1,0:T(4,128)}, bf16[4,512,3,64]{1,3,2,0:T(8,128)(2,1)}, s32[4,512]{1,0:T(4,...) while((s32[]{:T(128)}, bf16[4,512,3,64]{1,3,2,0:T(8,128)(2,1)}, ...), condition=%wide.region_3.4_spmd, body=%wide.region_0.3_spmd.sunk | while | flops 211122688 | bytes 11331685 | solution.py:139
  114.6 59.8 %reduce-scatter.5.cloned.1.call-done = bf16[512,768]{1,0:T(8,128)(2,1)} async-done(((bf16[2048,768]{1,0:T(8,128)(2,1)}), bf16[512,768]{1,0:T(8,128)(2,1)}) %reduce-scatter.5.cloned.1.call-update) | async-done | bytes 786448 | tf_op jit(solution)/shard_map/reduce_scatter | solution.py:145
  180.4 60.2 %all-gather.7.cloned.1.call-done = bf16[2048,768]{1,0:T(8,128)(2,1)} async-done(((bf16[512,768]{1,0:T(8,128)(2,1)}), bf16[2048,768]{1,0:T(8,128)(2,1)}) %all-gather.7.cloned.1.call-update) | async-done | bytes 3145744 | tf_op jit(solution)/shard_map/all_gather | solution.py:158
  240.5 17.9 %fusion.56 = (bf16[2048,768]{1,0:T(8,128)(2,1)S(1)}, f32[2048,768]{1,0:T(8,128)}) fusion(f32[768]{0:T(1024)} %convert_element_type.152, bf16[2048,768]{1,0:T(8,128)(2,1)} %all-gather.7.cloned.1.call-done, bf16[768,768]{1,0:T(8,128)(2,1)S(1)} %copy-done), kind=kOutput, calls=%fused_computation.66 | convolution fusion | flops 2519728128 | bytes 13765632 | tf_op jit(solution)/shard_map/dot_general | solution.py:159
  260.1 4.0 convolution_convert_fusion.1
  268.0 57.2 %reduce-scatter.7.cloned.1.call-done = bf16[512,768]{1,0:T(8,128)(2,1)} async-done(((bf16[2048,768]{1,0:T(8,128)(2,1)}), bf16[512,768]{1,0:T(8,128)(2,1)}) %reduce-scatter.7.cloned.1.call-update) | async-done | bytes 786448 | tf_op jit(solution)/shard_map/reduce_scatter | solution.py:163
  331.8 61.6 %all-gather.9.cloned.1.call-done = bf16[2048,768]{1,0:T(8,128)(2,1)} async-done(((bf16[512,768]{1,0:T(8,128)(2,1)}), bf16[2048,768]{1,0:T(8,128)(2,1)}) %all-gather.9.cloned.1.call-update) | async-done | bytes 3145744 | tf_op jit(solution)/shard_map/all_gather | solution.py:180
  393.4 7.5 convert_reduce_fusion
  402.6 4.0 convolution_convert_fusion
  406.9 60.8 %reduce-scatter.9.cloned.1.call-done = bf16[512,768]{1,0:T(8,128)(2,1)} async-done(((bf16[2048,768]{1,0:T(8,128)(2,1)}), bf16[512,768]{1,0:T(8,128)(2,1)}) %reduce-scatter.9.cloned.1.call-update) | async-done | bytes 786448 | tf_op jit(solution)/shard_map/reduce_scatter | solution.py:188
  467.7 3.2 multiply_reduce_fusion.1
  471.0 4.2 convert_reduce_fusion.3
  475.2 61.6 %all-gather.11.cloned.1.call-done = bf16[2048,768]{1,0:T(8,128)(2,1)} async-done(((bf16[512,768]{1,0:T(8,128)(2,1)}), bf16[2048,768]{1,0:T(8,128)(2,1)}) %all-gather.11.cloned.1.call-update) | async-done | bytes 3145744 | tf_op jit(solution)/shard_map/all_gather | solution.py:198
  536.9 3.0 convolution_convert_fusion.3
  545.6 34.5 %while.27 = (s32[]{:T(128)}, bf16[4,512,3,64]{1,3,2,0:T(8,128)(2,1)}, bf16[4,512,3,64]{1,3,2,0:T(8,128)(2,1)}, bf16[4,512,3,64]{1,3,2,0:T(8,128)(2,1)}, bf16[4,5...) while((s32[]{:T(128)}, ...), condition=%wide.region_17.18_spmd, body=%wide.region_15.17_spmd.sunk | while | flops 511146496 | bytes 26127484 | solution.py:201
  589.1 7.1 fusion.88
  596.2 4.2 fusion.87
  608.0 45.8 %all-reduce = (f32[768]{0:T(1024)}, f32[768]{0:T(1024)}, f32[768]{0:T(1024)}, f32[768]{0:T(1024)}, f32[768]{0:T(1024)}, /*index=5*/f32[768]{0:T(1024)}) all-reduce(f32[768]{0:T(1024)S(1)} %copy-done.34, f32[768]{0:T(1024)S(1)} %copy-done.32, f32[768]{0:T(1024)S(1)} %copy-done.33, ...), channel_id=1, replica_groups=mesh['dp'=8,'mp'=4] {'dp','mp'}, use_global_device_ids=true, to_apply=%region_28.29 | all-reduce | flops 4608 | bytes 36864 | tf_op jit(solution)/shard_map/psum | solution.py:263
  654.3 13.1 %all-reduce.1 = (f32[192]{0:T(256)}, f32[192]{0:T(256)}, f32[768]{0:T(1024)}) all-reduce(f32[192]{0:T(256)S(1)} %reduce_sum.184, f32[192]{0:T(256)S(1)} %reduce_sum.186, f32[768]{0:T(1024)S(1)} %copy-done.35), channel_id=1, replica_groups=mesh['dp'=8,'mp'=4] {'dp'}, use_global_device_ids=true, to_apply=%region_21.22 | all-reduce | flops 1152 | bytes 9216 | tf_op jit(solution)/shard_map/psum | solution.py:242
  669.7 100.8 %all-reduce.5.cloned.1.call-done = (f32[768,192]{0,1:T(8,128)}, f32[768,192]{0,1:T(8,128)}, f32[768,192]{0,1:T(8,128)}, f32[192,768]{1,0:T(8,128)}, f32[768,768]{1,0:T(8,128)}, /*index=5*/f32[768,768]{1,0:T(8,128)}) async-done(((f32[768,192]{0,1:T(8,128)}, f32[768,192]{0,1:T(8,128)}, f32[768,192]{0,1:T(8,128)}, f32[192,768]{1,0:T(8,128)}, f32[768,768]{1,0:T(8,128)}, /*index=5*/f32[768,768]{1,0:T(8,128)}), ...) | async-done | bytes 7077904 | tf_op jit(solution)/shard_map/psum | solution.py:242
  (230 shorter events, 124.3 us)
Async XLA Ops:
  7.2 233.4 %copy-start = (bf16[768,768]{1,0:T(8,128)(2,1)S(1)}, bf16[768,768]{1,0:T(8,128)(2,1)}, u32[]{:S(2)}) copy-start(bf16[768,768]{1,0:T(8,128)(2,1)} %param.33) | copy-start | bytes 3538948
  7.2 64.7 %all-gather.5.cloned.1.call-start = ((), (), s32[]{:S(2)}) async-start(), calls=%async_computation.4 | async-start | bytes 3932160 | tf_op jit(solution)/shard_map/all_gather | solution.py:129
  7.9 166.4 %reduce-scatter.5.cloned.1.call-start = ((), (), s32[]{:S(2)}) async-start(), calls=%async_computation.5 | async-start | bytes 3932160 | tf_op jit(solution)/shard_map/reduce_scatter | solution.py:145
  108.0 5.2 copy-start.7
  113.3 61.1 %copy-start.2 = (bf16[512,768]{1,0:T(8,128)(2,1)S(1)}, bf16[512,768]{1,0:T(8,128)(2,1)}, u32[]{:S(2)}) copy-start(bf16[512,768]{1,0:T(8,128)(2,1)} %param.22) | copy-start | bytes 2359300
  113.3 127.2 %all-gather.7.cloned.1.call-start = ((), (), s32[]{:S(2)}) async-start(), calls=%async_computation.6 | async-start | bytes 3932160 | tf_op jit(solution)/shard_map/all_gather | solution.py:158
  178.9 146.3 %reduce-scatter.7.cloned.1.call-start = ((), (), s32[]{:S(2)}) async-start(), calls=%async_computation.7 | async-start | bytes 3932160 | tf_op jit(solution)/shard_map/reduce_scatter | solution.py:163
  240.5 19.5 %copy-start.40 = (bf16[768,768]{1,0:T(8,128)(2,1)S(1)}, bf16[768,768]{1,0:T(8,128)(2,1)}, u32[]{:S(2)}) copy-start(bf16[768,768]{1,0:T(8,128)(2,1)} %param.35) | copy-start | bytes 3538948
  264.1 129.3 %all-gather.9.cloned.1.call-start = ((), (), s32[]{:S(2)}) async-start(), calls=%async_computation.8 | async-start | bytes 3932160 | tf_op jit(solution)/shard_map/all_gather | solution.py:180
  331.7 136.0 %reduce-scatter.9.cloned.1.call-start = ((), (), s32[]{:S(2)}) async-start(), calls=%async_computation.9 | async-start | bytes 3932160 | tf_op jit(solution)/shard_map/reduce_scatter | solution.py:188
  406.6 130.2 %all-gather.11.cloned.1.call-start = ((), (), s32[]{:S(2)}) async-start(), calls=%async_computation.10 | async-start | bytes 3932160 | tf_op jit(solution)/shard_map/all_gather | solution.py:198
  471.0 65.9 %copy-start.24 = (bf16[192,768]{1,0:T(8,128)(2,1)S(1)}, bf16[192,768]{1,0:T(8,128)(2,1)}, u32[]{:S(2)}) copy-start(bf16[192,768]{1,0:T(8,128)(2,1)} %param.29) | copy-start | bytes 884740
  475.2 192.3 %reduce-scatter.11.cloned.1.call-start = ((), (), s32[]{:S(2)}) async-start(), calls=%async_computation.11 | async-start | bytes 3932160 | tf_op jit(solution)/shard_map/reduce_scatter | solution.py:224
  539.9 5.7 copy-start.6
  539.9 5.6 copy-start.8
  588.8 181.7 %all-reduce.5.cloned.1.call-start = ((), (), s32[]{:S(2)}) async-start(), calls=%async_computation.12 | async-start | bytes 14155776 | tf_op jit(solution)/shard_map/psum | solution.py:242
  589.1 7.1 copy-start.39
  589.1 7.1 copy-start.43
  607.3 46.5 %copy-start.10 = (bf16[4,512,3,64]{1,3,2,0:T(8,128)(2,1)S(1)}, bf16[4,512,3,64]{1,3,2,0:T(8,128)(2,1)}, u32[]{:S(2)}) copy-start(bf16[4,512,3,64]{1,3,2,0:T(8,128)(2,1)} %get-tuple-element.113) | copy-start | bytes 2359300
  607.3 46.8 %copy-start.12 = (bf16[4,512,3,64]{1,3,2,0:T(8,128)(2,1)S(1)}, bf16[4,512,3,64]{1,3,2,0:T(8,128)(2,1)}, u32[]{:S(2)}) copy-start(bf16[4,512,3,64]{1,3,2,0:T(8,128)(2,1)} %get-tuple-element.111) | copy-start | bytes 2359300
  607.3 47.1 %copy-start.35 = (f32[768]{0:T(1024)S(1)}, f32[768]{0:T(1024)}, u32[]{:S(2)}) copy-start(f32[768]{0:T(1024)} %get-tuple-element.220) | copy-start | bytes 9220
  607.3 60.2 %copy-start.13 = (f32[512,768]{1,0:T(8,128)S(1)}, f32[512,768]{1,0:T(8,128)}, u32[]{:S(2)}) copy-start(f32[512,768]{1,0:T(8,128)} %get-tuple-element.210) | copy-start | bytes 4718596
  770.5 5.9 copy-start.19
  770.5 6.7 copy-start.18
  (29 other events, 54.1 us)
Sparse Core Ops, SparseCore 0:
  9.6 62.2 all-gather.4
  113.4 60.9 reduce-scatter.4
  179.0 61.4 all-gather.6
  264.2 60.9 reduce-scatter.6
  331.9 61.4 all-gather.8
  406.8 60.9 reduce-scatter.8
  475.3 61.5 all-gather.10
  588.9 61.9 reduce-scatter.10
  656.1 114.2 all-reduce.4
where the time goes:
time: 798 us; the launch traced here: 787 us
  waiting for transfers between devices  525 us (66%)
  matrix products  109 us (14%)
  blocking collectives  58.9 us (7%)
  local copies, waits for them, and re-layouts  39 us (5%)
  other arithmetic  38.3 us (5%)
  between operations  14.7 us (2%)
    psum x1, waiting for transfers between devices, shards(): lax.psum((grad_query, grad_query_bias, grad_key, grad_value, grad_value_b...  101 us
    all_gather x1, waiting for transfers between devices, shards(): group_tokens = lax.all_gather(tokens, 'mp', axis=0, tiled=True)  62.5 us
    all_gather x1, waiting for transfers between devices, shards(): group_grad_att = lax.all_gather(grad_attended, 'mp', axis=0, tiled=True)  61.6 us
    all_gather x1, waiting for transfers between devices, shards(): group_grad_mixed = lax.all_gather(grad_mixed, 'mp', axis=0, tiled=True)  61.6 us
    reduce_scatter x1, waiting for transfers between devices, shards(): lax.psum_scatter(outer_cols(rows, up_weight).astype(jnp.bfloat16), 'mp',...  60.8 us
    all_gather x1, waiting for transfers between devices, shards(): lax.all_gather(normed_one.astype(jnp.bfloat16), 'mp', axis=0, tiled=True)  60.2 us
    reduce_scatter x1, waiting for transfers between devices, shards(): lax.psum_scatter(jnp.dot(rows, output_weight, preferred_element_type=jnp....  59.8 us
    reduce_scatter x1, waiting for transfers between devices, shards(): lax.psum_scatter(jnp.dot(rows, down_weight, preferred_element_type=jnp.fl...  57.2 us
  transfers between devices with their start and end apart: 9, of which 8 were waited for; matrix products, arithmetic and copies ran while one was open for 3% of the time, Pallas kernels for 0%

commit v1 on v0

v1 whole, which is shorter than its diff:
```python
import math

import jax
import jax.numpy as jnp
from jax import lax
from jax.sharding import PartitionSpec as P

HEAD_DIM = 64
GROUP = 8
epsilon = 1e-05
bf16 = jnp.bfloat16
f32 = jnp.float32


def inner_rows(left, right):
    return lax.dot_general(left, right, (((0,), (0,)), ((), ())), preferred_element_type=f32)


def norm_forward(total, norm_gain, norm_shift):
    average = jnp.mean(total, axis=-1, keepdims=True)
    centred = total - average
    inverse = lax.rsqrt(jnp.mean(centred * centred, axis=-1, keepdims=True) + epsilon)
    normal = centred * inverse
    return (normal * norm_gain + norm_shift, normal, inverse)


def norm_backward(grad_out, normal, inverse, norm_gain):
    scaled = grad_out * norm_gain
    return inverse * (
        scaled
        - jnp.mean(scaled, axis=-1, keepdims=True)
        - normal * jnp.mean(scaled * normal, axis=-1, keepdims=True)
    )


def gelu_slope(hidden):
    cumulative = 0.5 * (1.0 + lax.erf(hidden * 0.7071067811865476))
    density = jnp.exp(-0.5 * hidden * hidden) * 0.3989422804014327
    return cumulative + hidden * density


def masked_scores(queries, key_vecs, segment_row):
    scale_factor = 1.0 / math.sqrt(queries.shape[-1])
    scores = (
        jnp.einsum("qhd,khd->hqk", queries, key_vecs, preferred_element_type=f32) * scale_factor
    )
    allowed = segment_row[:, None] == segment_row[None, :]
    return jnp.where(allowed[None], scores, -1e30)


def row_forward(queries, key_vecs, values, segment_row):
    masked = masked_scores(queries, key_vecs, segment_row)
    highest_score = jnp.max(masked, axis=-1, keepdims=True)
    expo = jnp.exp(masked - highest_score)
    denominator = jnp.sum(expo, axis=-1, keepdims=True)
    probs = (expo / denominator).astype(bf16)
    context = jnp.einsum("hqk,khd->qhd", probs, values, preferred_element_type=f32)
    log_total = highest_score[..., 0] + jnp.log(denominator[..., 0])
    return (context.astype(bf16), log_total)


def row_backward(queries, key_vecs, values, segment_row, log_total, grad_context):
    scale_factor = 1.0 / math.sqrt(queries.shape[-1])
    masked = masked_scores(queries, key_vecs, segment_row)
    probs = jnp.exp(masked - log_total[..., None])
    grad_probs = jnp.einsum("qhd,khd->hqk", grad_context, values, preferred_element_type=f32)
    grad_values = jnp.einsum(
        "hqk,qhd->khd", probs.astype(bf16), grad_context, preferred_element_type=f32
    )
    inner = jnp.sum(grad_probs * probs, axis=-1, keepdims=True)
    grad_scores = (probs * (grad_probs - inner)).astype(bf16)
    grad_queries = (
        jnp.einsum("hqk,khd->qhd", grad_scores, key_vecs, preferred_element_type=f32) * scale_factor
    )
    grad_keys = (
        jnp.einsum("hqk,qhd->khd", grad_scores, queries, preferred_element_type=f32) * scale_factor
    )
    return (grad_queries.astype(bf16), grad_keys.astype(bf16), grad_values.astype(bf16))


def solution(mesh):
    n_dp, n_mp = mesh.shape["dp"], mesh.shape["mp"]
    if n_dp % GROUP:
        raise ValueError("dp size")

    def rotate(array, step):
        return lax.ppermute(array, "mp", [(i, (i + step) % n_mp) for i in range(n_mp)])

    def swap(array, bits):
        return lax.ppermute(array, "dp", [(i, i ^ bits) for i in range(n_dp)])

    def plane_gather(array):
        four = jnp.stack([array, swap(array, 2), swap(array, 4), swap(array, 6)])
        other = swap(four, 1)
        return jnp.stack([four, other], axis=1).reshape((GROUP,) + array.shape)

    def gather_weights(quarter, order, extra=None):
        rows = quarter.shape[0] // GROUP
        index = lax.axis_index("dp") % GROUP
        piece = lax.dynamic_slice_in_dim(quarter, index * rows, rows, 0)
        if extra is not None:
            piece = jnp.concatenate([piece, extra])
        got = [rotate(piece, r) for r in range(1, n_mp)]
        slots = plane_gather(jnp.stack([g[:rows] for g in got]))
        slots = slots[order].transpose(1, 0, 2, 3).reshape((n_mp - 1,) + quarter.shape)
        full = jnp.concatenate([quarter[None], slots])
        if extra is None:
            return full
        return full, jnp.stack([extra] + [g[rows:] for g in got])

    def reduce_grads(grads, order):
        quarters, height, width = grads.shape
        rows = height // GROUP
        half = width // 2
        slots = grads.astype(bf16).reshape(quarters, GROUP, rows, width)[:, order]
        slots = slots.reshape(quarters, GROUP // 2, 2, rows, width)
        part = (slots[:, :, 0].astype(f32) + swap(slots[:, :, 1], 1).astype(f32)).astype(bf16)
        left, right = part[..., :half], part[..., half:]
        left_got = swap(left[:, jnp.array([1, 3])], 2)
        right_got = swap(right[:, 2:], 4)
        left = (left[:, jnp.array([0, 2])].astype(f32) + left_got.astype(f32)).astype(bf16)
        right = (right[:, :2].astype(f32) + right_got.astype(f32)).astype(bf16)
        left_got = swap(left[:, 1], 4)
        right_got = swap(right[:, 1], 2)
        left = left[:, 0].astype(f32) + left_got.astype(f32)
        right = right[:, 0].astype(f32) + right_got.astype(f32)
        part = jnp.concatenate([left, right], axis=-1).astype(bf16)
        total = part[0].astype(f32)
        for r in range(1, n_mp):
            total = total + rotate(part[r], -r).astype(f32)
        if n_dp > GROUP:
            total = lax.psum(
                total,
                "dp",
                axis_index_groups=[
                    [i + GROUP * k for k in range(n_dp // GROUP)] for i in range(GROUP)
                ],
            )
        return plane_gather(total.astype(bf16))[order].astype(f32).reshape(height, width)

    def shards(
        tokens,
        segment_ids,
        query_weight,
        query_bias,
        key_weight,
        value_weight,
        value_bias,
        output_weight,
        output_bias,
        first_gain,
        first_shift,
        up_weight,
        up_bias,
        down_weight,
        down_bias,
        second_gain,
        second_shift,
        cotangent,
    ):
        length, width = tokens.shape
        head_width = query_weight.shape[1]
        units = up_weight.shape[1]
        heads = n_mp * head_width // HEAD_DIM
        order = jnp.arange(GROUP) ^ (lax.axis_index("dp") % GROUP)
        place = lax.axis_index("mp")
        row = lax.dynamic_index_in_dim(segment_ids, place, 0, keepdims=False)

        biases = jnp.zeros((8, units), bf16)
        biases = biases.at[0, :head_width].set(query_bias)
        biases = biases.at[0, head_width : 2 * head_width].set(value_bias)
        biases = biases.at[1].set(up_bias)
        att_quarter = jnp.concatenate(
            [query_weight, key_weight, value_weight, output_weight.T], axis=1
        )
        att, biases = gather_weights(att_quarter, order, biases)
        up = gather_weights(up_weight, order)
        down = gather_weights(down_weight, order)

        def columns(array):
            return array.transpose(1, 0, 2).reshape(array.shape[1], -1)

        w = head_width
        query_all, key_all, value_all, output_all = (
            columns(att[:, :, i * w : (i + 1) * w]) for i in range(4)
        )
        up_all, down_all = columns(up), down.reshape(-1, width)
        query_bias_all = biases[:, 0, :w].reshape(-1)
        value_bias_all = biases[:, 0, w : 2 * w].reshape(-1)
        up_bias_all = biases[:, 1].reshape(-1)

        def by_heads(array):
            return array.reshape(length, heads, HEAD_DIM)

        def flat(array):
            return array.reshape(length, heads * HEAD_DIM)

        def mm(left, right):
            return jnp.dot(left, right, preferred_element_type=f32)

        def mmt(left, right):
            return lax.dot_general(left, right, (((1,), (1,)), ((), ())), preferred_element_type=f32)

        queries = by_heads((mm(tokens, query_all) + query_bias_all).astype(bf16))
        key_vecs = by_heads(mm(tokens, key_all).astype(bf16))
        values = by_heads((mm(tokens, value_all) + value_bias_all).astype(bf16))
        contexts, log_total = row_forward(queries, key_vecs, values, row)
        contexts = flat(contexts)
        attended = mmt(contexts, output_all) + output_bias
        gain_one = first_gain.astype(f32)
        gain_two = second_gain.astype(f32)
        normed_one, normal_one, inverse_one = norm_forward(
            tokens.astype(f32) + attended, gain_one, first_shift.astype(f32)
        )
        normed_low = normed_one.astype(bf16)
        hidden = mm(normed_low, up_all) + up_bias_all
        activated = jax.nn.gelu(hidden, approximate=False).astype(bf16)
        mixed = mm(activated, down_all) + down_bias
        result, normal_two, inverse_two = norm_forward(
            normed_one + mixed, gain_two, second_shift.astype(f32)
        )
        grad_out = cotangent.astype(f32)
        grad_second_gain = jnp.sum(grad_out * normal_two, axis=0)
        grad_second_shift = jnp.sum(grad_out, axis=0)
        grad_two = norm_backward(grad_out, normal_two, inverse_two, gain_two)
        grad_mixed = grad_two.astype(bf16)
        grad_down_bias = jnp.sum(grad_mixed.astype(f32), axis=0)

        grad_down = inner_rows(activated, grad_mixed).reshape(n_mp, units, width)
        grad_down = reduce_grads(grad_down, order)
        grad_hidden = (mmt(grad_mixed, down_all) * gelu_slope(hidden)).astype(bf16)
        grad_up_bias = jnp.sum(grad_hidden.astype(f32), axis=0)

        def quarters(array):
            return array.reshape(array.shape[0], n_mp, -1).transpose(1, 0, 2)

        grad_up = reduce_grads(quarters(inner_rows(normed_low, grad_hidden)), order)
        grad_normed = mmt(grad_hidden, up_all) + grad_two
        grad_first_gain = jnp.sum(grad_normed * normal_one, axis=0)
        grad_first_shift = jnp.sum(grad_normed, axis=0)
        grad_one = norm_backward(grad_normed, normal_one, inverse_one, gain_one)
        grad_attended = grad_one.astype(bf16)
        grad_output_bias = jnp.sum(grad_attended.astype(f32), axis=0)
        grad_contexts = mm(grad_attended, output_all).astype(bf16)
        grad_queries, grad_keys, grad_values = map(
            flat,
            row_backward(queries, key_vecs, values, row, log_total, by_heads(grad_contexts)),
        )
        grad_query_bias = jnp.sum(grad_queries.astype(f32), axis=0)
        grad_value_bias = jnp.sum(grad_values.astype(f32), axis=0)
        grad_att = jnp.concatenate(
            [
                quarters(inner_rows(tokens, grad_queries)),
                quarters(inner_rows(tokens, grad_keys)),
                quarters(inner_rows(tokens, grad_values)),
                quarters(inner_rows(grad_attended, contexts)),
            ],
            axis=-1,
        )
        grad_att = reduce_grads(grad_att, order)
        grad_tokens = (
            mmt(grad_queries, query_all)
            + mmt(grad_keys, key_all)
            + mmt(grad_values, value_all)
            + grad_one
        )
        mine = jnp.concatenate(
            [
                grad_query_bias.reshape(n_mp, -1),
                grad_value_bias.reshape(n_mp, -1),
                grad_up_bias.reshape(n_mp, -1),
            ],
            axis=1,
        )
        mine = mine[(place - jnp.arange(n_mp)) % n_mp]
        shared = jnp.stack(
            [
                grad_output_bias,
                grad_first_gain,
                grad_first_shift,
                grad_down_bias,
                grad_second_gain,
                grad_second_shift,
            ]
        )
        mine, shared = lax.psum((mine, shared), ("dp", "mp"))
        mine = lax.dynamic_index_in_dim(mine, place, 0, keepdims=False)
        return (
            result.astype(bf16),
            grad_tokens.astype(bf16),
            grad_att[:, :w],
            mine[:w],
            grad_att[:, w : 2 * w],
            grad_att[:, 2 * w : 3 * w],
            mine[w : 2 * w],
            grad_att[:, 3 * w :].T,
            shared[0],
            shared[1],
            shared[2],
            grad_up,
            mine[2 * w :],
            grad_down,
            shared[3],
            shared[4],
            shared[5],
        )

    in_specs = (
        P(("dp", "mp"), None),
        P("dp", None),
        P(None, "mp"),
        P("mp"),
        P(None, "mp"),
        P(None, "mp"),
        P("mp"),
        P("mp", None),
        P(),
        P(),
        P(),
        P(None, "mp"),
        P("mp"),
        P("mp", None),
        P(),
        P(),
        P(),
        P(("dp", "mp"), None),
    )
    out_specs = (
        P(("dp", "mp"), None),
        P(("dp", "mp"), None),
        P(None, "mp"),
        P("mp"),
        P(None, "mp"),
        P(None, "mp"),
        P("mp"),
        P("mp", None),
        P(),
        P(),
        P(),
        P(None, "mp"),
        P("mp"),
        P("mp", None),
        P(),
        P(),
        P(),
    )
    return jax.shard_map(shards, mesh=mesh, in_specs=in_specs, out_specs=out_specs, check_vma=False)
```

time: 798 us -> 509 us (0.64)
  waiting for transfers between devices: 525 us -> 92 us
  local copies, waits for them, and re-layouts: 39 us -> 130 us
  starting transfers between devices: 1.01 us -> 78.3 us
  other arithmetic: 38.3 us -> 71.9 us
  matrix products: 109 us -> 84.6 us
  blocking collectives: 58.9 us -> 38.8 us
  between operations: 14.7 us -> 2.56 us
    all_gather x4 -> x0, waiting for transfers between devices: 246 us -> none  [the longest x1 62.5 us: shards(): group_tokens = lax.all_gather(tokens, 'mp', axis=0, tiled=True)]
    reduce_scatter x4 -> x0, waiting for transfers between devices: 178 us -> none  [the longest x1 60.8 us: shards(): lax.psum_scatter(outer_cols(rows, up_weight).astype(jnp.bfloat16), 'mp',...]
    psum x1 -> x0, waiting for transfers between devices: 101 us -> none  [shards(): lax.psum((grad_query, grad_query_bias, grad_key, grad_value, grad_value_b...]
    ppermute x0 -> x57, waiting for transfers between devices: none -> 92 us  [the longest x39 65.5 us: swap(): return lax.ppermute(array, 'dp', [(i, i ^ bits) for i in range(n_dp)])]
    ppermute x0 -> x57, starting transfers between devices: none -> 78.3 us  [the longest x39 52.8 us: swap(): return lax.ppermute(array, 'dp', [(i, i ^ bits) for i in range(n_dp)])]
    gather x0 -> x18, local copies, waits for them, and re-layouts: none -> 45.2 us  [the longest x5 23.6 us: reduce_grads(): slots = grads.astype(bf16).reshape(quarters, GROUP, rows, width)[:, order]]
    transpose x0 -> x12, local copies, waits for them, and re-layouts: none -> 31.7 us  [the longest x5 14.8 us: columns(): return array.transpose(1, 0, 2).reshape(array.shape[1], -1)]
    dot_general x36 -> x17, matrix products: 87.5 us -> 63.4 us  [the longest x6 24.1 us: mm(): return jnp.dot(left, right, preferred_element_type=f32)]
  transfers between devices with their start and end apart: 9 -> 57, of which waited for: 8 -> 21; matrix products, arithmetic and copies ran while one was open for 3% -> 31% of each run, Pallas kernels for 0% -> 0%
where the time goes in v1:
time: 509 us; the launch traced here: 499 us
  local copies, waits for them, and re-layouts  130 us (26%)
  waiting for transfers between devices  92 us (18%)
  matrix products  84.6 us (17%)
  starting transfers between devices  78.3 us (15%)
  other arithmetic  71.9 us (14%)
  blocking collectives  38.8 us (8%)
    ppermute x39, waiting for transfers between devices, swap(): return lax.ppermute(array, 'dp', [(i, i ^ bits) for i in range(n_dp)])  65.5 us
    ppermute x39, starting transfers between devices, swap(): return lax.ppermute(array, 'dp', [(i, i ^ bits) for i in range(n_dp)])  52.8 us
    psum x1, blocking collectives, shards(): mine, shared = lax.psum((mine, shared), ('dp', 'mp'))  38.8 us
    ppermute x18, waiting for transfers between devices, rotate(): lax.ppermute(array, 'mp', [(i, (i + step) % n_mp) for i in range(n_mp)])  26.5 us
    ppermute x18, starting transfers between devices, rotate(): lax.ppermute(array, 'mp', [(i, (i + step) % n_mp) for i in range(n_mp)])  25.5 us
    dot_general x6, matrix products, mm(): return jnp.dot(left, right, preferred_element_type=f32)  24.1 us
    gather x5, local copies, waits for them, and re-layouts, reduce_grads(): slots = grads.astype(bf16).reshape(quarters, GROUP, rows, width)[:, order]  23.6 us
    dot_general x6, matrix products, inner_rows(): lax.dot_general(left, right, (((0,), (0,)), ((), ())), preferred_element_...  19.3 us
  transfers between devices with their start and end apart: 57, of which 21 were waited for; matrix products, arithmetic and copies ran while one was open for 31% of the time, Pallas kernels for 0%

profile of v1, /device:TPU:9, one launch (start us, length us, event | category | flops | bytes accessed | tf_op | source)
XLA Modules:
  0.0 498.7 jit_solution(7196510737156142588)
XLA Ops:
  24.9 6.1 %collective-permute-done.8 = bf16[96,768]{1,0:T(8,128)(2,1)S(1)} collective-permute-done((bf16[96,768]{1,0:T(8,128)(2,1)S(1)}, bf16[96,768]{1,0:T(8,128)(2,1)S(1)}, u32[]{:S(2)}, u32[]{:S(2)}) %collective-permute-start.8) | collective-permute-done | bytes 147488 | tf_op jit(solution)/shard_map/ppermute | solution.py:87
  45.5 10.5 %collective-permute-done.19 = bf16[3,96,768]{2,1,0:T(8,128)(2,1)S(1)} collective-permute-done((bf16[3,96,768]{2,1,0:T(8,128)(2,1)S(1)}, bf16[3,96,768]{2,1,0:T(8,128)(2,1)S(1)}, u32[]{:S(2)}, u32[]{:S(2)}) %collective-permute-start.19) | collective-permute-done | bytes 442400 | tf_op jit(solution)/shard_map/ppermute | solution.py:90
  58.1 5.8 %collective-permute-start.20 = (bf16[4,3,96,768]{3,2,1,0:T(8,128)(2,1)}, bf16[4,3,96,768]{3,2,1,0:T(8,128)(2,1)S(1)}, u32[]{:S(2)}, u32[]{:S(2)}) collective-permute-start(bf16[4,3,96,768]{3,2,1,0:T(8,128)(2,1)} %get-tuple-element.135), channel_id=1, source_target_pairs={{0,4},{4,0},{8,12},{12,8},{16,20},{20,16},{24,28},{28,24},{1,5},{5... | collective-permute-start | bytes 5308424 | tf_op jit(solution)/shard_map/ppermute | solution.py:90
  64.5 10.4 %collective-permute-done.12 = bf16[3,96,768]{2,1,0:T(8,128)(2,1)S(1)} collective-permute-done((bf16[3,96,768]{2,1,0:T(8,128)(2,1)S(1)}, bf16[3,96,768]{2,1,0:T(8,128)(2,1)S(1)}, u32[]{:S(2)}, u32[]{:S(2)}) %collective-permute-start.12) | collective-permute-done | bytes 442400 | tf_op jit(solution)/shard_map/ppermute | solution.py:90
  85.4 6.6 %collective-permute-done.4 = bf16[3,96,768]{2,1,0:T(8,128)(2,1)S(1)} collective-permute-done((bf16[3,96,768]{2,1,0:T(8,128)(2,1)S(1)}, bf16[3,96,768]{2,1,0:T(8,128)(2,1)S(1)}, u32[]{:S(2)}, u32[]{:S(2)}) %collective-permute-start.4) | collective-permute-done | bytes 442400 | tf_op jit(solution)/shard_map/ppermute | solution.py:90
  92.0 10.3 %collective-permute-done.5 = bf16[3,96,768]{2,1,0:T(8,128)(2,1)S(1)} collective-permute-done((bf16[3,96,768]{2,1,0:T(8,128)(2,1)S(1)}, bf16[3,96,768]{2,1,0:T(8,128)(2,1)S(1)}, u32[]{:S(2)}, u32[]{:S(2)}) %collective-permute-start.5) | collective-permute-done | bytes 442400 | tf_op jit(solution)/shard_map/ppermute | solution.py:90
  128.4 6.9 %copy.144 = bf16[768,4,768]{0,2,1:T(8,128)(2,1)} copy(bf16[768,4,768]{2,0,1:T(8,128)(2,1)} %maximum_bitcast_fusion) | data formatting | bytes 9437184 | tf_op jit(solution)/shard_map/transpose | solution.py:181
  173.3 15.9 %fusion.4 = (bf16[512,3072]{1,0:T(8,128)(2,1)S(1)}, f32[512,3072]{1,0:T(8,128)S(1)}) fusion(f32[3072]{0:T(1024)S(1)} %bitcast.450, bf16[768,3072]{0,1:T(8,128)(2,1)S(1)} %bitcast.380, f32[512,768]{1,0:T(8,128)S(1)} %get-tuple-element.169, f32[768]{0:T(1024)S(1)} %copy-done.38, f32[768]{0:T(1024)S(1)} %convert_element_type.401, f32[512]{0:T(512)S(1)} %add_rsqrt_fusion.1, ...), kind=kOutput, calls=%fused_computation.31 | convolution fusion | flops 2521694208 | bytes 15751168 | tf_op jit(solution)/shard_map/dot_general | solution.py:199
  215.3 7.4 %convert_reduce_fusion.4 = (f32[12,64]{1,0:T(8,128)S(1)}, bf16[12,64,512]{2,1,0:T(8,128)(2,1)}) fusion(bf16[512,12,64]{0,2,1:T(8,128)(2,1)S(1)} %bitcast.391, f32[12,512]{1,0:T(8,128)S(1)} %log_add_fusion, f32[12,512,512]{1,2,0:T(8,128)} %copy-done.2, pred[512,512]{0,1:T(8,128)(4,1)S(1)} %copy-done.9), kind=kOutput, calls=%fused_computation.105 | convolution fusion | flops 416414976 | bytes 14445568 | tf_op jit(solution)/shard_map/hqk,qhd->khd/dot_general | solution.py:67
  222.7 9.6 %multiply_reduce_fusion = (f32[12,512]{1,0:T(8,128)S(1)}, f32[12,512,512]{1,2,0:T(8,128)}) fusion(f32[12,512]{1,0:T(8,128)S(1)} %log_add_fusion, f32[12,512,512]{1,2,0:T(8,128)} %copy-done.2, pred[512,512]{0,1:T(8,128)(4,1)S(1)} %copy-done.9, bf16[512,12,64]{0,2,1:T(8,128)(2,1)S(1)} %bitcast.392, bf16[512,12,64]{0,2,1:T(8,128)(2,1)S(1)} %bitcast.410), kind=kOutput, calls=%fused_computation.17 | convolution fusion | flops 418375680 | bytes 27049984 | tf_op jit(solution)/shard_map/qhd,khd->hqk/dot_general | solution.py:66
  232.3 6.8 %multiply_convert_fusion = bf16[12,512,512]{1,2,0:T(8,128)(2,1)S(1)} fusion(f32[12,512,512]{1,2,0:T(8,128)} %get-tuple-element.176, f32[12,512]{1,0:T(8,128)S(1)} %get-tuple-element.175, f32[12,512]{1,0:T(8,128)S(1)} %log_add_fusion, f32[12,512,512]{1,2,0:T(8,128)S(1)} %bitcast.347, pred[512,512]{0,1:T(8,128)(4,1)S(1)} %copy-done.9), kind=kLoop, calls=%fused_computation.16 | loop fusion | flops 18874368 | bytes 31768576 | tf_op jit(solution)/shard_map/convert_element_type | solution.py:71
  253.5 5.4 %gather_fusion.12 = bf16[8,4,96,768]{3,2,1,0:T(8,128)(2,1)} fusion(bf16[4,8,96,768]{3,2,1,0:T(8,128)(2,1)} %bitcast.386, s32[1024]{0:T(1024)S(1)} %copy-done.35), kind=kCustom, calls=%fused_computation.12 | custom fusion | bytes 9437216 | tf_op jit(solution)/shard_map/gather | solution.py:115
  273.6 6.6 %pad_maximum_fusion.1 = bf16[4,8,96,768]{3,2,1,0:T(8,128)(2,1)} fusion(bf16[4,8,96,192]{3,2,1,0:T(8,128)(2,1)S(1)} %bitcast.371, bf16[4,8,96,192]{3,2,1,0:T(8,128)(2,1)} %bitcast.372, bf16[4,8,96,192]{3,2,1,0:T(8,128)(2,1)} %bitcast.374, bf16[4,8,96,192]{3,2,1,0:T(8,128)(2,1)} %bitcast.373), kind=kLoop, calls=%fused_computation.64 | loop fusion | flops 18874368 | bytes 9437184 | tf_op jit(solution)/shard_map/concatenate | solution.py:251
  280.2 9.7 %convert_element_type.455 = bf16[768,4,768]{2,1,0:T(4,128)(2,1)} reshape(bf16[768,3072]{1,0:T(8,128)(2,1)} %convolution_convert_fusion.1) | data formatting | bytes 9437184 | tf_op jit(solution)/shard_map/convert_element_type | solution.py:115
  289.9 5.1 %copy.161 = bf16[4,768,768]{2,1,0:T(8,128)(2,1)} copy(bf16[4,768,768]{2,0,1:T(4,128)(2,1)} %bitcast.356) | data formatting | bytes 9437184 | tf_op jit(solution)/shard_map/convert_element_type | solution.py:115
  295.0 5.4 %gather_fusion.8 = bf16[8,4,96,768]{3,2,1,0:T(8,128)(2,1)} fusion(bf16[4,8,96,768]{3,2,1,0:T(8,128)(2,1)} %bitcast.357, s32[1024]{0:T(1024)S(1)} %copy-done.35), kind=kCustom, calls=%fused_computation.8 | custom fusion | bytes 9437216 | tf_op jit(solution)/shard_map/gather | solution.py:115
  305.2 5.4 %gather_fusion.3 = bf16[8,4,96,768]{3,2,1,0:T(8,128)(2,1)} fusion(bf16[4,8,96,768]{3,2,1,0:T(8,128)(2,1)} %pad_maximum_fusion.1, s32[1024]{0:T(1024)S(1)} %copy-done.35), kind=kCustom, calls=%fused_computation.3 | custom fusion | bytes 9437216 | tf_op jit(solution)/shard_map/gather | solution.py:115
  317.7 38.8 %all-reduce.1 = (f32[4,1152]{1,0:T(4,128)}, f32[6,768]{1,0:T(8,128)}) all-reduce(f32[4,1152]{1,0:T(4,128)S(1)} %gather_fusion.7, f32[6,768]{1,0:T(8,128)S(1)} %stack.271), channel_id=1, replica_groups=mesh['dp'=8,'mp'=4] {'dp','mp'}, use_global_device_ids=true, to_apply=%region_15.16 | all-reduce | flops 9216 | bytes 73728 | tf_op jit(solution)/shard_map/psum | solution.py:286
  397.1 5.2 %collective-permute-done.36 = bf16[4,2,96,384]{3,2,1,0:T(8,128)(2,1)S(1)} collective-permute-done((bf16[4,2,96,384]{3,2,1,0:T(8,128)(2,1)}, bf16[4,2,96,384]{3,2,1,0:T(8,128)(2,1)S(1)}, u32[]{:S(2)}, u32[]{:S(2)}) %collective-permute-start.36) | collective-permute-done | bytes 589856 | tf_op jit(solution)/shard_map/ppermute | solution.py:90
  406.3 8.7 %collective-permute-done.24 = bf16[4,2,96,384]{3,2,0,1:T(8,128)(2,1)S(1)} collective-permute-done((bf16[4,2,96,384]{3,2,0,1:T(8,128)(2,1)}, bf16[4,2,96,384]{3,2,0,1:T(8,128)(2,1)S(1)}, u32[]{:S(2)}, u32[]{:S(2)}) %collective-permute-start.24) | collective-permute-done | bytes 589856 | tf_op jit(solution)/shard_map/ppermute | solution.py:90
  417.9 5.3 %collective-permute-done.49 = bf16[4,96,384]{2,1,0:T(8,128)(2,1)S(1)} collective-permute-done((bf16[4,96,384]{2,1,0:T(8,128)(2,1)S(1)}, bf16[4,96,384]{2,1,0:T(8,128)(2,1)S(1)}, u32[]{:S(2)}, u32[]{:S(2)}) %collective-permute-start.49) | collective-permute-done | bytes 294944 | tf_op jit(solution)/shard_map/ppermute | solution.py:90
  443.2 9.2 %collective-permute-done.38 = bf16[96,768]{1,0:T(8,128)(2,1)S(1)} collective-permute-done((bf16[96,768]{1,0:T(8,128)(2,1)S(1)}, bf16[96,768]{1,0:T(8,128)(2,1)S(1)}, u32[]{:S(2)}, u32[]{:S(2)}) %collective-permute-start.38) | collective-permute-done | bytes 147488 | tf_op jit(solution)/shard_map/ppermute | solution.py:87
  463.5 8.1 %collective-permute-start.56 = (bf16[4,96,768]{2,1,0:T(8,128)(2,1)S(1)}, bf16[4,96,768]{2,1,0:T(8,128)(2,1)S(1)}, u32[]{:S(2)}, u32[]{:S(2)}) collective-permute-start(bf16[4,96,768]{2,1,0:T(8,128)(2,1)S(1)} %get-tuple-element.142), channel_id=1, source_target_pairs={{0,4},{4,0},{8,12},{12,8},{16,20},{20,16},{24,28},{28,24},{1,5},{5... | collective-permute-start | bytes 1769480 | tf_op jit(solution)/shard_map/ppermute | solution.py:90
  479.6 5.5 %collective-permute-start.32 = (bf16[4,96,768]{2,1,0:T(8,128)(2,1)}, bf16[4,96,768]{2,1,0:T(8,128)(2,1)}, u32[]{:S(2)}, u32[]{:S(2)}) collective-permute-start(bf16[4,96,768]{2,1,0:T(8,128)(2,1)} %get-tuple-element.152), channel_id=1, source_target_pairs={{0,4},{4,0},{8,12},{12,8},{16,20},{20,16},{24,28},{28,24},{1,5},{5... | collective-permute-start | bytes 1769480 | tf_op jit(solution)/shard_map/ppermute | solution.py:90
  (419 shorter events, 281.3 us)
Async XLA Ops:
  1.7 19.5 %collective-permute-start.15 = (bf16[96,768]{1,0:T(8,128)(2,1)S(1)}, bf16[96,768]{1,0:T(8,128)(2,1)S(1)}, u32[]{:S(2)}, u32[]{:S(2)}) collective-permute-start(bf16[96,768]{1,0:T(8,128)(2,1)S(1)} %constant_dynamic-slice_fusion.1), channel_id=1, source_target_pairs={{0,2},{1,3},{2,0},{3,1},{4,6},{5,7},{6,4},{7,5},{8,10},{9,11},{10,... | collective-permute-start | bytes 442376 | tf_op jit(solution)/shard_map/ppermute | solution.py:87
  4.2 18.6 %collective-permute-start.14 = (bf16[96,768]{1,0:T(8,128)(2,1)S(1)}, bf16[96,768]{1,0:T(8,128)(2,1)S(1)}, u32[]{:S(2)}, u32[]{:S(2)}) collective-permute-start(bf16[96,768]{1,0:T(8,128)(2,1)S(1)} %constant_dynamic-slice_fusion.1), channel_id=1, source_target_pairs={{0,1},{1,2},{2,3},{3,0},{4,5},{5,6},{6,7},{7,4},{8,9},{9,10},{10,1... | collective-permute-start | bytes 442376 | tf_op jit(solution)/shard_map/ppermute | solution.py:87
  7.4 23.6 %collective-permute-start.8 = (bf16[96,768]{1,0:T(8,128)(2,1)S(1)}, bf16[96,768]{1,0:T(8,128)(2,1)S(1)}, u32[]{:S(2)}, u32[]{:S(2)}) collective-permute-start(bf16[96,768]{1,0:T(8,128)(2,1)S(1)} %constant_dynamic-slice_fusion.2), channel_id=1, source_target_pairs={{0,2},{1,3},{2,0},{3,1},{4,6},{5,7},{6,4},{7,5},{8,10},{9,11},{10,... | collective-permute-start | bytes 442376 | tf_op jit(solution)/shard_map/ppermute | solution.py:87
  22.9 21.2 %collective-permute-start.18 = (bf16[3,96,768]{2,1,0:T(8,128)(2,1)S(1)}, bf16[3,96,768]{2,1,0:T(8,128)(2,1)S(1)}, u32[]{:S(2)}, u32[]{:S(2)}) collective-permute-start(bf16[3,96,768]{2,1,0:T(8,128)(2,1)S(1)} %get-tuple-element.157), channel_id=1, source_target_pairs={{0,16},{4,20},{8,24},{12,28},{16,0},{20,4},{24,8},{28,12},{1,17},{... | collective-permute-start | bytes 1327112 | tf_op jit(solution)/shard_map/ppermute | solution.py:90
  39.4 24.4 %collective-permute-start.11 = (bf16[3,96,768]{2,1,0:T(8,128)(2,1)S(1)}, bf16[3,96,768]{2,1,0:T(8,128)(2,1)S(1)}, u32[]{:S(2)}, u32[]{:S(2)}) collective-permute-start(bf16[3,96,768]{2,1,0:T(8,128)(2,1)S(1)} %get-tuple-element.161), channel_id=1, source_target_pairs={{0,16},{4,20},{8,24},{12,28},{16,0},{20,4},{24,8},{28,12},{1,17},{... | collective-permute-start | bytes 1327112 | tf_op jit(solution)/shard_map/ppermute | solution.py:90
  42.8 21.7 %collective-permute-start.10 = (bf16[3,96,768]{2,1,0:T(8,128)(2,1)S(1)}, bf16[3,96,768]{2,1,0:T(8,128)(2,1)S(1)}, u32[]{:S(2)}, u32[]{:S(2)}) collective-permute-start(bf16[3,96,768]{2,1,0:T(8,128)(2,1)S(1)} %get-tuple-element.161), channel_id=1, source_target_pairs={{0,8},{4,12},{8,0},{12,4},{16,24},{20,28},{24,16},{28,20},{1,9},{5... | collective-permute-start | bytes 1327112 | tf_op jit(solution)/shard_map/ppermute | solution.py:90
  44.1 30.9 %collective-permute-start.12 = (bf16[3,96,768]{2,1,0:T(8,128)(2,1)S(1)}, bf16[3,96,768]{2,1,0:T(8,128)(2,1)S(1)}, u32[]{:S(2)}, u32[]{:S(2)}) collective-permute-start(bf16[3,96,768]{2,1,0:T(8,128)(2,1)S(1)} %get-tuple-element.161), channel_id=1, source_target_pairs={{0,24},{4,28},{8,16},{12,20},{16,8},{20,12},{24,0},{28,4},{1,25},{... | collective-permute-start | bytes 1327112 | tf_op jit(solution)/shard_map/ppermute | solution.py:90
  58.1 50.8 %collective-permute-start.20 = (bf16[4,3,96,768]{3,2,1,0:T(8,128)(2,1)}, bf16[4,3,96,768]{3,2,1,0:T(8,128)(2,1)S(1)}, u32[]{:S(2)}, u32[]{:S(2)}) collective-permute-start(bf16[4,3,96,768]{3,2,1,0:T(8,128)(2,1)} %get-tuple-element.135), channel_id=1, source_target_pairs={{0,4},{4,0},{8,12},{12,8},{16,20},{20,16},{24,28},{28,24},{1,5},{5... | collective-permute-start | bytes 5308424 | tf_op jit(solution)/shard_map/ppermute | solution.py:90
  77.0 42.1 %collective-permute-start.13 = (bf16[4,3,96,768]{3,2,1,0:T(8,128)(2,1)}, bf16[4,3,96,768]{3,2,1,0:T(8,128)(2,1)}, u32[]{:S(2)}, u32[]{:S(2)}) collective-permute-start(bf16[4,3,96,768]{3,2,1,0:T(8,128)(2,1)} %get-tuple-element.139), channel_id=1, source_target_pairs={{0,4},{4,0},{8,12},{12,8},{16,20},{20,16},{24,28},{28,24},{1,5},{5... | collective-permute-start | bytes 5308424 | tf_op jit(solution)/shard_map/ppermute | solution.py:90
  81.7 20.7 %collective-permute-start.5 = (bf16[3,96,768]{2,1,0:T(8,128)(2,1)S(1)}, bf16[3,96,768]{2,1,0:T(8,128)(2,1)S(1)}, u32[]{:S(2)}, u32[]{:S(2)}) collective-permute-start(bf16[3,96,768]{2,1,0:T(8,128)(2,1)S(1)} %get-tuple-element.159), channel_id=1, source_target_pairs={{0,24},{4,28},{8,16},{12,20},{16,8},{20,12},{24,0},{28,4},{1,25},{... | collective-permute-start | bytes 1327112 | tf_op jit(solution)/shard_map/ppermute | solution.py:90
  104.4 34.9 %collective-permute-start.6 = (bf16[4,3,96,768]{3,2,1,0:T(8,128)(2,1)}, bf16[4,3,96,768]{3,2,1,0:T(8,128)(2,1)}, u32[]{:S(2)}, u32[]{:S(2)}) collective-permute-start(bf16[4,3,96,768]{3,2,1,0:T(8,128)(2,1)} %get-tuple-element.137), channel_id=1, source_target_pairs={{0,4},{4,0},{8,12},{12,8},{16,20},{20,16},{24,28},{28,24},{1,5},{5... | collective-permute-start | bytes 5308424 | tf_op jit(solution)/shard_map/ppermute | solution.py:90
  263.2 98.9 %collective-permute-start.45 = (bf16[4,4,96,768]{3,2,1,0:T(8,128)(2,1)}, bf16[4,4,96,768]{3,2,1,0:T(8,128)(2,1)}, u32[]{:S(2)}, u32[]{:S(2)}) collective-permute-start(bf16[4,4,96,768]{3,2,1,0:T(8,128)(2,1)} %slice_bitcast_fusion), channel_id=1, source_target_pairs={{0,4},{4,0},{8,12},{12,8},{16,20},{20,16},{24,28},{28,24},{1,5},{5... | collective-permute-start | bytes 7077896 | tf_op jit(solution)/shard_map/ppermute | solution.py:90
  314.0 56.1 %collective-permute-start.21 = (bf16[4,4,96,768]{3,2,0,1:T(8,128)(2,1)}, bf16[4,4,96,768]{3,2,0,1:T(8,128)(2,1)}, u32[]{:S(2)}, u32[]{:S(2)}) collective-permute-start(bf16[4,4,96,768]{3,2,0,1:T(8,128)(2,1)} %slice_bitcast_fusion.2), channel_id=1, source_target_pairs={{0,4},{4,0},{8,12},{12,8},{16,20},{20,16},{24,28},{28,24},{1,5},{5... | collective-permute-start | bytes 7077896 | tf_op jit(solution)/shard_map/ppermute | solution.py:90
  315.7 57.5 %collective-permute-start.33 = (bf16[4,4,96,768]{3,2,1,0:T(8,128)(2,1)}, bf16[4,4,96,768]{3,2,1,0:T(8,128)(2,1)}, u32[]{:S(2)}, u32[]{:S(2)}) collective-permute-start(bf16[4,4,96,768]{3,2,1,0:T(8,128)(2,1)} %slice_bitcast_fusion.1), channel_id=1, source_target_pairs={{0,4},{4,0},{8,12},{12,8},{16,20},{20,16},{24,28},{28,24},{1,5},{5... | collective-permute-start | bytes 7077896 | tf_op jit(solution)/shard_map/ppermute | solution.py:90
  366.2 26.6 %collective-permute-start.48 = (bf16[4,2,96,384]{3,2,1,0:T(8,128)(2,1)}, bf16[4,2,96,384]{3,2,1,0:T(8,128)(2,1)}, u32[]{:S(2)}, u32[]{:S(2)}) collective-permute-start(bf16[4,2,96,384]{3,2,1,0:T(8,128)(2,1)} %slice.423), channel_id=1, source_target_pairs={{0,16},{4,20},{8,24},{12,28},{16,0},{20,4},{24,8},{28,12},{1,17},{... | collective-permute-start | bytes 1769480 | tf_op jit(solution)/shard_map/ppermute | solution.py:90
  369.9 24.7 %collective-permute-start.46 = (bf16[4,2,96,384]{3,2,0,1:T(8,128)(2,1)}, bf16[4,2,96,384]{3,2,0,1:T(8,128)(2,1)}, u32[]{:S(2)}, u32[]{:S(2)}) collective-permute-start(bf16[4,2,96,384]{3,2,0,1:T(8,128)(2,1)} %bitcast.161), channel_id=1, source_target_pairs={{0,8},{4,12},{8,0},{12,4},{16,24},{20,28},{24,16},{28,20},{1,9},{5... | collective-permute-start | bytes 1769480 | tf_op jit(solution)/shard_map/ppermute | solution.py:90
  391.4 23.6 %collective-permute-start.24 = (bf16[4,2,96,384]{3,2,0,1:T(8,128)(2,1)}, bf16[4,2,96,384]{3,2,0,1:T(8,128)(2,1)S(1)}, u32[]{:S(2)}, u32[]{:S(2)}) collective-permute-start(bf16[4,2,96,384]{3,2,0,1:T(8,128)(2,1)} %slice.386), channel_id=1, source_target_pairs={{0,16},{4,20},{8,24},{12,28},{16,0},{20,4},{24,8},{28,12},{1,17},{... | collective-permute-start | bytes 1769480 | tf_op jit(solution)/shard_map/ppermute | solution.py:90
  392.9 24.4 %collective-permute-start.22 = (bf16[4,2,96,384]{3,2,0,1:T(8,128)(2,1)}, bf16[4,2,96,384]{3,2,0,1:T(8,128)(2,1)S(1)}, u32[]{:S(2)}, u32[]{:S(2)}) collective-permute-start(bf16[4,2,96,384]{3,2,0,1:T(8,128)(2,1)} %bitcast.420), channel_id=1, source_target_pairs={{0,8},{4,12},{8,0},{12,4},{16,24},{20,28},{24,16},{28,20},{1,9},{5... | collective-permute-start | bytes 1769480 | tf_op jit(solution)/shard_map/ppermute | solution.py:90
  394.6 28.5 %collective-permute-start.49 = (bf16[4,96,384]{2,1,0:T(8,128)(2,1)S(1)}, bf16[4,96,384]{2,1,0:T(8,128)(2,1)S(1)}, u32[]{:S(2)}, u32[]{:S(2)}) collective-permute-start(bf16[4,96,384]{2,1,0:T(8,128)(2,1)S(1)} %slice_bitcast_fusion.5), channel_id=1, source_target_pairs={{0,8},{4,12},{8,0},{12,4},{16,24},{20,28},{24,16},{28,20},{1,9},{5... | collective-permute-start | bytes 884744 | tf_op jit(solution)/shard_map/ppermute | solution.py:90
  402.3 20.9 %collective-permute-start.47 = (bf16[4,96,384]{2,1,0:T(8,128)(2,1)S(1)}, bf16[4,96,384]{2,1,0:T(8,128)(2,1)S(1)}, u32[]{:S(2)}, u32[]{:S(2)}) collective-permute-start(bf16[4,96,384]{2,1,0:T(8,128)(2,1)S(1)} %slice_bitcast_fusion.7), channel_id=1, source_target_pairs={{0,16},{4,20},{8,24},{12,28},{16,0},{20,4},{24,8},{28,12},{1,17},{... | collective-permute-start | bytes 884744 | tf_op jit(solution)/shard_map/ppermute | solution.py:90
  405.7 23.7 %collective-permute-start.37 = (bf16[4,96,384]{2,1,0:T(8,128)(2,1)S(1)}, bf16[4,96,384]{2,1,0:T(8,128)(2,1)S(1)}, u32[]{:S(2)}, u32[]{:S(2)}) collective-permute-start(bf16[4,96,384]{2,1,0:T(8,128)(2,1)S(1)} %slice_bitcast_fusion.9), channel_id=1, source_target_pairs={{0,8},{4,12},{8,0},{12,4},{16,24},{20,28},{24,16},{28,20},{1,9},{5... | collective-permute-start | bytes 884744 | tf_op jit(solution)/shard_map/ppermute | solution.py:90
  417.3 18.5 %collective-permute-start.25 = (bf16[4,96,384]{2,1,0:T(8,128)(2,1)S(1)}, bf16[4,96,384]{2,1,0:T(8,128)(2,1)S(1)}, u32[]{:S(2)}, u32[]{:S(2)}) collective-permute-start(bf16[4,96,384]{2,1,0:T(8,128)(2,1)S(1)} %slice_bitcast_fusion.13), channel_id=1, source_target_pairs={{0,8},{4,12},{8,0},{12,4},{16,24},{20,28},{24,16},{28,20},{1,9},{5... | collective-permute-start | bytes 884744 | tf_op jit(solution)/shard_map/ppermute | solution.py:90
  423.1 32.1 %collective-permute-start.23 = (bf16[4,96,384]{2,1,0:T(8,128)(2,1)S(1)}, bf16[4,96,384]{2,1,0:T(8,128)(2,1)S(1)}, u32[]{:S(2)}, u32[]{:S(2)}) collective-permute-start(bf16[4,96,384]{2,1,0:T(8,128)(2,1)S(1)} %slice_bitcast_fusion.15), channel_id=1, source_target_pairs={{0,16},{4,20},{8,24},{12,28},{16,0},{20,4},{24,8},{28,12},{1,17},{... | collective-permute-start | bytes 884744 | tf_op jit(solution)/shard_map/ppermute | solution.py:90
  463.5 21.6 %collective-permute-start.56 = (bf16[4,96,768]{2,1,0:T(8,128)(2,1)S(1)}, bf16[4,96,768]{2,1,0:T(8,128)(2,1)S(1)}, u32[]{:S(2)}, u32[]{:S(2)}) collective-permute-start(bf16[4,96,768]{2,1,0:T(8,128)(2,1)S(1)} %get-tuple-element.142), channel_id=1, source_target_pairs={{0,4},{4,0},{8,12},{12,8},{16,20},{20,16},{24,28},{28,24},{1,5},{5... | collective-permute-start | bytes 1769480 | tf_op jit(solution)/shard_map/ppermute | solution.py:90
  (96 other events, 870.2 us)

commit v2 on v1

v2 whole, which is shorter than its diff:
```python
import functools
import math

import jax
import jax.numpy as jnp
from jax import lax
from jax.experimental import pallas as pl
from jax.experimental.pallas import tpu as pltpu
from jax.sharding import PartitionSpec as P

HEAD_DIM = 64
PASSAGE = 128
GROUP = 8
EXTRA = 8
LANES = 128
CHUNK = 64
SCOPED = {
    "first_piece": 60,
    "att_forward": 9,
    "ffn_first": 7,
    "ffn_last": 12,
    "ffn_backward": 18,
    "att_backward": 13,
    "input_backward": 6,
    "finish_down": 6,
    "finish_up": 6,
    "finish_att": 8,
}
epsilon = 1e-05
bf16 = jnp.bfloat16
f32 = jnp.float32


def nn(left, right):
    return lax.dot_general(left, right, (((1,), (0,)), ((), ())), preferred_element_type=f32)


def nt(left, right):
    return lax.dot_general(left, right, (((1,), (1,)), ((), ())), preferred_element_type=f32)


def tn(left, right):
    return lax.dot_general(left, right, (((0,), (0,)), ((), ())), preferred_element_type=f32)


def call(body, name, outs, args, spaces, scratch=(), out_spaces=None):
    def spec(kind):
        if kind == "s":
            return pl.BlockSpec(memory_space=pltpu.SMEM)
        if kind == "h":
            return pl.BlockSpec(memory_space=pltpu.HBM)
        return pl.BlockSpec(memory_space=pltpu.VMEM)

    out_spaces = out_spaces or "v" * len(outs)
    def size(array):
        return math.prod(array.shape) * jnp.dtype(array.dtype).itemsize

    every = list(zip(args, spaces)) + list(zip(outs, out_spaces))
    moved = sum(size(array) for array, kind in every)
    return pl.pallas_call(
        body,
        name=name,
        out_shape=tuple(outs),
        in_specs=[spec(k) for k in spaces],
        out_specs=tuple(spec(k) for k in out_spaces),
        scratch_shapes=list(scratch),
        compiler_params=pltpu.CompilerParams(vmem_limit_bytes=SCOPED[name] << 20),
        cost_estimate=pl.CostEstimate(flops=0, bytes_accessed=moved // 64, transcendentals=0),
    )(*args)


def vector(ref):
    return ref[...].astype(f32).reshape(1, ref.shape[0])


def places_by_axis(index):
    x, y = index & 3, ((index >> 1) & 2) | (index & 1)
    return [x, x ^ 1, x ^ 2, x ^ 3, 4 + y, 4 + (y ^ 1), 4 + (y ^ 2), 4 + (y ^ 3)]


def place_slots(four, other, r, low, rows, places, dest, base, columns):
    for s in range(GROUP):
        at = pl.multiple_of(base + places[s] * rows, rows)
        dest[pl.ds(at, rows), columns] = (other if s % 2 else four)[s // 2, r, low : low + rows]


def put_slots(index, r, rows, low, keep, send):
    size = rows[0].shape[0]
    for odd in range(2):

        @pl.when((index & 1) == odd)
        def _():
            for d in range(GROUP):
                dest = send if (d ^ odd) & 1 else keep
                dest[(index ^ d) >> 1, r, low : low + size] = rows[d]


def normalize(total):
    centred = total - jnp.mean(total, axis=-1, keepdims=True)
    inverse = lax.rsqrt(jnp.mean(centred * centred, axis=-1, keepdims=True) + epsilon)
    return centred * inverse, inverse


def norm_backward(grad_out, normal, inverse, norm_gain):
    scaled = grad_out * norm_gain
    return inverse * (
        scaled
        - jnp.mean(scaled, axis=-1, keepdims=True)
        - normal * jnp.mean(scaled * normal, axis=-1, keepdims=True)
    )


def column_sum(array):
    return jnp.sum(array, axis=0, keepdims=True)


def folded(array):
    return jnp.sum(array.reshape(-1, 8, array.shape[1]), axis=0)


def by_rows(length, body, sums, width):
    def step(i, totals):
        found = body(pl.ds(pl.multiple_of(i * CHUNK, CHUNK), CHUNK))
        return tuple(t + folded(f) for t, f in zip(totals, found))

    zeros = tuple(jnp.zeros((8, width), f32) for _ in range(sums))
    totals = lax.fori_loop(0, length // CHUNK, step, zeros, unroll=2)
    return tuple(column_sum(t) for t in totals)


def band(block, length):
    return max(0, (block - 1) * PASSAGE), min(length, (block + 2) * PASSAGE)


def clear_outside(array, length):
    for b in range(length // PASSAGE):
        lo, hi = band(b, length)
        block = slice(b * PASSAGE, (b + 1) * PASSAGE)
        for low, high in ((0, lo), (hi, length)):
            if high > low:
                shape = (array.shape[0], high - low, PASSAGE)
                array[:, low:high, block] = jnp.zeros(shape, array.dtype)


def fill_bias(bias, seg_row, seg_col, length):
    for b in range(length // PASSAGE):
        lo, hi = band(b, length)
        same = seg_col[lo:hi, :] == seg_row[:, b * PASSAGE : (b + 1) * PASSAGE]
        bias[b, : hi - lo, :] = jnp.where(same, 0.0, -1e30)


def softmax_columns(scores):
    expo = jnp.exp(scores - jnp.max(scores, axis=0, keepdims=True))
    return expo * (1.0 / jnp.sum(expo, axis=0, keepdims=True))


def first_piece(
    index_ref, own_q, own_k, own_v, own_o, query_bias, value_bias, up_bias, out, owns,
    query_row, value_row, up_row, sems,
):
    w = own_q.shape[0]
    rows = w // 2
    small = [
        pltpu.make_async_copy(own, owns.at[pl.ds(m * w, w)], sems.at[3 + m])
        for m, own in enumerate((own_q, own_k, own_v, own_o))
    ]
    small += [
        pltpu.make_async_copy(query_bias, query_row, sems.at[0]),
        pltpu.make_async_copy(value_bias, value_row, sems.at[1]),
        pltpu.make_async_copy(up_bias, up_row, sems.at[2]),
    ]
    for copy in small:
        copy.start()
    for copy in small:
        copy.wait()
    out[:rows, :] = owns[pl.ds(pl.multiple_of(index_ref[0] * rows, rows), rows), :]
    out[rows:, :] = jnp.zeros((EXTRA, out.shape[1]), bf16)
    out[rows : rows + 1, :w] = vector(query_row).astype(bf16)
    out[rows : rows + 1, w : 2 * w] = vector(value_row).astype(bf16)
    out[rows + 1 : rows + 2, :] = vector(up_row).astype(bf16)


def att_forward(
    index_ref, tokens, owns, four, other, bias_0, bias_1, bias_2, bias_3,
    output_bias, seg_row, seg_col,
    queries, keys, values, contexts, normal, inverse, weights, wo,
    bias, probs_t, row, attended,
):
    length, width = tokens.shape
    w = owns.shape[0] // 4
    quarters = width // w
    rows = four.shape[2]
    index = index_ref[0]
    for m in range(3):
        weights[m, :w, :] = owns[m * w : (m + 1) * w, :]
    wo[:w, :] = owns[3 * w :, :]
    for r in range(1, quarters):
        for s in range(GROUP):
            owner = index ^ s
            at = pl.multiple_of(r * w + (owner & 1) * rows, rows)
            source = other if s % 2 else four

            @pl.when(owner < 6)
            def _():
                weights[owner >> 1, pl.ds(at, rows), :] = source[s // 2, r - 1]

            @pl.when(owner >= 6)
            def _():
                wo[pl.ds(at, rows), :] = source[s // 2, r - 1]

    fill_bias(bias, seg_row, seg_col, length)
    clear_outside(probs_t, length)
    for r, source in enumerate((bias_0, bias_1, bias_2, bias_3)):
        for i in range(2):
            piece = source[rows : rows + 1, i * w : (i + 1) * w].astype(f32)
            row[i : i + 1, r * w : (r + 1) * w] = piece
    low = (nt(tokens[...], weights[0]) + row[0:1, :]).astype(bf16)
    queries[...] = (low.astype(f32) * (HEAD_DIM**-0.5)).astype(bf16)
    keys[...] = nt(tokens[...], weights[1]).astype(bf16)
    values[...] = (nt(tokens[...], weights[2]) + row[1:2, :]).astype(bf16)
    first = lax.broadcasted_iota(jnp.int32, (PASSAGE, LANES), 1) < HEAD_DIM
    first_all = lax.broadcasted_iota(jnp.int32, (length, LANES), 1) < HEAD_DIM

    def pair(i, carry):
        at = pl.ds(pl.multiple_of(i * LANES, LANES), LANES)
        for half, mine in enumerate((first, jnp.logical_not(first))):
            for b in range(length // PASSAGE):
                lo, hi = band(b, length)
                block = slice(b * PASSAGE, (b + 1) * PASSAGE)
                q = queries[block, at]
                masked = jnp.where(mine, q, jnp.zeros_like(q))
                scores = nt(keys[lo:hi, at], masked) + bias[b, : hi - lo, :]
                probs_t[half, lo:hi, block] = softmax_columns(scores).astype(bf16)
        found = [tn(probs_t[half], values[:, at]) for half in range(2)]
        contexts[:, at] = jnp.where(first_all, *found).astype(bf16)
        return carry

    lax.fori_loop(0, width // LANES, pair, 0)
    attended[...] = nn(contexts[...], wo[...]) + vector(output_bias)

    def norm(rows):
        n, r = normalize(tokens[rows, :].astype(f32) + attended[rows, :])
        normal[rows, :] = n
        inverse[rows, :] = r
        return ()

    by_rows(length, norm, 0, width)


def gelu_parts(hidden):
    cumulative = 0.5 * (1.0 + lax.erf(hidden * 0.7071067811865476))
    density = jnp.exp(-0.5 * hidden * hidden) * 0.3989422804014327
    return (hidden * cumulative).astype(bf16), (cumulative + hidden * density).astype(bf16)


def ffn_first(
    index_ref, normal, gain, shift, down_bias, bias_0, bias_1, bias_2, own_up, own_down, four, other,
    activated, slope, low_t, mixed, up, down,
):
    units = own_up.shape[1]
    rows = four.shape[2] // 2
    quarters = four.shape[1] + 1
    biases = (bias_0, bias_1, bias_2)
    places = places_by_axis(index_ref[0])
    normed = normal[...] * vector(gain) + vector(shift)
    low = normed.astype(bf16)
    low_t[...] = low.T
    mixed[...] = normed + vector(down_bias)
    for r in range(quarters):
        mine = slice(r * units, (r + 1) * units)
        if r == 0:
            up[:, mine] = own_up[...]
            down[mine, :] = own_down[...]
        else:
            place_slots(four, other, r - 1, 0, rows, places, up, 0, mine)
            place_slots(four, other, r - 1, rows, rows, places, down, r * units, slice(None))
        at = biases[r].shape[0] - EXTRA + 1
        hidden = nn(low, up[:, mine]) + biases[r][at : at + 1, :].astype(f32)
        activated[:, mine], slope[:, mine] = gelu_parts(hidden)
    mixed[...] += nn(activated[...], down[...])


def ffn_last(
    index_ref, normal, cotangent, gain, shift, second_gain, second_shift, bias, activated, mixed,
    four, other,
    output, grad_mixed, grad_two, sums, slope, up, down, keep, send,
    own, total,
):
    length, width = normal.shape
    units = up.shape[1]
    rows = four.shape[2] // 2
    index = index_ref[0]
    places = places_by_axis(index)
    place_slots(four, other, 0, 0, rows, places, up, 0, slice(None))
    place_slots(four, other, 0, rows, rows, places, down, 0, slice(None))
    low = (normal[...] * vector(gain) + vector(shift)).astype(bf16)
    at = bias.shape[0] - EXTRA + 1
    own[...], slope[...] = gelu_parts(nn(low, up[...]) + bias[at : at + 1, :].astype(f32))
    total[...] = mixed[...] + nn(own[...], down[...])
    out_gain, out_shift = vector(second_gain), vector(second_shift)

    def norm(rows):
        n, inverse = normalize(total[rows, :])
        output[rows, :] = (n * out_gain + out_shift).astype(bf16)
        grad_out = cotangent[rows, :].astype(f32)
        two = norm_backward(grad_out, n, inverse, out_gain)
        grad_two[rows, :] = two
        low = two.astype(bf16)
        grad_mixed[rows, :] = low
        return low.astype(f32), grad_out * n, grad_out

    sums[...] = jnp.zeros_like(sums)
    for i, found in enumerate(by_rows(length, norm, 3, width)):
        sums[i : i + 1, :] = found
    quarters = keep.shape[1]
    for r in range(quarters):
        left = own[...] if r == quarters - 1 else activated[:, r * units : (r + 1) * units]
        grad = tn(left, grad_mixed[...]).astype(bf16)
        put_slots(index, r, grad.reshape(GROUP, -1, width), 0, keep, send)


def ffn_backward(
    index_ref, grad_mixed, low_t, slope, slope_last, grad_two, normal, inverse, gain_ref, sums_two,
    up, up_last, down, down_last,
    grad_one, grad_attended, keep, send,
    hidden, total,
):
    length, width = grad_mixed.shape
    units = down_last.shape[0]
    quarters, rows = keep.shape[1], keep.shape[2] - EXTRA
    index = index_ref[0]
    low_sums = []
    for r in range(quarters):
        mine = slice(r * units, (r + 1) * units)
        last = r == quarters - 1
        weight = down_last[...] if last else down[mine, :]
        factor = slope_last[...] if last else slope[:, mine]
        low = (nt(grad_mixed[...], weight) * factor.astype(f32)).astype(bf16)
        hidden[:, mine] = low
        low_sums.append(column_sum(low.astype(f32)))
        grad = nn(low_t[...], low).astype(bf16)
        put_slots(index, r, grad.reshape(GROUP, rows, units), 0, keep, send)
    inner = up.shape[1]
    total[...] = nt(hidden[:, :inner], up[...]) + grad_two[...]
    total[...] += nt(hidden[:, inner:], up_last[...])
    gain = vector(gain_ref)

    def norm(at):
        grad_normed = total[at, :]
        n = normal[at, :]
        one = norm_backward(grad_normed, n, inverse[at, :], gain)
        grad_one[at, :] = one
        low = one.astype(bf16)
        grad_attended[at, :] = low
        return low.astype(f32), grad_normed * n, grad_normed

    shared = list(by_rows(length, norm, 3, width))
    shared += [sums_two[i : i + 1, :] for i in range(3)] + [jnp.zeros_like(gain)]
    for r in range(quarters):
        extra = [
            jnp.broadcast_to(total, (EXTRA, units)).astype(bf16) for total in [low_sums[r]] + shared
        ]
        put_slots(index, r, jnp.stack(extra), rows, keep, send)


def att_backward(
    part, index_ref, queries, keys, values, contexts, grad_attended, tokens, wo, seg_row, seg_col,
    grad_queries, grad_keys, grad_values, keep, send,
    grad_contexts, bias, probs_t, scores_t,
):
    length, width = tokens.shape
    quarters, rows = keep.shape[1], keep.shape[2] - EXTRA
    w = 2 * rows
    across = quarters * w
    index = index_ref[0]
    scale = HEAD_DIM**-0.5
    low = part * across
    fill_bias(bias, seg_row, seg_col, length)
    clear_outside(probs_t, length)
    clear_outside(scores_t, length)
    grad_contexts[...] = nt(grad_attended[...], wo[low : low + across, :]).astype(bf16)
    first = lax.broadcasted_iota(jnp.int32, (PASSAGE, LANES), 1) < HEAD_DIM
    first_all = lax.broadcasted_iota(jnp.int32, (length, LANES), 1) < HEAD_DIM

    def pair(i, carry):
        here = pl.ds(pl.multiple_of(i * LANES, LANES), LANES)
        at = pl.ds(pl.multiple_of(low + i * LANES, LANES), LANES)
        found = []
        for half, mine in enumerate((first, jnp.logical_not(first))):
            for b in range(length // PASSAGE):
                lo, hi = band(b, length)
                block = slice(b * PASSAGE, (b + 1) * PASSAGE)
                q = queries[block, at]
                g = grad_contexts[block, here]
                zero = jnp.zeros_like(q)
                scores = nt(keys[lo:hi, at], jnp.where(mine, q, zero)) + bias[b, : hi - lo, :]
                probs = softmax_columns(scores)
                grad_probs = nt(values[lo:hi, at], jnp.where(mine, g, zero))
                inner = jnp.sum(grad_probs * probs, axis=0, keepdims=True)
                probs_t[half, lo:hi, block] = probs.astype(bf16)
                scores_t[half, lo:hi, block] = (probs * (grad_probs - inner)).astype(bf16)
            found.append(
                (
                    tn(scores_t[half], keys[:, at]),
                    nn(scores_t[half], queries[:, at]),
                    nn(probs_t[half], grad_contexts[:, here]),
                )
            )
        dq, dk, dv = (jnp.where(first_all, a, b) for a, b in zip(*found))
        grad_queries[:, here] = (dq * scale).astype(bf16)
        grad_keys[:, here] = dk.astype(bf16)
        grad_values[:, here] = dv.astype(bf16)
        return carry

    lax.fori_loop(0, across // LANES, pair, 0)
    grads = (
        lambda: tn(grad_queries[...], tokens[...]),
        lambda: tn(grad_keys[...], tokens[...]),
        lambda: tn(grad_values[...], tokens[...]),
        lambda: tn(contexts[:, low : low + across], grad_attended[...]),
    )
    grads = [make().astype(bf16).reshape(quarters, 2, rows, width) for make in grads]
    query_sum = column_sum(grad_queries[...].astype(f32))
    value_sum = column_sum(grad_values[...].astype(f32))
    for r in range(quarters):
        put_slots(index, r, [grads[d // 2][r, d % 2] for d in range(GROUP)], 0, keep, send)
        cols = slice(r * w, (r + 1) * w)
        line = jnp.concatenate(
            [query_sum[:, cols], value_sum[:, cols], jnp.zeros((1, width - 2 * w), f32)], axis=1
        )
        line = jnp.broadcast_to(line, (EXTRA, width)).astype(bf16)
        put_slots(index, r, [line] * GROUP, rows, keep, send)


def input_backward(q0, k0, v0, q1, k1, v1, grad_one, weights, out):
    half = q0.shape[1]
    total = grad_one[...]
    for m, (left, right) in enumerate(((q0, q1), (k0, k1), (v0, v1))):
        total += nn(left[...], weights[m, :half]) + nn(right[...], weights[m, half:])
    out[...] = total.astype(bf16)


def finish_down(index_ref, four, other, out):
    rows = four.shape[1]
    for s in range(GROUP):
        at = pl.multiple_of((index_ref[0] ^ s) * rows, rows)
        out[pl.ds(at, rows), :] = (other if s % 2 else four)[s // 2].astype(f32)


def finish_up(index_ref, four, other, out, sums):
    rows = four.shape[1] - EXTRA
    for s in range(GROUP):
        owner = index_ref[0] ^ s
        slot = (other if s % 2 else four)[s // 2].astype(f32)
        out[pl.ds(pl.multiple_of(owner * rows, rows), rows), :] = slot[:rows]
        sums[pl.ds(pl.multiple_of(owner * EXTRA, EXTRA), EXTRA), :] = slot[rows:]


def finish_att(index_ref, four, other, gq, gk, gv, go, sums, whole):
    rows = four.shape[1] - EXTRA
    w = 2 * rows
    for s in range(GROUP):
        slot = (other if s % 2 else four)[s // 2].astype(f32)
        owner = index_ref[0] ^ s
        whole[pl.ds(pl.multiple_of(owner * rows, rows), rows), :] = slot[:rows]
        sums[pl.ds(pl.multiple_of(owner * EXTRA, EXTRA), EXTRA), :] = slot[rows:]
    for m, out in enumerate((gq, gk, gv, go)):
        out[...] = whole[m * w : (m + 1) * w, :]


def solution(mesh):
    n_dp, n_mp = mesh.shape["dp"], mesh.shape["mp"]
    if n_dp % GROUP or n_mp % 2:
        raise ValueError("mesh")

    def rotate(array, step):
        return lax.ppermute(array, "mp", [(i, (i + step) % n_mp) for i in range(n_mp)])

    def swap(array, bits):
        return lax.ppermute(array, "dp", [(i, i ^ bits) for i in range(n_dp)])

    def plane_swap(array):
        return [array, swap(array, 2), swap(array, 4), swap(array, 6)]

    def add(left, right):
        return (left.astype(f32) + right.astype(f32)).astype(bf16)

    def tie(*arrays):
        return lax.optimization_barrier(arrays)

    def after(array, *others):
        return tie(array, *others)[0]

    def first_axis(bits):
        go = slice(1, None, 2) if bits == 2 else slice(2, None)
        stay = slice(0, None, 2) if bits == 2 else slice(0, 2)
        return go, stay

    def plane_first(keep, got, bits):
        go, stay = first_axis(bits)
        return add(keep[go], got[go]), add(keep[stay], got[stay])

    def line_moves(parts):
        return [parts[0]] + [rotate(parts[r], -r) for r in range(1, n_mp)]

    def line_total(moved):
        moved = [array.astype(f32) for array in moved]
        total = sum(moved[0::2][1:], moved[0]) + sum(moved[1::2][1:], moved[1])
        if n_dp > GROUP:
            groups = [[i + GROUP * k for k in range(n_dp // GROUP)] for i in range(GROUP)]
            total = lax.psum(total, "dp", axis_index_groups=groups)
        return total.astype(bf16)

    def shards(
        tokens,
        segment_ids,
        query_weight,
        query_bias,
        key_weight,
        value_weight,
        value_bias,
        output_weight,
        output_bias,
        first_gain,
        first_shift,
        up_weight,
        up_bias,
        down_weight,
        down_bias,
        second_gain,
        second_shift,
        cotangent,
    ):
        length, width = tokens.shape
        w = query_weight.shape[1]
        units = up_weight.shape[1]
        rows = width // GROUP
        blocks = length // PASSAGE
        half, part = GROUP // 2, units // GROUP
        shape = jax.ShapeDtypeStruct
        place = lax.axis_index("mp")
        within = lax.axis_index("dp") % GROUP
        index = within.astype(jnp.int32).reshape(1)
        seg_row = lax.dynamic_slice_in_dim(segment_ids, place, 1, 0)
        seg_col = seg_row.reshape(length, 1)

        def slot(array, at, size):
            return lax.dynamic_slice_in_dim(array, at * size, size, 0)

        owns = [query_weight.T, key_weight.T, value_weight.T, output_weight]
        piece, owns = call(
            first_piece,
            "first_piece",
            [shape((rows + EXTRA, width), bf16), shape((4 * w, width), bf16)],
            [index, *owns, query_bias, value_bias, up_bias],
            "s" + "h" * 7,
            [
                pltpu.VMEM((w,), bf16),
                pltpu.VMEM((w,), bf16),
                pltpu.VMEM((units,), bf16),
                pltpu.SemaphoreType.DMA((7,)),
            ],
        )
        biases = [piece] + [rotate(piece, r) for r in range(1, n_mp)]
        att_line = jnp.stack([g[:rows] for g in biases[1:]])
        by_x, by_y = within & 3, ((within >> 1) & 2) | (within & 1)
        piece = jnp.concatenate(
            [
                slot(up_weight, by_x, rows),
                slot(down_weight, by_x, part),
                slot(up_weight, 4 + by_y, rows),
                slot(down_weight, 4 + by_y, part),
            ]
        )
        ffn_line = [rotate(piece, r) for r in range(1, n_mp)]

        def plane_by_axis(line):
            cut = line[0].shape[0] // 2
            left = jnp.stack([g[:cut] for g in line])
            right = jnp.stack([g[cut:] for g in line])
            return left, swap(left, 2), right, swap(right, 4)

        att_four = jnp.stack([att_line] + [swap(att_line, b) for b in (2, 4, 6)])
        att_other = swap(att_four, 1)
        ffn_four = plane_by_axis(ffn_line[:-1])

        tok_low = shape((length, width), bf16)
        tok_wide = shape((length, width), f32)
        queries, keys, values, contexts, normal, inverse, weights, wo = call(
            att_forward,
            "att_forward",
            [tok_low] * 4
            + [
                tok_wide,
                shape((length, 1), f32),
                shape((3, n_mp * w, width), bf16),
                shape((n_mp * w, width), bf16),
            ],
            [
                index,
                tokens,
                owns,
                att_four,
                att_other,
                *biases,
                output_bias,
                seg_row,
                seg_col,
            ],
            "s" + "v" * 11,
            [
                pltpu.VMEM((blocks, 3 * PASSAGE, PASSAGE), f32),
                pltpu.VMEM((2, length, length), bf16),
                pltpu.VMEM((8, width), f32),
                pltpu.VMEM((length, width), f32),
            ],
        )
        normal, ffn_four, ffn_line[-1] = tie(normal, ffn_four, ffn_line[-1])
        ffn_four = jnp.stack(ffn_four)
        ffn_other = swap(ffn_four, 1)
        last_four = plane_by_axis(ffn_line[-1:])
        inner = (n_mp - 1) * units
        hidden_low = shape((length, inner), bf16)
        activated, slope, low_t, mixed, up, down = call(
            ffn_first,
            "ffn_first",
            [
                hidden_low,
                hidden_low,
                shape((width, length), bf16),
                tok_wide,
                shape((width, inner), bf16),
                shape((inner, width), bf16),
            ],
            [
                index,
                normal,
                first_gain,
                first_shift,
                down_bias,
                *biases[:-1],
                up_weight,
                down_weight,
                ffn_four,
                ffn_other,
            ],
            "s" + "v" * 11,
        )
        activated, last_four = tie(activated, last_four)
        last_four = jnp.stack(last_four)
        last_other = swap(last_four, 1)
        pieces = shape((half, n_mp, part, width), bf16)
        (
            output,
            grad_mixed,
            grad_two,
            sums_two,
            slope_last,
            up_last,
            down_last,
            keep_down,
            send_down,
        ) = call(
            ffn_last,
            "ffn_last",
            [
                tok_low,
                tok_low,
                tok_wide,
                shape((8, width), f32),
                shape((length, units), bf16),
                shape((width, units), bf16),
                shape((units, width), bf16),
                pieces,
                pieces,
            ],
            [
                index,
                normal,
                cotangent,
                first_gain,
                first_shift,
                second_gain,
                second_shift,
                biases[-1],
                activated,
                mixed,
                last_four,
                last_other,
            ],
            "s" + "v" * 11,
            [pltpu.VMEM((length, units), bf16), pltpu.VMEM((length, width), f32)],
        )
        got_down = swap(send_down, 1)
        pieces = shape((half, n_mp, rows + EXTRA, units), bf16)
        grad_one, grad_attended, keep_up, send_up = call(
            ffn_backward,
            "ffn_backward",
            [tok_wide, tok_low, pieces, pieces],
            [
                index,
                grad_mixed,
                low_t,
                slope,
                slope_last,
                grad_two,
                normal,
                inverse,
                first_gain,
                sums_two,
                up,
                up_last,
                down,
                down_last,
            ],
            "s" + "v" * 13,
            [pltpu.VMEM((length, n_mp * units), bf16), pltpu.VMEM((length, width), f32)],
        )
        grad_attended, got_down = tie(grad_attended, got_down)
        got_up = swap(send_up, 1)
        leave_down, stay_down = plane_first(keep_down, got_down, 2)
        come_down = swap(leave_down, 2)
        leave_up, stay_up = plane_first(keep_up, got_up, 4)
        come_up = swap(leave_up, 4)
        grad_attended, leave_down, leave_up = tie(grad_attended, leave_down, leave_up)

        halves = n_mp // 2
        across = halves * w
        pieces = shape((half, halves, rows + EXTRA, width), bf16)

        def attention(which, grad_attended):
            return call(
                functools.partial(att_backward, which),
                "att_backward",
                [shape((length, across), bf16)] * 3 + [pieces] * 2,
                [
                    index,
                    queries,
                    keys,
                    values,
                    contexts,
                    grad_attended,
                    tokens,
                    wo,
                    seg_row,
                    seg_col,
                ],
                "s" + "v" * 9,
                [
                    pltpu.VMEM((length, across), bf16),
                    pltpu.VMEM((blocks, 3 * PASSAGE, PASSAGE), f32),
                    pltpu.VMEM((2, length, length), bf16),
                    pltpu.VMEM((2, length, length), bf16),
                ],
            )

        q0, k0, v0, keep_left, send_left = attention(0, grad_attended)
        grad_attended, q0, send_left = tie(grad_attended, q0, send_left)
        got_left = swap(send_left, 1)
        q1, k1, v1, keep_right, send_right = attention(1, grad_attended)
        got_left, come_down, come_up = (
            after(array, q1) for array in (got_left, come_down, come_up)
        )
        q1, k1, v1, keep_right, send_right = tie(q1, k1, v1, keep_right, send_right)
        got_right = swap(send_right, 1)
        down_now = add(stay_down, come_down)
        come_down = swap(down_now[1], 4)
        up_now = add(stay_up, come_up)
        come_up = swap(up_now[1], 2)
        (grad_tokens,) = call(
            input_backward,
            "input_backward",
            [tok_low],
            [q0, k0, v0, q1, k1, v1, grad_one, weights],
            "v" * 8,
        )
        leave_left, stay_left = plane_first(keep_left, got_left, 2)
        leave_right, stay_right = plane_first(keep_right, got_right, 4)
        come_down, come_up, grad_tokens, leave_left, leave_right = tie(
            come_down, come_up, grad_tokens, leave_left, leave_right
        )
        down_parts, up_parts = add(down_now[0], come_down), add(up_now[0], come_up)
        down_line = line_moves(down_parts)
        come_left, come_right = swap(leave_left, 2), swap(leave_right, 4)
        down_line, come_left, come_right, up_parts = tie(
            down_line, come_left, come_right, up_parts
        )
        up_line = line_moves(up_parts)
        left_now, right_now = add(stay_left, come_left), add(stay_right, come_right)
        come_left, come_right = swap(left_now[1], 4), swap(right_now[1], 2)
        down_total = line_total(down_line)
        up_line, come_left, come_right, down_total = tie(
            up_line, come_left, come_right, down_total
        )
        left_parts, right_parts = add(left_now[0], come_left), add(right_now[0], come_right)
        att_line = line_moves(
            [left_parts[r] for r in range(halves)] + [right_parts[r] for r in range(halves)]
        )
        down_four = plane_swap(down_total)
        up_four = plane_swap(line_total(up_line))
        att_line, down_four, up_four = tie(att_line, down_four, up_four)
        att_four = plane_swap(line_total(att_line))
        down_four, up_four = jnp.stack(down_four), jnp.stack(up_four)
        (grad_down,) = call(
            finish_down,
            "finish_down",
            [shape((units, width), f32)],
            [index, down_four, swap(down_four, 1)],
            "svv",
        )
        grad_up, sums = call(
            finish_up,
            "finish_up",
            [shape((width, units), f32), shape((GROUP * EXTRA, units), f32)],
            [index, up_four, swap(up_four, 1)],
            "svv",
        )
        att_four, grad_down, grad_up, sums = tie(att_four, grad_down, grad_up, sums)
        att_four = jnp.stack(att_four)
        att_other = swap(att_four, 1)
        grad_query, grad_key, grad_value, grad_output, att_sums = call(
            finish_att,
            "finish_att",
            [shape((w, width), f32)] * 4 + [shape((GROUP * EXTRA, width), f32)],
            [index, att_four, att_other],
            "svv",
            [pltpu.VMEM((4 * w, width), f32)],
        )
        return (
            output,
            grad_tokens,
            grad_query.T,
            att_sums[0, :w],
            grad_key.T,
            grad_value.T,
            att_sums[0, w : 2 * w],
            grad_output,
            sums[EXTRA],
            sums[2 * EXTRA],
            sums[3 * EXTRA],
            grad_up,
            sums[0],
            grad_down,
            sums[4 * EXTRA],
            sums[5 * EXTRA],
            sums[6 * EXTRA],
        )

    everywhere, rows, columns, units = P(), P(("dp", "mp"), None), P(None, "mp"), P("mp")
    in_specs = (
        rows,
        P("dp", None),
        columns,
        units,
        columns,
        columns,
        units,
        P("mp", None),
        everywhere,
        everywhere,
        everywhere,
        columns,
        units,
        P("mp", None),
        everywhere,
        everywhere,
        everywhere,
        rows,
    )
    out_specs = (
        rows,
        rows,
        columns,
        units,
        columns,
        columns,
        units,
        P("mp", None),
        everywhere,
        everywhere,
        everywhere,
        columns,
        units,
        P("mp", None),
        everywhere,
        everywhere,
        everywhere,
    )
    return jax.shard_map(shards, mesh=mesh, in_specs=in_specs, out_specs=out_specs, check_vma=False)
```

time: 509 us -> 267 us (0.52); the launches traced: 499 us -> 264 us
  local copies, waits for them, and re-layouts: 130 us -> 8.72 us
  matrix products: 84.6 us -> 0 us
  Pallas kernels: 0 us -> 68.2 us
  other arithmetic: 71.9 us -> 9.5 us
  waiting for transfers between devices: 92 us -> 131 us
  blocking collectives: 38.8 us -> 0 us
  starting transfers between devices: 78.3 us -> 44.9 us
    dot_general x24 -> x0, matrix products: 84.6 us -> none  [the longest x6 24.1 us: mm(): return jnp.dot(left, right, preferred_element_type=f32)]
    pallas_call x0 -> x11, Pallas kernels: none -> 68.2 us  [call(): pl.pallas_call(body, name=name, out_shape=tuple(outs), in_specs=[spec(k)...]
    ppermute x18 -> x15, waiting for transfers between devices: 26.5 us -> 71.8 us  [rotate(): lax.ppermute(array, 'mp', [(i, (i + step) % n_mp) for i in range(n_mp)])]
    gather x18 -> x0, local copies, waits for them, and re-layouts: 45.2 us -> none  [the longest x5 23.6 us: reduce_grads(): slots = grads.astype(bf16).reshape(quarters, GROUP, rows, width)[:, order]]
    psum x1 -> x0, blocking collectives: 38.8 us -> none  [shards(): mine, shared = lax.psum((mine, shared), ('dp', 'mp'))]
    transpose x12 -> x0, local copies, waits for them, and re-layouts: 31.7 us -> none  [the longest x5 14.8 us: columns(): return array.transpose(1, 0, 2).reshape(array.shape[1], -1)]
    convert_element_type x24 -> x15, other arithmetic: 26 us -> 2.97 us  [the longest x12 2.72 us: add(): return (left.astype(f32) + right.astype(f32)).astype(bf16)]
    ppermute x39 -> x34, starting transfers between devices: 52.8 us -> 31.3 us  [swap(): return lax.ppermute(array, 'dp', [(i, i ^ bits) for i in range(n_dp)])]
  transfers between devices with their start and end apart: 57 -> 49, of which waited for: 21 -> 27; matrix products, arithmetic and copies ran while one was open for 31% -> 4% of each run, Pallas kernels for 0% -> 21%
where the time goes in v2:
time: 267 us; the launch traced here: 264 us
  waiting for transfers between devices  131 us (49%)
  Pallas kernels  68.2 us (26%)
  starting transfers between devices  44.9 us (17%)
  other arithmetic  9.5 us (4%)
  local copies, waits for them, and re-layouts  8.72 us (3%)
    ppermute x15, waiting for transfers between devices, rotate(): lax.ppermute(array, 'mp', [(i, (i + step) % n_mp) for i in range(n_mp)])  71.8 us
    pallas_call x11, Pallas kernels, call(): pl.pallas_call(body, name=name, out_shape=tuple(outs), in_specs=[spec(k)...  68.2 us
    ppermute x34, waiting for transfers between devices, swap(): return lax.ppermute(array, 'dp', [(i, i ^ bits) for i in range(n_dp)])  59 us
    ppermute x34, starting transfers between devices, swap(): return lax.ppermute(array, 'dp', [(i, i ^ bits) for i in range(n_dp)])  31.3 us
    ppermute x15, starting transfers between devices, rotate(): lax.ppermute(array, 'mp', [(i, (i + step) % n_mp) for i in range(n_mp)])  13.6 us
  transfers between devices with their start and end apart: 49, of which 27 were waited for; matrix products, arithmetic and copies ran while one was open for 4% of the time, Pallas kernels for 21%

profile of v2, /device:TPU:9, one launch (start us, length us, event | category | flops | bytes accessed | tf_op | source)
XLA Modules:
  0.0 263.6 jit_solution(8140647079566920734)
XLA Ops:
  8.3 7.4 %collective-permute-done.1.bias_2 = bf16[104,768]{1,0:T(8,128)(2,1)S(1)} collective-permute-done((bf16[104,768]{1,0:T(8,128)(2,1)}, bf16[104,768]{1,0:T(8,128)(2,1)S(1)}, u32[]{:S(2)}, u32[]{:S(2)}) %collective-permute-start.1) | collective-permute-done | bytes 159776 | tf_op jit(solution)/shard_map/ppermute | solution.py:477
  15.7 3.6 %collective-permute-done.bias_1 = bf16[104,768]{1,0:T(8,128)(2,1)S(1)} collective-permute-done((bf16[104,768]{1,0:T(8,128)(2,1)}, bf16[104,768]{1,0:T(8,128)(2,1)S(1)}, u32[]{:S(2)}, u32[]{:S(2)}) %collective-permute-start) | collective-permute-done | bytes 159776 | tf_op jit(solution)/shard_map/ppermute | solution.py:477
  24.1 5.7 %collective-permute-done.4 = bf16[3,96,768]{2,1,0:T(8,128)(2,1)S(1)} collective-permute-done((bf16[3,96,768]{2,1,0:T(8,128)(2,1)S(1)}, bf16[3,96,768]{2,1,0:T(8,128)(2,1)S(1)}, u32[]{:S(2)}, u32[]{:S(2)}) %collective-permute-start.4) | collective-permute-done | bytes 442400 | tf_op jit(solution)/shard_map/ppermute | solution.py:480
  30.8 9.4 %collective-permute-done.5 = bf16[3,96,768]{2,1,0:T(8,128)(2,1)S(1)} collective-permute-done((bf16[3,96,768]{2,1,0:T(8,128)(2,1)S(1)}, bf16[3,96,768]{2,1,0:T(8,128)(2,1)S(1)}, u32[]{:S(2)}, u32[]{:S(2)}) %collective-permute-start.5) | collective-permute-done | bytes 442400 | tf_op jit(solution)/shard_map/ppermute | solution.py:480
  47.1 26.1 %collective-permute-done.7 = bf16[384,768]{1,0:T(8,128)(2,1)S(1)} collective-permute-done((bf16[384,768]{1,0:T(8,128)(2,1)}, bf16[384,768]{1,0:T(8,128)(2,1)S(1)}, u32[]{:S(2)}, u32[]{:S(2)}) %collective-permute-start.7) | collective-permute-done | bytes 589856 | tf_op jit(solution)/shard_map/ppermute | solution.py:477
  79.0 12.6 %att_forward.1 = (bf16[512,768]{1,0:T(8,128)(2,1)S(1)}, bf16[512,768]{1,0:T(8,128)(2,1)S(1)}, bf16[512,768]{1,0:T(8,128)(2,1)S(1)}, bf16[512,768]{1,0:T(8,128)(2...) custom-call(s32[1]{0:T(128)} %bitcast.index_ref, ...), custom_call_target="tpu_custom_call" | custom-call | bytes 243576 | tf_op jit(solution)/shard_map/att_forward/pallas_call | solution.py:60
  93.7 3.2 %collective-permute-start.12 = (bf16[4,2,192,768]{3,2,1,0:T(8,128)(2,1)S(1)}, bf16[4,2,192,768]{3,2,1,0:T(8,128)(2,1)S(1)}, u32[]{:S(2)}, u32[]{:S(2)}) collective-permute-start(bf16[4,2,192,768]{3,2,1,0:T(8,128)(2,1)S(1)} %pad_maximum_fusion.four), channel_id=1, source_target_pairs={{0,4},{4,0},{8,12},{12,8},{16,20},{20,16},{24,28},{28,24},{1,5},{5... | collective-permute-start | bytes 7077896 | tf_op jit(solution)/shard_map/ppermute | solution.py:480
  101.1 5.2 %ffn_first.1 = (bf16[512,2304]{1,0:T(8,128)(2,1)S(1)}, bf16[512,2304]{1,0:T(8,128)(2,1)S(1)}, bf16[768,512]{1,0:T(8,128)(2,1)S(1)}, f32[512,768]{1,0:T(8,128)S(1...) custom-call(s32[1]{0:T(128)} %bitcast.index_ref, f32[512,768]{1,0:T(8,128)S(1)} %get-tuple-element.125.normal, ...), custom_call_target="tpu_custom_call" | custom-call | bytes 363912 | tf_op jit(solution)/shard_map/ffn_first/pallas_call | solution.py:60
  110.4 9.2 %ffn_last.1 = (bf16[512,768]{1,0:T(8,128)(2,1)}, bf16[512,768]{1,0:T(8,128)(2,1)S(1)}, f32[512,768]{1,0:T(8,128)S(1)}, f32[8,768]{1,0:T(8,128)S(1)}, bf16[512,76...) custom-call(s32[1]{0:T(128)} %bitcast.index_ref, ...), custom_call_target="tpu_custom_call" | custom-call | bytes 310176 | tf_op jit(solution)/shard_map/ffn_last/pallas_call | solution.py:60
  122.5 12.1 %ffn_backward.1 = (f32[512,768]{1,0:T(8,128)S(1)}, bf16[512,768]{1,0:T(8,128)(2,1)S(1)}, bf16[4,4,104,768]{3,2,1,0:T(8,128)(2,1)S(1)}, bf16[4,4,104,768]{3,2,1,0:T(8,128)(2,1)S(1)}) custom-call(s32[1]{0:T(128)} %bitcast.index_ref, bf16[512,768]{1,0:T(8,128)(2,1)S(1)} %get-tuple-element.140.grad_mixed, bf16[768,512]{1,0:T(8,128)(2,1)S(1)} %get-tuple-element.141.low_t, ...), custom_call_target="tpu_custom_call" | custom-call | bytes 387512 | tf_op jit(solution)/shard_map/ffn_backward/pallas_call | solution.py:60
  135.5 4.1 %collective-permute-done.18 = bf16[4,4,104,768]{3,2,1,0:T(8,128)(2,1)S(1)} collective-permute-done((bf16[4,4,104,768]{3,2,1,0:T(8,128)(2,1)S(1)}, bf16[4,4,104,768]{3,2,1,0:T(8,128)(2,1)S(1)}, u32[]{:S(2)}, u32[]{:S(2)}) %collective-permute-start.18) | collective-permute-done | bytes 2555936 | tf_op jit(solution)/shard_map/ppermute | solution.py:480
  141.1 9.1 %att_backward.2 = (bf16[512,384]{1,0:T(8,128)(2,1)S(1)}, bf16[512,384]{1,0:T(8,128)(2,1)S(1)}, bf16[512,384]{1,0:T(8,128)(2,1)S(1)}, bf16[4,2,104,768]{3,2,1,0:T(8,128)(2,1)S(1)}, bf16[4,2,104,768]{3,2,1,0:T(8,128)(2,1)S(1)}) custom-call(s32[1]{0:T(128)} %bitcast.index_ref, bf16[512,768]{1,0:T(8,128)(2,1)S(1)} %get-tuple-element.154.queries, ...), custom_call_target="tpu_custom_call" | custom-call | bytes 150592 | tf_op jit(solution)/shard_map/att_backward/pallas_call | solution.py:60
  150.7 9.5 %att_backward.3 = (bf16[512,384]{1,0:T(8,128)(2,1)S(1)}, bf16[512,384]{1,0:T(8,128)(2,1)S(1)}, bf16[512,384]{1,0:T(8,128)(2,1)S(1)}, bf16[4,2,104,768]{3,2,1,0:T(8,128)(2,1)S(1)}, bf16[4,2,104,768]{3,2,1,0:T(8,128)(2,1)S(1)}) custom-call(s32[1]{0:T(128)} %bitcast.index_ref, bf16[512,768]{1,0:T(8,128)(2,1)S(1)} %get-tuple-element.154.queries, ...), custom_call_target="tpu_custom_call" | custom-call | bytes 150592 | tf_op jit(solution)/shard_map/att_backward/pallas_call | solution.py:60
  162.8 6.6 %collective-permute-done.20 = bf16[2,4,104,768]{3,2,1,0:T(8,128)(2,1)S(1)} collective-permute-done((bf16[2,4,104,768]{3,2,1,0:T(8,128)(2,1)S(1)}, bf16[2,4,104,768]{3,2,1,0:T(8,128)(2,1)S(1)}, u32[]{:S(2)}, u32[]{:S(2)}) %collective-permute-start.20) | collective-permute-done | bytes 1277984 | tf_op jit(solution)/shard_map/ppermute | solution.py:480
  171.6 3.5 %input_backward.1 = bf16[512,768]{1,0:T(8,128)(2,1)} custom-call(bf16[512,384]{1,0:T(8,128)(2,1)S(1)} %get-tuple-element.169.q0, bf16[512,384]{1,0:T(8,128)(2,1)S(1)} %get-tuple-element.170.k0, bf16[512,384]{1,0:T(8,128)(2,1)S(1)} %get-tuple-element.171.v0, bf16[512,384]{1,0:T(8,128)(2,1)S(1)} %get-tuple-element.172.q1, ...), custom_call_target="tpu_custom_call" | custom-call | bytes 129024 | tf_op jit(solution)/shard_map/input_backward/pallas_call | solution.py:60
  175.4 8.6 %collective-permute-done.19 = bf16[4,96,768]{2,1,0:T(8,128)(2,1)S(1)} collective-permute-done((bf16[4,96,768]{2,1,0:T(8,128)(2,1)S(1)}, bf16[4,96,768]{2,1,0:T(8,128)(2,1)S(1)}, u32[]{:S(2)}, u32[]{:S(2)}) %collective-permute-start.19) | collective-permute-done | bytes 589856 | tf_op jit(solution)/shard_map/ppermute | solution.py:480
  191.3 3.0 %collective-permute-done.25 = bf16[96,768]{1,0:T(8,128)(2,1)S(1)} collective-permute-done((bf16[96,768]{1,0:T(8,128)(2,1)S(1)}, bf16[96,768]{1,0:T(8,128)(2,1)S(1)}, u32[]{:S(2)}, u32[]{:S(2)}) %collective-permute-start.25) | collective-permute-done | bytes 147488 | tf_op jit(solution)/shard_map/ppermute | solution.py:477
  194.3 9.2 %collective-permute-done.24 = bf16[96,768]{1,0:T(8,128)(2,1)S(1)} collective-permute-done((bf16[96,768]{1,0:T(8,128)(2,1)S(1)}, bf16[96,768]{1,0:T(8,128)(2,1)S(1)}, u32[]{:S(2)}, u32[]{:S(2)}) %collective-permute-start.24) | collective-permute-done | bytes 147488 | tf_op jit(solution)/shard_map/ppermute | solution.py:477
  207.9 3.0 %collective-permute-done.31 = bf16[104,768]{1,0:T(8,128)(2,1)S(1)} collective-permute-done((bf16[104,768]{1,0:T(8,128)(2,1)S(1)}, bf16[104,768]{1,0:T(8,128)(2,1)S(1)}, u32[]{:S(2)}, u32[]{:S(2)}) %collective-permute-start.31) | collective-permute-done | bytes 159776 | tf_op jit(solution)/shard_map/ppermute | solution.py:477
  213.2 8.8 %collective-permute-done.29 = bf16[104,768]{1,0:T(8,128)(2,1)S(1)} collective-permute-done((bf16[104,768]{1,0:T(8,128)(2,1)S(1)}, bf16[104,768]{1,0:T(8,128)(2,1)S(1)}, u32[]{:S(2)}, u32[]{:S(2)}) %collective-permute-start.29) | collective-permute-done | bytes 159776 | tf_op jit(solution)/shard_map/ppermute | solution.py:477
  228.0 2.9 %collective-permute-done.38 = bf16[96,768]{1,0:T(8,128)(2,1)S(1)} collective-permute-done((bf16[96,768]{1,0:T(8,128)(2,1)S(1)}, bf16[96,768]{1,0:T(8,128)(2,1)S(1)}, u32[]{:S(2)}, u32[]{:S(2)}) %collective-permute-start.38) | collective-permute-done | bytes 147488 | tf_op jit(solution)/shard_map/ppermute | solution.py:480
  234.4 3.3 %collective-permute-done.41 = bf16[104,768]{1,0:T(8,128)(2,1)S(1)} collective-permute-done((bf16[104,768]{1,0:T(8,128)(2,1)S(1)}, bf16[104,768]{1,0:T(8,128)(2,1)S(1)}, u32[]{:S(2)}, u32[]{:S(2)}) %collective-permute-start.41) | collective-permute-done | bytes 159776 | tf_op jit(solution)/shard_map/ppermute | solution.py:480
  237.8 8.0 %collective-permute-done.34 = bf16[104,768]{1,0:T(8,128)(2,1)S(1)} collective-permute-done((bf16[104,768]{1,0:T(8,128)(2,1)S(1)}, bf16[104,768]{1,0:T(8,128)(2,1)S(1)}, u32[]{:S(2)}, u32[]{:S(2)}) %collective-permute-start.34) | collective-permute-done | bytes 159776 | tf_op jit(solution)/shard_map/ppermute | solution.py:477
  253.9 4.0 %collective-permute-done.44 = bf16[104,768]{1,0:T(8,128)(2,1)S(1)} collective-permute-done((bf16[104,768]{1,0:T(8,128)(2,1)S(1)}, bf16[104,768]{1,0:T(8,128)(2,1)S(1)}, u32[]{:S(2)}, u32[]{:S(2)}) %collective-permute-start.44) | collective-permute-done | bytes 159776 | tf_op jit(solution)/shard_map/ppermute | solution.py:480
  (168 shorter events, 84.2 us)
Async XLA Ops:
  3.1 12.6 %collective-permute-start.1 = (bf16[104,768]{1,0:T(8,128)(2,1)}, bf16[104,768]{1,0:T(8,128)(2,1)S(1)}, u32[]{:S(2)}, u32[]{:S(2)}) collective-permute-start(bf16[104,768]{1,0:T(8,128)(2,1)} %get-tuple-element.123.bias_0), channel_id=1, source_target_pairs={{0,2},{1,3},{2,0},{3,1},{4,6},{5,7},{6,4},{7,5},{8,10},{9,11},{10,... | collective-permute-start | bytes 479240 | tf_op jit(solution)/shard_map/ppermute | solution.py:477
  5.6 13.7 %collective-permute-start = (bf16[104,768]{1,0:T(8,128)(2,1)}, bf16[104,768]{1,0:T(8,128)(2,1)S(1)}, u32[]{:S(2)}, u32[]{:S(2)}) collective-permute-start(bf16[104,768]{1,0:T(8,128)(2,1)} %get-tuple-element.123.bias_0), channel_id=1, source_target_pairs={{0,1},{1,2},{2,3},{3,0},{4,5},{5,6},{6,7},{7,4},{8,9},{9,10},{10,1... | collective-permute-start | bytes 479240 | tf_op jit(solution)/shard_map/ppermute | solution.py:477
  21.9 18.3 %collective-permute-start.5 = (bf16[3,96,768]{2,1,0:T(8,128)(2,1)S(1)}, bf16[3,96,768]{2,1,0:T(8,128)(2,1)S(1)}, u32[]{:S(2)}, u32[]{:S(2)}) collective-permute-start(bf16[3,96,768]{2,1,0:T(8,128)(2,1)S(1)} %get-tuple-element.253), channel_id=1, source_target_pairs={{0,24},{4,28},{8,16},{12,20},{16,8},{20,12},{24,0},{28,4},{1,25},{... | collective-permute-start | bytes 1327112 | tf_op jit(solution)/shard_map/ppermute | solution.py:480
  24.1 23.0 %collective-permute-start.8 = (bf16[384,768]{1,0:T(8,128)(2,1)}, bf16[384,768]{1,0:T(8,128)(2,1)S(1)}, u32[]{:S(2)}, u32[]{:S(2)}) collective-permute-start(bf16[384,768]{1,0:T(8,128)(2,1)} %pad_maximum_fusion.5), channel_id=1, source_target_pairs={{0,2},{1,3},{2,0},{3,1},{4,6},{5,7},{6,4},{7,5},{8,10},{9,11},{10,... | collective-permute-start | bytes 1769480 | tf_op jit(solution)/shard_map/ppermute | solution.py:477
  42.4 35.3 %collective-permute-start.6 = (bf16[4,3,96,768]{3,2,1,0:T(8,128)(2,1)S(1)}, bf16[4,3,96,768]{3,2,1,0:T(8,128)(2,1)}, u32[]{:S(2)}, u32[]{:S(2)}) collective-permute-start(bf16[4,3,96,768]{3,2,1,0:T(8,128)(2,1)S(1)} %pad_maximum_fusion.1.four), channel_id=1, source_target_pairs={{0,4},{4,0},{8,12},{12,8},{16,20},{20,16},{24,28},{28,24},{1,5},{5... | collective-permute-start | bytes 5308424 | tf_op jit(solution)/shard_map/ppermute | solution.py:480
  45.0 28.3 %collective-permute-start.7 = (bf16[384,768]{1,0:T(8,128)(2,1)}, bf16[384,768]{1,0:T(8,128)(2,1)S(1)}, u32[]{:S(2)}, u32[]{:S(2)}) collective-permute-start(bf16[384,768]{1,0:T(8,128)(2,1)} %pad_maximum_fusion.5), channel_id=1, source_target_pairs={{0,1},{1,2},{2,3},{3,0},{4,5},{5,6},{6,7},{7,4},{8,9},{9,10},{10,1... | collective-permute-start | bytes 1769480 | tf_op jit(solution)/shard_map/ppermute | solution.py:477
  47.1 44.5 %collective-permute-start.11 = (bf16[384,768]{1,0:T(8,128)(2,1)}, bf16[384,768]{1,0:T(8,128)(2,1)}, u32[]{:S(2)}, u32[]{:S(2)}) collective-permute-start(bf16[384,768]{1,0:T(8,128)(2,1)} %pad_maximum_fusion.5), channel_id=1, source_target_pairs={{0,3},{1,0},{2,1},{3,2},{4,7},{5,4},{6,5},{7,6},{8,11},{9,8},{10,9... | collective-permute-start | bytes 1769480 | tf_op jit(solution)/shard_map/ppermute | solution.py:477
  74.2 17.4 %collective-permute-start.9 = (bf16[2,192,768]{2,1,0:T(8,128)(2,1)}, bf16[2,192,768]{2,1,0:T(8,128)(2,1)}, u32[]{:S(2)}, u32[]{:S(2)}) collective-permute-start(bf16[2,192,768]{2,1,0:T(8,128)(2,1)} %pad_maximum_fusion.6), channel_id=1, source_target_pairs={{0,8},{4,12},{8,0},{12,4},{16,24},{20,28},{24,16},{28,20},{1,9},{5... | collective-permute-start | bytes 1769480 | tf_op jit(solution)/shard_map/ppermute | solution.py:480
  76.3 15.4 %collective-permute-start.10 = (bf16[2,192,768]{2,1,0:T(8,128)(2,1)}, bf16[2,192,768]{2,1,0:T(8,128)(2,1)}, u32[]{:S(2)}, u32[]{:S(2)}) collective-permute-start(bf16[2,192,768]{2,1,0:T(8,128)(2,1)} %pad_maximum_fusion.7), channel_id=1, source_target_pairs={{0,16},{4,20},{8,24},{12,28},{16,0},{20,4},{24,8},{28,12},{1,17},{... | collective-permute-start | bytes 1769480 | tf_op jit(solution)/shard_map/ppermute | solution.py:480
  120.8 14.1 %collective-permute-start.16 = (bf16[4,4,96,768]{3,2,1,0:T(8,128)(2,1)S(1)}, bf16[4,4,96,768]{3,2,1,0:T(8,128)(2,1)S(1)}, u32[]{:S(2)}, u32[]{:S(2)}) collective-permute-start(bf16[4,4,96,768]{3,2,1,0:T(8,128)(2,1)S(1)} %get-tuple-element.152), channel_id=1, source_target_pairs={{0,4},{4,0},{8,12},{12,8},{16,20},{20,16},{24,28},{28,24},{1,5},{5... | collective-permute-start | bytes 7077896 | tf_op jit(solution)/shard_map/ppermute | solution.py:480
  135.1 27.2 %collective-permute-start.17 = (bf16[2,4,96,768]{3,2,1,0:T(8,128)(2,1)S(1)}, bf16[2,4,96,768]{3,2,1,0:T(8,128)(2,1)S(1)}, u32[]{:S(2)}, u32[]{:S(2)}) collective-permute-start(bf16[2,4,96,768]{3,2,1,0:T(8,128)(2,1)S(1)} %add_convert_fusion.4), channel_id=1, source_target_pairs={{0,8},{4,12},{8,0},{12,4},{16,24},{20,28},{24,16},{28,20},{1,9},{5... | collective-permute-start | bytes 3538952 | tf_op jit(solution)/shard_map/ppermute | solution.py:480
  139.8 29.6 %collective-permute-start.20 = (bf16[2,4,104,768]{3,2,1,0:T(8,128)(2,1)S(1)}, bf16[2,4,104,768]{3,2,1,0:T(8,128)(2,1)S(1)}, u32[]{:S(2)}, u32[]{:S(2)}) collective-permute-start(bf16[2,4,104,768]{3,2,1,0:T(8,128)(2,1)S(1)} %add_convert_fusion.2), channel_id=1, source_target_pairs={{0,16},{4,20},{8,24},{12,28},{16,0},{20,4},{24,8},{28,12},{1,17},{... | collective-permute-start | bytes 3833864 | tf_op jit(solution)/shard_map/ppermute | solution.py:480
  150.2 24.9 %collective-permute-start.22 = (bf16[4,2,104,768]{3,2,1,0:T(8,128)(2,1)S(1)}, bf16[4,2,104,768]{3,2,1,0:T(8,128)(2,1)S(1)}, u32[]{:S(2)}, u32[]{:S(2)}) collective-permute-start(bf16[4,2,104,768]{3,2,1,0:T(8,128)(2,1)S(1)} %get-tuple-element.178), channel_id=1, source_target_pairs={{0,4},{4,0},{8,12},{12,8},{16,20},{20,16},{24,28},{28,24},{1,5},{5... | collective-permute-start | bytes 3833864 | tf_op jit(solution)/shard_map/ppermute | solution.py:480
  160.2 15.1 %collective-permute-start.23 = (bf16[4,2,104,768]{3,2,1,0:T(8,128)(2,1)S(1)}, bf16[4,2,104,768]{3,2,1,0:T(8,128)(2,1)S(1)}, u32[]{:S(2)}, u32[]{:S(2)}) collective-permute-start(bf16[4,2,104,768]{3,2,1,0:T(8,128)(2,1)S(1)} %get-tuple-element.181), channel_id=1, source_target_pairs={{0,4},{4,0},{8,12},{12,8},{16,20},{20,16},{24,28},{28,24},{1,5},{5... | collective-permute-start | bytes 3833864 | tf_op jit(solution)/shard_map/ppermute | solution.py:480
  170.0 15.0 %collective-permute-start.21 = (bf16[4,104,768]{2,1,0:T(8,128)(2,1)S(1)}, bf16[4,104,768]{2,1,0:T(8,128)(2,1)S(1)}, u32[]{:S(2)}, u32[]{:S(2)}) collective-permute-start(bf16[4,104,768]{2,1,0:T(8,128)(2,1)S(1)} %slice_bitcast_fusion.1), channel_id=1, source_target_pairs={{0,8},{4,12},{8,0},{12,4},{16,24},{20,28},{24,16},{28,20},{1,9},{5... | collective-permute-start | bytes 1916936 | tf_op jit(solution)/shard_map/ppermute | solution.py:480
  170.3 13.7 %collective-permute-start.19 = (bf16[4,96,768]{2,1,0:T(8,128)(2,1)S(1)}, bf16[4,96,768]{2,1,0:T(8,128)(2,1)S(1)}, u32[]{:S(2)}, u32[]{:S(2)}) collective-permute-start(bf16[4,96,768]{2,1,0:T(8,128)(2,1)S(1)} %slice_bitcast_fusion.3), channel_id=1, source_target_pairs={{0,16},{4,20},{8,24},{12,28},{16,0},{20,4},{24,8},{28,12},{1,17},{... | collective-permute-start | bytes 1769480 | tf_op jit(solution)/shard_map/ppermute | solution.py:480
  185.0 18.5 %collective-permute-start.27 = (bf16[2,2,104,768]{3,2,1,0:T(8,128)(2,1)S(1)}, bf16[2,2,104,768]{3,2,1,0:T(8,128)(2,1)S(1)}, u32[]{:S(2)}, u32[]{:S(2)}) collective-permute-start(bf16[2,2,104,768]{3,2,1,0:T(8,128)(2,1)S(1)} %add_convert_fusion.11), channel_id=1, source_target_pairs={{0,8},{4,12},{8,0},{12,4},{16,24},{20,28},{24,16},{28,20},{1,9},{5... | collective-permute-start | bytes 1916936 | tf_op jit(solution)/shard_map/ppermute | solution.py:480
  185.2 18.3 %collective-permute-start.28 = (bf16[2,2,104,768]{3,2,1,0:T(8,128)(2,1)S(1)}, bf16[2,2,104,768]{3,2,1,0:T(8,128)(2,1)S(1)}, u32[]{:S(2)}, u32[]{:S(2)}) collective-permute-start(bf16[2,2,104,768]{3,2,1,0:T(8,128)(2,1)S(1)} %add_convert_fusion.10), channel_id=1, source_target_pairs={{0,16},{4,20},{8,24},{12,28},{16,0},{20,4},{24,8},{28,12},{1,17},{... | collective-permute-start | bytes 1916936 | tf_op jit(solution)/shard_map/ppermute | solution.py:480
  189.8 13.7 %collective-permute-start.24 = (bf16[96,768]{1,0:T(8,128)(2,1)S(1)}, bf16[96,768]{1,0:T(8,128)(2,1)S(1)}, u32[]{:S(2)}, u32[]{:S(2)}) collective-permute-start(bf16[96,768]{1,0:T(8,128)(2,1)S(1)} %get-tuple-element.244), channel_id=1, source_target_pairs={{0,3},{1,0},{2,1},{3,2},{4,7},{5,4},{6,5},{7,6},{8,11},{9,8},{10,9... | collective-permute-start | bytes 442376 | tf_op jit(solution)/shard_map/ppermute | solution.py:477
  204.0 17.9 %collective-permute-start.33 = (bf16[2,104,768]{2,1,0:T(8,128)(2,1)S(1)}, bf16[2,104,768]{2,1,0:T(8,128)(2,1)S(1)}, u32[]{:S(2)}, u32[]{:S(2)}) collective-permute-start(bf16[2,104,768]{2,1,0:T(8,128)(2,1)S(1)} %slice_bitcast_fusion.5), channel_id=1, source_target_pairs={{0,8},{4,12},{8,0},{12,4},{16,24},{20,28},{24,16},{28,20},{1,9},{5... | collective-permute-start | bytes 958472 | tf_op jit(solution)/shard_map/ppermute | solution.py:480
  205.3 16.6 %collective-permute-start.32 = (bf16[2,104,768]{2,1,0:T(8,128)(2,1)S(1)}, bf16[2,104,768]{2,1,0:T(8,128)(2,1)S(1)}, u32[]{:S(2)}, u32[]{:S(2)}) collective-permute-start(bf16[2,104,768]{2,1,0:T(8,128)(2,1)S(1)} %slice_bitcast_fusion.6), channel_id=1, source_target_pairs={{0,16},{4,20},{8,24},{12,28},{16,0},{20,4},{24,8},{28,12},{1,17},{... | collective-permute-start | bytes 958472 | tf_op jit(solution)/shard_map/ppermute | solution.py:480
  206.5 15.5 %collective-permute-start.29 = (bf16[104,768]{1,0:T(8,128)(2,1)S(1)}, bf16[104,768]{1,0:T(8,128)(2,1)S(1)}, u32[]{:S(2)}, u32[]{:S(2)}) collective-permute-start(bf16[104,768]{1,0:T(8,128)(2,1)S(1)} %get-tuple-element.240), channel_id=1, source_target_pairs={{0,3},{1,0},{2,1},{3,2},{4,7},{5,4},{6,5},{7,6},{8,11},{9,8},{10,9... | collective-permute-start | bytes 479240 | tf_op jit(solution)/shard_map/ppermute | solution.py:477
  225.2 12.5 %collective-permute-start.41 = (bf16[104,768]{1,0:T(8,128)(2,1)S(1)}, bf16[104,768]{1,0:T(8,128)(2,1)S(1)}, u32[]{:S(2)}, u32[]{:S(2)}) collective-permute-start(bf16[104,768]{1,0:T(8,128)(2,1)S(1)} %add_convert_fusion.13), channel_id=1, source_target_pairs={{0,16},{4,20},{8,24},{12,28},{16,0},{20,4},{24,8},{28,12},{1,17},{... | collective-permute-start | bytes 479240 | tf_op jit(solution)/shard_map/ppermute | solution.py:480
  234.4 11.4 %collective-permute-start.34 = (bf16[104,768]{1,0:T(8,128)(2,1)S(1)}, bf16[104,768]{1,0:T(8,128)(2,1)S(1)}, u32[]{:S(2)}, u32[]{:S(2)}) collective-permute-start(bf16[104,768]{1,0:T(8,128)(2,1)S(1)} %get-tuple-element.256), channel_id=1, source_target_pairs={{0,3},{1,0},{2,1},{3,2},{4,7},{5,4},{6,5},{7,6},{8,11},{9,8},{10,9... | collective-permute-start | bytes 479240 | tf_op jit(solution)/shard_map/ppermute | solution.py:477
  (44 other events, 348.0 us)

commit v3 on v2

--- a/solution.py
+++ b/solution.py
@@ -16,15 +16,15 @@
 CHUNK = 64
 SCOPED = {
     "first_piece": 60,
-    "att_forward": 9,
-    "ffn_first": 7,
-    "ffn_last": 12,
-    "ffn_backward": 18,
-    "att_backward": 13,
-    "input_backward": 6,
-    "finish_down": 6,
-    "finish_up": 6,
-    "finish_att": 8,
+    "att_forward": 7,
+    "ffn_first": 5,
+    "ffn_last": 10,
+    "ffn_backward": 16,
+    "att_backward": 11,
+    "input_backward": 4,
+    "finish_down": 4,
+    "finish_up": 4,
+    "finish_att": 6,
 }
 epsilon = 1e-05
 bf16 = jnp.bfloat16
@@ -78,21 +78,34 @@
     return [x, x ^ 1, x ^ 2, x ^ 3, 4 + y, 4 + (y ^ 1), 4 + (y ^ 2), 4 + (y ^ 3)]
 
 
+def eighths(index):
+    return [index ^ s for s in range(GROUP)]
+
+
+def places_gathered(index):
+    places = places_by_axis(index)
+    return places[:4] + places[6:] + places[4:6]
+
+
 def place_slots(four, other, r, low, rows, places, dest, base, columns):
     for s in range(GROUP):
         at = pl.multiple_of(base + places[s] * rows, rows)
         dest[pl.ds(at, rows), columns] = (other if s % 2 else four)[s // 2, r, low : low + rows]
 
 
-def put_slots(index, r, rows, low, keep, send):
+def put_slots(index, r, rows, low, keep, send, by_axis=False):
     size = rows[0].shape[0]
+    x, y = index & 3, ((index >> 1) & 2) | (index & 1)
     for odd in range(2):
 
         @pl.when((index & 1) == odd)
         def _():
             for d in range(GROUP):
                 dest = send if (d ^ odd) & 1 else keep
-                dest[(index ^ d) >> 1, r, low : low + size] = rows[d]
+                spot = (index ^ d) >> 1
+                if by_axis:
+                    spot = (x ^ d) >> 1 if d < 4 else 2 + ((y ^ (d - 4)) >> 1)
+                dest[spot, r, low : low + size] = rows[d]
 
 
 def normalize(total):
@@ -261,7 +274,7 @@
     rows = four.shape[2] // 2
     quarters = four.shape[1] + 1
     biases = (bias_0, bias_1, bias_2)
-    places = places_by_axis(index_ref[0])
+    up_places, down_places = eighths(index_ref[0]), places_gathered(index_ref[0])
     normed = normal[...] * vector(gain) + vector(shift)
     low = normed.astype(bf16)
     low_t[...] = low.T
@@ -272,8 +285,8 @@
             up[:, mine] = own_up[...]
             down[mine, :] = own_down[...]
         else:
-            place_slots(four, other, r - 1, 0, rows, places, up, 0, mine)
-            place_slots(four, other, r - 1, rows, rows, places, down, r * units, slice(None))
+            place_slots(four, other, r - 1, 0, rows, up_places, up, 0, mine)
+            place_slots(four, other, r - 1, rows, rows, down_places, down, r * units, slice(None))
         at = biases[r].shape[0] - EXTRA + 1
         hidden = nn(low, up[:, mine]) + biases[r][at : at + 1, :].astype(f32)
         activated[:, mine], slope[:, mine] = gelu_parts(hidden)
@@ -290,9 +303,8 @@
     units = up.shape[1]
     rows = four.shape[2] // 2
     index = index_ref[0]
-    places = places_by_axis(index)
-    place_slots(four, other, 0, 0, rows, places, up, 0, slice(None))
-    place_slots(four, other, 0, rows, rows, places, down, 0, slice(None))
+    place_slots(four, other, 0, 0, rows, eighths(index), up, 0, slice(None))
+    place_slots(four, other, 0, rows, rows, places_gathered(index), down, 0, slice(None))
     low = (normal[...] * vector(gain) + vector(shift)).astype(bf16)
     at = bias.shape[0] - EXTRA + 1
     own[...], slope[...] = gelu_parts(nn(low, up[...]) + bias[at : at + 1, :].astype(f32))
@@ -316,7 +328,7 @@
     for r in range(quarters):
         left = own[...] if r == quarters - 1 else activated[:, r * units : (r + 1) * units]
         grad = tn(left, grad_mixed[...]).astype(bf16)
-        put_slots(index, r, grad.reshape(GROUP, -1, width), 0, keep, send)
+        put_slots(index, r, grad.reshape(GROUP, -1, width), 0, keep, send, True)
 
 
 def ffn_backward(
@@ -442,8 +454,8 @@
 
 def finish_down(index_ref, four, other, out):
     rows = four.shape[1]
-    for s in range(GROUP):
-        at = pl.multiple_of((index_ref[0] ^ s) * rows, rows)
+    for s, place in enumerate(places_by_axis(index_ref[0])):
+        at = pl.multiple_of(place * rows, rows)
         out[pl.ds(at, rows), :] = (other if s % 2 else four)[s // 2].astype(f32)
 
 
@@ -500,8 +512,9 @@
         go, stay = first_axis(bits)
         return add(keep[go], got[go]), add(keep[stay], got[stay])
 
-    def line_moves(parts):
-        return [parts[0]] + [rotate(parts[r], -r) for r in range(1, n_mp)]
+    def line_moves(parts, order):
+        found = {r: rotate(parts[i], -r) if r else parts[i] for i, r in enumerate(order)}
+        return [found[r] for r in range(n_mp)]
 
     def line_total(moved):
         moved = [array.astype(f32) for array in moved]
@@ -562,28 +575,36 @@
             ],
         )
         biases = [piece] + [rotate(piece, r) for r in range(1, n_mp)]
+        order = [r for r in range(n_mp) if r != n_mp // 2] + [n_mp // 2]
+        ffn_biases = [biases[r] for r in order]
         att_line = jnp.stack([g[:rows] for g in biases[1:]])
         by_x, by_y = within & 3, ((within >> 1) & 2) | (within & 1)
         piece = jnp.concatenate(
             [
-                slot(up_weight, by_x, rows),
                 slot(down_weight, by_x, part),
-                slot(up_weight, 4 + by_y, rows),
+                slot(up_weight, within, rows),
                 slot(down_weight, 4 + by_y, part),
             ]
         )
-        ffn_line = [rotate(piece, r) for r in range(1, n_mp)]
-
-        def plane_by_axis(line):
-            cut = line[0].shape[0] // 2
-            left = jnp.stack([g[:cut] for g in line])
-            right = jnp.stack([g[cut:] for g in line])
-            return left, swap(left, 2), right, swap(right, 4)
-
-        att_four = jnp.stack([att_line] + [swap(att_line, b) for b in (2, 4, 6)])
+        piece, att_line = tie(piece, att_line)
+        ffn_line = [rotate(piece, r) for r in order[1:]]
+
+        def plane_mixed(line):
+            up_rows = slice(part, part + rows)
+            left = jnp.stack([jnp.concatenate([g[up_rows], g[:part]]) for g in line])
+            right = jnp.stack([g[part:] for g in line])
+            corner = swap(jnp.stack([g[up_rows] for g in line]), 6)
+            return left, swap(left, 2), swap(right, 4), corner, right[:, rows:]
+
+        def slots_mixed(pieces):
+            left, from_x, from_y, corner, own = pieces
+            return jnp.stack([left, from_x, from_y, jnp.concatenate([corner, own], axis=1)])
+
+        att_four = [att_line] + [swap(att_line, b) for b in (2, 4, 6)]
+        att_four, ffn_line[:-1] = tie(att_four, ffn_line[:-1])
+        att_four = jnp.stack(att_four)
         att_other = swap(att_four, 1)
-        ffn_four = plane_by_axis(ffn_line[:-1])
-
+        ffn_four = plane_mixed(ffn_line[:-1])
         tok_low = shape((length, width), bf16)
         tok_wide = shape((length, width), f32)
         queries, keys, values, contexts, normal, inverse, weights, wo = call(
@@ -616,9 +637,9 @@
             ],
         )
         normal, ffn_four, ffn_line[-1] = tie(normal, ffn_four, ffn_line[-1])
-        ffn_four = jnp.stack(ffn_four)
+        ffn_four = slots_mixed(ffn_four)
         ffn_other = swap(ffn_four, 1)
-        last_four = plane_by_axis(ffn_line[-1:])
+        last_four = plane_mixed(ffn_line[-1:])
         inner = (n_mp - 1) * units
         hidden_low = shape((length, inner), bf16)
         activated, slope, low_t, mixed, up, down = call(
@@ -638,7 +659,7 @@
                 first_gain,
                 first_shift,
                 down_bias,
-                *biases[:-1],
+                *ffn_biases[:-1],
                 up_weight,
                 down_weight,
                 ffn_four,
@@ -647,7 +668,7 @@
             "s" + "v" * 11,
         )
         activated, last_four = tie(activated, last_four)
-        last_four = jnp.stack(last_four)
+        last_four = slots_mixed(last_four)
         last_other = swap(last_four, 1)
         pieces = shape((half, n_mp, part, width), bf16)
         (
@@ -682,7 +703,7 @@
                 first_shift,
                 second_gain,
                 second_shift,
-                biases[-1],
+                ffn_biases[-1],
                 activated,
                 mixed,
                 last_four,
@@ -716,13 +737,12 @@
             "s" + "v" * 13,
             [pltpu.VMEM((length, n_mp * units), bf16), pltpu.VMEM((length, width), f32)],
         )
-        grad_attended, got_down = tie(grad_attended, got_down)
+        grad_attended, keep_up, send_up, got_down = tie(grad_attended, keep_up, send_up, got_down)
         got_up = swap(send_up, 1)
-        leave_down, stay_down = plane_first(keep_down, got_down, 2)
-        come_down = swap(leave_down, 2)
-        leave_up, stay_up = plane_first(keep_up, got_up, 4)
-        come_up = swap(leave_up, 4)
-        grad_attended, leave_down, leave_up = tie(grad_attended, leave_down, leave_up)
+        leave_x, leave_y = add(keep_down[1], got_down[1]), add(keep_down[3], got_down[3])
+        stay_x, stay_y = add(keep_down[0], got_down[0]), add(keep_down[2], got_down[2])
+        grad_attended, leave_x, leave_y = tie(grad_attended, leave_x, leave_y)
+        come_x, come_y = swap(leave_x, 2), swap(leave_y, 4)
 
         halves = n_mp // 2
         across = halves * w
@@ -755,18 +775,32 @@
             )
 
         q0, k0, v0, keep_left, send_left = attention(0, grad_attended)
-        grad_attended, q0, send_left = tie(grad_attended, q0, send_left)
+        got_up, come_x, come_y, q0, k0, v0, keep_left, send_left = tie(
+            got_up, come_x, come_y, q0, k0, v0, keep_left, send_left
+        )
         got_left = swap(send_left, 1)
+        cut = units // 2
+        left, right = slice(0, cut), slice(cut, None)
+        leave_l = add(keep_up[1::2, ..., left], got_up[1::2, ..., left])
+        leave_r = add(keep_up[2:, ..., right], got_up[2:, ..., right])
+        stay_l = add(keep_up[0::2, ..., left], got_up[0::2, ..., left])
+        stay_r = add(keep_up[:2, ..., right], got_up[:2, ..., right])
+        parts_x, parts_y = add(stay_x, come_x), add(stay_y, come_y)
+        grad_attended, leave_l, leave_r, parts_x, parts_y, got_left = tie(
+            grad_attended, leave_l, leave_r, parts_x, parts_y, got_left
+        )
+        come_l, come_r = swap(leave_l, 2), swap(leave_r, 4)
+        line_x = line_moves(parts_x, order)
         q1, k1, v1, keep_right, send_right = attention(1, grad_attended)
-        got_left, come_down, come_up = (
-            after(array, q1) for array in (got_left, come_down, come_up)
-        )
-        q1, k1, v1, keep_right, send_right = tie(q1, k1, v1, keep_right, send_right)
+        q1, k1, v1, keep_right, send_right, come_l, come_r, line_x, parts_y = tie(
+            q1, k1, v1, keep_right, send_right, come_l, come_r, line_x, parts_y
+        )
         got_right = swap(send_right, 1)
-        down_now = add(stay_down, come_down)
-        come_down = swap(down_now[1], 4)
-        up_now = add(stay_up, come_up)
-        come_up = swap(up_now[1], 2)
+        line_y = line_moves(parts_y, order)
+        now_l, now_r = add(stay_l, come_l), add(stay_r, come_r)
+        come_l, come_r = swap(now_l[1], 4), swap(now_r[1], 2)
+        leave_left, stay_left = plane_first(keep_left, got_left, 2)
+        leave_right, stay_right = plane_first(keep_right, got_right, 4)
         (grad_tokens,) = call(
             input_backward,
             "input_backward",
@@ -774,30 +808,30 @@
             [q0, k0, v0, q1, k1, v1, grad_one, weights],
             "v" * 8,
         )
-        leave_left, stay_left = plane_first(keep_left, got_left, 2)
-        leave_right, stay_right = plane_first(keep_right, got_right, 4)
-        come_down, come_up, grad_tokens, leave_left, leave_right = tie(
-            come_down, come_up, grad_tokens, leave_left, leave_right
-        )
-        down_parts, up_parts = add(down_now[0], come_down), add(up_now[0], come_up)
-        down_line = line_moves(down_parts)
+        come_l, come_r, leave_left, leave_right, grad_tokens = tie(
+            come_l, come_r, leave_left, leave_right, grad_tokens
+        )
         come_left, come_right = swap(leave_left, 2), swap(leave_right, 4)
-        down_line, come_left, come_right, up_parts = tie(
-            down_line, come_left, come_right, up_parts
-        )
-        up_line = line_moves(up_parts)
+        up_parts = jnp.concatenate([add(now_l[0], come_l), add(now_r[0], come_r)], axis=-1)
+        up_parts, line_y = tie(up_parts, line_y)
+        up_line = line_moves(up_parts, order)
+        down_x, down_y = line_total(line_x), line_total(line_y)
+        come_left, come_right, up_line[1] = tie(come_left, come_right, up_line[1])
         left_now, right_now = add(stay_left, come_left), add(stay_right, come_right)
         come_left, come_right = swap(left_now[1], 4), swap(right_now[1], 2)
-        down_total = line_total(down_line)
-        up_line, come_left, come_right, down_total = tie(
-            up_line, come_left, come_right, down_total
+        come_x, come_y = swap(down_x, 4), swap(down_y, 2)
+        up_line[2:], come_left, come_right, come_x, come_y = tie(
+            up_line[2:], come_left, come_right, come_x, come_y
         )
         left_parts, right_parts = add(left_now[0], come_left), add(right_now[0], come_right)
         att_line = line_moves(
-            [left_parts[r] for r in range(halves)] + [right_parts[r] for r in range(halves)]
-        )
-        down_four = plane_swap(down_total)
+            [left_parts[r] for r in range(halves)] + [right_parts[r] for r in range(halves)],
+            range(n_mp),
+        )
         up_four = plane_swap(line_total(up_line))
+        down_x, down_y = add(down_x, come_x), add(down_y, come_y)
+        att_line[1], down_x, down_y = tie(att_line[1], down_x, down_y)
+        down_four = [down_x, swap(down_x, 2), down_y, swap(down_y, 4)]
         att_line, down_four, up_four = tie(att_line, down_four, up_four)
         att_four = plane_swap(line_total(att_line))
         down_four, up_four = jnp.stack(down_four), jnp.stack(up_four)

time: 267 us -> 242 us (0.906)
  the two profiles are of different devices: /device:TPU:9 before, /device:TPU:0 now
where the time goes in v3:
time: 242 us; the launch traced here: 239 us
  waiting for transfers between devices  82.8 us (34%)
  Pallas kernels  67.8 us (28%)
  starting transfers between devices  67.7 us (28%)
  other arithmetic  11.3 us (5%)
  local copies, waits for them, and re-layouts  7.93 us (3%)
    pallas_call x11, Pallas kernels, call(): pl.pallas_call(body, name=name, out_shape=tuple(outs), in_specs=[spec(k)...  67.8 us
    ppermute x18, waiting for transfers between devices, rotate(): lax.ppermute(array, 'mp', [(i, (i + step) % n_mp) for i in range(n_mp)])  48.2 us
    ppermute x39, waiting for transfers between devices, swap(): return lax.ppermute(array, 'dp', [(i, i ^ bits) for i in range(n_dp)])  34.6 us
    ppermute x18, starting transfers between devices, rotate(): lax.ppermute(array, 'mp', [(i, (i + step) % n_mp) for i in range(n_mp)])  34.3 us
    ppermute x39, starting transfers between devices, swap(): return lax.ppermute(array, 'dp', [(i, i ^ bits) for i in range(n_dp)])  33.4 us
  transfers between devices with their start and end apart: 57, of which 27 were waited for; matrix products, arithmetic and copies ran while one was open for 6% of the time, Pallas kernels for 23%

profile of v3, /device:TPU:0, one launch (start us, length us, event | category | flops | bytes accessed | tf_op | source)
XLA Modules:
  0.0 239.1 jit_solution(7853101761878607341)
XLA Ops:
  3.0 5.1 %collective-permute-start.2 = (bf16[104,768]{1,0:T(8,128)(2,1)}, bf16[104,768]{1,0:T(8,128)(2,1)S(1)}, u32[]{:S(2)}, u32[]{:S(2)}) collective-permute-start(bf16[104,768]{1,0:T(8,128)(2,1)} %get-tuple-element.159.bias_0), channel_id=1, source_target_pairs={{0,3},{1,0},{2,1},{3,2},{4,7},{5,4},{6,5},{7,6},{8,11},{9,8},{10,9... | collective-permute-start | bytes 479240 | tf_op jit(solution)/shard_map/ppermute | solution.py:489
  13.0 8.9 %collective-permute-done.1.bias_2.bias = bf16[104,768]{1,0:T(8,128)(2,1)S(1)} collective-permute-done((bf16[104,768]{1,0:T(8,128)(2,1)}, bf16[104,768]{1,0:T(8,128)(2,1)S(1)}, u32[]{:S(2)}, u32[]{:S(2)}) %collective-permute-start.1) | collective-permute-done | bytes 159776 | tf_op jit(solution)/shard_map/ppermute | solution.py:489
  27.6 6.3 %collective-permute-done.7 = bf16[288,768]{1,0:T(8,128)(2,1)S(1)} collective-permute-done((bf16[288,768]{1,0:T(8,128)(2,1)S(1)}, bf16[288,768]{1,0:T(8,128)(2,1)S(1)}, u32[]{:S(2)}, u32[]{:S(2)}) %collective-permute-start.7) | collective-permute-done | bytes 442400 | tf_op jit(solution)/shard_map/ppermute | solution.py:489
  33.9 11.2 %collective-permute-done.6 = bf16[288,768]{1,0:T(8,128)(2,1)S(1)} collective-permute-done((bf16[288,768]{1,0:T(8,128)(2,1)S(1)}, bf16[288,768]{1,0:T(8,128)(2,1)S(1)}, u32[]{:S(2)}, u32[]{:S(2)}) %collective-permute-start.6) | collective-permute-done | bytes 442400 | tf_op jit(solution)/shard_map/ppermute | solution.py:489
  58.8 12.2 %att_forward.1 = (bf16[512,768]{1,0:T(8,128)(2,1)S(1)}, bf16[512,768]{1,0:T(8,128)(2,1)S(1)}, bf16[512,768]{1,0:T(8,128)(2,1)S(1)}, bf16[512,768]{1,0:T(8,128)(2...) custom-call(s32[1]{0:T(128)} %bitcast.index_ref, ...), custom_call_target="tpu_custom_call" | custom-call | bytes 243576 | tf_op jit(solution)/shard_map/att_forward/pallas_call | solution.py:60
  71.0 2.8 %collective-permute-done.12 = bf16[288,768]{1,0:T(8,128)(2,1)} collective-permute-done((bf16[288,768]{1,0:T(8,128)(2,1)}, bf16[288,768]{1,0:T(8,128)(2,1)}, u32[]{:S(2)}, u32[]{:S(2)}) %collective-permute-start.12) | collective-permute-done | bytes 442400 | tf_op jit(solution)/shard_map/ppermute | solution.py:489
  82.6 5.2 %ffn_first.1 = (bf16[512,2304]{1,0:T(8,128)(2,1)S(1)}, bf16[512,2304]{1,0:T(8,128)(2,1)S(1)}, bf16[768,512]{1,0:T(8,128)(2,1)S(1)}, f32[512,768]{1,0:T(8,128)S(1...) custom-call(s32[1]{0:T(128)} %bitcast.index_ref, f32[512,768]{1,0:T(8,128)S(1)} %get-tuple-element.169.normal, ...), custom_call_target="tpu_custom_call" | custom-call | bytes 363912 | tf_op jit(solution)/shard_map/ffn_first/pallas_call | solution.py:60
  87.8 4.3 %collective-permute-done.16 = bf16[1,96,768]{2,1,0:T(8,128)(2,1)S(1)} collective-permute-done((bf16[1,96,768]{2,1,0:T(8,128)(2,1)S(1)}, bf16[1,96,768]{2,1,0:T(8,128)(2,1)S(1)}, u32[]{:S(2)}, u32[]{:S(2)}) %collective-permute-start.16) | collective-permute-done | bytes 147488 | tf_op jit(solution)/shard_map/ppermute | solution.py:492
  92.5 2.8 %collective-permute-done.17.other = bf16[4,1,192,768]{3,2,1,0:T(8,128)(2,1)S(1)} collective-permute-done((bf16[4,1,192,768]{3,2,1,0:T(8,128)(2,1)S(1)}, bf16[4,1,192,768]{3,2,1,0:T(8,128)(2,1)S(1)}, u32[]{:S(2)}, u32[]{:S(2)}) %collective-permute-start.17) | collective-permute-done | bytes 1179680 | tf_op jit(solution)/shard_map/ppermute | solution.py:492
  95.3 9.2 %ffn_last.1 = (bf16[512,768]{1,0:T(8,128)(2,1)}, bf16[512,768]{1,0:T(8,128)(2,1)S(1)}, f32[512,768]{1,0:T(8,128)S(1)}, f32[8,768]{1,0:T(8,128)S(1)}, bf16[512,76...) custom-call(s32[1]{0:T(128)} %bitcast.index_ref, ...), custom_call_target="tpu_custom_call" | custom-call | bytes 310176 | tf_op jit(solution)/shard_map/ffn_last/pallas_call | solution.py:60
  104.7 12.2 %ffn_backward.1 = (f32[512,768]{1,0:T(8,128)S(1)}, bf16[512,768]{1,0:T(8,128)(2,1)S(1)}, bf16[4,4,104,768]{3,2,1,0:T(8,128)(2,1)S(1)}, bf16[4,4,104,768]{3,2,1,0:T(8,128)(2,1)S(1)}) custom-call(s32[1]{0:T(128)} %bitcast.index_ref, bf16[512,768]{1,0:T(8,128)(2,1)S(1)} %get-tuple-element.185.grad_mixed, bf16[768,512]{1,0:T(8,128)(2,1)S(1)} %get-tuple-element.186.low_t, ...), custom_call_target="tpu_custom_call" | custom-call | bytes 387512 | tf_op jit(solution)/shard_map/ffn_backward/pallas_call | solution.py:60
  119.9 9.1 %att_backward.2 = (bf16[512,384]{1,0:T(8,128)(2,1)S(1)}, bf16[512,384]{1,0:T(8,128)(2,1)S(1)}, bf16[512,384]{1,0:T(8,128)(2,1)S(1)}, bf16[4,2,104,768]{3,2,1,0:T(8,128)(2,1)S(1)}, bf16[4,2,104,768]{3,2,1,0:T(8,128)(2,1)S(1)}) custom-call(s32[1]{0:T(128)} %bitcast.index_ref, bf16[512,768]{1,0:T(8,128)(2,1)S(1)} %get-tuple-element.207.queries, ...), custom_call_target="tpu_custom_call" | custom-call | bytes 150592 | tf_op jit(solution)/shard_map/att_backward/pallas_call | solution.py:60
  129.0 4.2 %collective-permute-done.20 = bf16[4,96,768]{2,1,0:T(8,128)(2,1)S(1)} collective-permute-done((bf16[4,96,768]{2,1,0:T(8,128)(2,1)S(1)}, bf16[4,96,768]{2,1,0:T(8,128)(2,1)S(1)}, u32[]{:S(2)}, u32[]{:S(2)}) %collective-permute-start.20) | collective-permute-done | bytes 589856 | tf_op jit(solution)/shard_map/ppermute | solution.py:492
  143.0 9.2 %att_backward.3 = (bf16[512,384]{1,0:T(8,128)(2,1)S(1)}, bf16[512,384]{1,0:T(8,128)(2,1)S(1)}, bf16[512,384]{1,0:T(8,128)(2,1)S(1)}, bf16[4,2,104,768]{3,2,1,0:T(8,128)(2,1)S(1)}, bf16[4,2,104,768]{3,2,1,0:T(8,128)(2,1)S(1)}) custom-call(s32[1]{0:T(128)} %bitcast.index_ref, bf16[512,768]{1,0:T(8,128)(2,1)S(1)} %get-tuple-element.207.queries, ...), custom_call_target="tpu_custom_call" | custom-call | bytes 150592 | tf_op jit(solution)/shard_map/att_backward/pallas_call | solution.py:60
  160.1 3.5 %input_backward.1 = bf16[512,768]{1,0:T(8,128)(2,1)} custom-call(bf16[512,384]{1,0:T(8,128)(2,1)S(1)} %get-tuple-element.238.q0, bf16[512,384]{1,0:T(8,128)(2,1)S(1)} %get-tuple-element.239.k0, bf16[512,384]{1,0:T(8,128)(2,1)S(1)} %get-tuple-element.240.v0, bf16[512,384]{1,0:T(8,128)(2,1)S(1)} %get-tuple-element.241.q1, ...), custom_call_target="tpu_custom_call" | custom-call | bytes 129024 | tf_op jit(solution)/shard_map/input_backward/pallas_call | solution.py:60
  168.0 3.3 %collective-permute-done.34 = bf16[96,768]{1,0:T(8,128)(2,1)S(1)} collective-permute-done((bf16[96,768]{1,0:T(8,128)(2,1)S(1)}, bf16[96,768]{1,0:T(8,128)(2,1)S(1)}, u32[]{:S(2)}, u32[]{:S(2)}) %collective-permute-start.34) | collective-permute-done | bytes 147488 | tf_op jit(solution)/shard_map/ppermute | solution.py:489
  172.0 2.7 %collective-permute-start.36 = (bf16[104,768]{1,0:T(8,128)(2,1)S(1)}, bf16[104,768]{1,0:T(8,128)(2,1)S(1)}, u32[]{:S(2)}, u32[]{:S(2)}) collective-permute-start(bf16[104,768]{1,0:T(8,128)(2,1)S(1)} %get-tuple-element.316), channel_id=1, source_target_pairs={{0,3},{1,0},{2,1},{3,2},{4,7},{5,4},{6,5},{7,6},{8,11},{9,8},{10,9... | collective-permute-start | bytes 479240 | tf_op jit(solution)/shard_map/ppermute | solution.py:489
  176.1 3.3 %collective-permute-done.36 = bf16[104,768]{1,0:T(8,128)(2,1)S(1)} collective-permute-done((bf16[104,768]{1,0:T(8,128)(2,1)S(1)}, bf16[104,768]{1,0:T(8,128)(2,1)S(1)}, u32[]{:S(2)}, u32[]{:S(2)}) %collective-permute-start.36) | collective-permute-done | bytes 159776 | tf_op jit(solution)/shard_map/ppermute | solution.py:489
  179.5 6.5 %collective-permute-start.37 = (bf16[104,768]{1,0:T(8,128)(2,1)S(1)}, bf16[104,768]{1,0:T(8,128)(2,1)S(1)}, u32[]{:S(2)}, u32[]{:S(2)}) collective-permute-start(bf16[104,768]{1,0:T(8,128)(2,1)S(1)} %get-tuple-element.318), channel_id=1, source_target_pairs={{0,2},{1,3},{2,0},{3,1},{4,6},{5,7},{6,4},{7,5},{8,10},{9,11},{10,... | collective-permute-start | bytes 479240 | tf_op jit(solution)/shard_map/ppermute | solution.py:489
  189.7 8.4 %collective-permute-done.42 = bf16[96,768]{1,0:T(8,128)(2,1)S(1)} collective-permute-done((bf16[96,768]{1,0:T(8,128)(2,1)S(1)}, bf16[96,768]{1,0:T(8,128)(2,1)S(1)}, u32[]{:S(2)}, u32[]{:S(2)}) %collective-permute-start.42) | collective-permute-done | bytes 147488 | tf_op jit(solution)/shard_map/ppermute | solution.py:492
  203.1 2.9 %collective-permute-start.43 = (bf16[104,768]{1,0:T(8,128)(2,1)S(1)}, bf16[104,768]{1,0:T(8,128)(2,1)S(1)}, u32[]{:S(2)}, u32[]{:S(2)}) collective-permute-start(bf16[104,768]{1,0:T(8,128)(2,1)S(1)} %get-tuple-element.338), channel_id=1, source_target_pairs={{0,3},{1,0},{2,1},{3,2},{4,7},{5,4},{6,5},{7,6},{8,11},{9,8},{10,9... | collective-permute-start | bytes 479240 | tf_op jit(solution)/shard_map/ppermute | solution.py:489
  206.1 4.0 %collective-permute-done.43 = bf16[104,768]{1,0:T(8,128)(2,1)S(1)} collective-permute-done((bf16[104,768]{1,0:T(8,128)(2,1)S(1)}, bf16[104,768]{1,0:T(8,128)(2,1)S(1)}, u32[]{:S(2)}, u32[]{:S(2)}) %collective-permute-start.43) | collective-permute-done | bytes 159776 | tf_op jit(solution)/shard_map/ppermute | solution.py:489
  212.5 5.5 %collective-permute-done.44 = bf16[104,768]{1,0:T(8,128)(2,1)S(1)} collective-permute-done((bf16[104,768]{1,0:T(8,128)(2,1)S(1)}, bf16[104,768]{1,0:T(8,128)(2,1)S(1)}, u32[]{:S(2)}, u32[]{:S(2)}) %collective-permute-start.44) | collective-permute-done | bytes 159776 | tf_op jit(solution)/shard_map/ppermute | solution.py:489
  218.9 4.2 %collective-permute-done.47 = bf16[96,768]{1,0:T(8,128)(2,1)S(1)} collective-permute-done((bf16[96,768]{1,0:T(8,128)(2,1)S(1)}, bf16[96,768]{1,0:T(8,128)(2,1)S(1)}, u32[]{:S(2)}, u32[]{:S(2)}) %collective-permute-start.47) | collective-permute-done | bytes 147488 | tf_op jit(solution)/shard_map/ppermute | solution.py:492
  (197 shorter events, 90.4 us)
Async XLA Ops:
  8.2 13.7 %collective-permute-start.1 = (bf16[104,768]{1,0:T(8,128)(2,1)}, bf16[104,768]{1,0:T(8,128)(2,1)S(1)}, u32[]{:S(2)}, u32[]{:S(2)}) collective-permute-start(bf16[104,768]{1,0:T(8,128)(2,1)} %get-tuple-element.159.bias_0), channel_id=1, source_target_pairs={{0,2},{1,3},{2,0},{3,1},{4,6},{5,7},{6,4},{7,5},{8,10},{9,11},{10,... | collective-permute-start | bytes 479240 | tf_op jit(solution)/shard_map/ppermute | solution.py:489
  8.2 13.8 %collective-permute-start = (bf16[104,768]{1,0:T(8,128)(2,1)}, bf16[104,768]{1,0:T(8,128)(2,1)S(1)}, u32[]{:S(2)}, u32[]{:S(2)}) collective-permute-start(bf16[104,768]{1,0:T(8,128)(2,1)} %get-tuple-element.159.bias_0), channel_id=1, source_target_pairs={{0,1},{1,2},{2,3},{3,0},{4,5},{5,6},{6,7},{7,4},{8,9},{9,10},{10,1... | collective-permute-start | bytes 479240 | tf_op jit(solution)/shard_map/ppermute | solution.py:489
  23.2 21.8 %collective-permute-start.6 = (bf16[288,768]{1,0:T(8,128)(2,1)S(1)}, bf16[288,768]{1,0:T(8,128)(2,1)S(1)}, u32[]{:S(2)}, u32[]{:S(2)}) collective-permute-start(bf16[288,768]{1,0:T(8,128)(2,1)S(1)} %pad_maximum_fusion.9), channel_id=1, source_target_pairs={{0,1},{1,2},{2,3},{3,0},{4,5},{5,6},{6,7},{7,4},{8,9},{9,10},{10,1... | collective-permute-start | bytes 1327112 | tf_op jit(solution)/shard_map/ppermute | solution.py:489
  24.1 21.0 %collective-permute-start.5 = (bf16[3,96,768]{2,1,0:T(8,128)(2,1)S(1)}, bf16[3,96,768]{2,1,0:T(8,128)(2,1)S(1)}, u32[]{:S(2)}, u32[]{:S(2)}) collective-permute-start(bf16[3,96,768]{2,1,0:T(8,128)(2,1)S(1)} %pad_maximum_fusion.10), channel_id=1, source_target_pairs={{0,24},{4,28},{8,16},{12,20},{16,8},{20,12},{24,0},{28,4},{1,25},{... | collective-permute-start | bytes 1327112 | tf_op jit(solution)/shard_map/ppermute | solution.py:492
  26.5 19.0 %collective-permute-start.4 = (bf16[3,96,768]{2,1,0:T(8,128)(2,1)S(1)}, bf16[3,96,768]{2,1,0:T(8,128)(2,1)S(1)}, u32[]{:S(2)}, u32[]{:S(2)}) collective-permute-start(bf16[3,96,768]{2,1,0:T(8,128)(2,1)S(1)} %pad_maximum_fusion.10), channel_id=1, source_target_pairs={{0,16},{4,20},{8,24},{12,28},{16,0},{20,4},{24,8},{28,12},{1,17},{... | collective-permute-start | bytes 1327112 | tf_op jit(solution)/shard_map/ppermute | solution.py:492
  27.0 18.6 %collective-permute-start.3 = (bf16[3,96,768]{2,1,0:T(8,128)(2,1)S(1)}, bf16[3,96,768]{2,1,0:T(8,128)(2,1)S(1)}, u32[]{:S(2)}, u32[]{:S(2)}) collective-permute-start(bf16[3,96,768]{2,1,0:T(8,128)(2,1)S(1)} %pad_maximum_fusion.10), channel_id=1, source_target_pairs={{0,8},{4,12},{8,0},{12,4},{16,24},{20,28},{24,16},{28,20},{1,9},{5... | collective-permute-start | bytes 1327112 | tf_op jit(solution)/shard_map/ppermute | solution.py:492
  46.9 26.9 %collective-permute-start.10 = (bf16[2,192,768]{2,1,0:T(8,128)(2,1)}, bf16[2,192,768]{2,1,0:T(8,128)(2,1)}, u32[]{:S(2)}, u32[]{:S(2)}) collective-permute-start(bf16[2,192,768]{2,1,0:T(8,128)(2,1)} %pad_maximum_fusion.3), channel_id=1, source_target_pairs={{0,16},{4,20},{8,24},{12,28},{16,0},{20,4},{24,8},{28,12},{1,17},{... | collective-permute-start | bytes 1769480 | tf_op jit(solution)/shard_map/ppermute | solution.py:492
  50.1 23.8 %collective-permute-start.9 = (bf16[2,192,768]{2,1,0:T(8,128)(2,1)}, bf16[2,192,768]{2,1,0:T(8,128)(2,1)}, u32[]{:S(2)}, u32[]{:S(2)}) collective-permute-start(bf16[2,192,768]{2,1,0:T(8,128)(2,1)} %pad_maximum_fusion.7), channel_id=1, source_target_pairs={{0,8},{4,12},{8,0},{12,4},{16,24},{20,28},{24,16},{28,20},{1,9},{5... | collective-permute-start | bytes 1769480 | tf_op jit(solution)/shard_map/ppermute | solution.py:492
  51.2 22.7 %collective-permute-start.12 = (bf16[288,768]{1,0:T(8,128)(2,1)}, bf16[288,768]{1,0:T(8,128)(2,1)}, u32[]{:S(2)}, u32[]{:S(2)}) collective-permute-start(bf16[288,768]{1,0:T(8,128)(2,1)} %copy-done.17), channel_id=1, source_target_pairs={{0,2},{1,3},{2,0},{3,1},{4,6},{5,7},{6,4},{7,5},{8,10},{9,11},{10,... | collective-permute-start | bytes 1327112 | tf_op jit(solution)/shard_map/ppermute | solution.py:489
  55.0 18.8 %collective-permute-start.11 = (bf16[2,96,768]{2,1,0:T(8,128)(2,1)}, bf16[2,96,768]{2,1,0:T(8,128)(2,1)}, u32[]{:S(2)}, u32[]{:S(2)}) collective-permute-start(bf16[2,96,768]{2,1,0:T(8,128)(2,1)} %pad_maximum_fusion.11), channel_id=1, source_target_pairs={{0,24},{4,28},{8,16},{12,20},{16,8},{20,12},{24,0},{28,4},{1,25},{... | collective-permute-start | bytes 884744 | tf_op jit(solution)/shard_map/ppermute | solution.py:492
  117.0 17.0 %collective-permute-start.19 = (bf16[4,4,104,768]{3,2,1,0:T(8,128)(2,1)S(1)}, bf16[4,4,104,768]{3,2,1,0:T(8,128)(2,1)S(1)}, u32[]{:S(2)}, u32[]{:S(2)}) collective-permute-start(bf16[4,4,104,768]{3,2,1,0:T(8,128)(2,1)S(1)} %get-tuple-element.201), channel_id=1, source_target_pairs={{0,4},{4,0},{8,12},{12,8},{16,20},{20,16},{24,28},{28,24},{1,5},{5... | collective-permute-start | bytes 7667720 | tf_op jit(solution)/shard_map/ppermute | solution.py:492
  117.8 15.4 %collective-permute-start.20 = (bf16[4,96,768]{2,1,0:T(8,128)(2,1)S(1)}, bf16[4,96,768]{2,1,0:T(8,128)(2,1)S(1)}, u32[]{:S(2)}, u32[]{:S(2)}) collective-permute-start(bf16[4,96,768]{2,1,0:T(8,128)(2,1)S(1)} %get-tuple-element.205), channel_id=1, source_target_pairs={{0,8},{4,12},{8,0},{12,4},{16,24},{20,28},{24,16},{28,20},{1,9},{5... | collective-permute-start | bytes 1769480 | tf_op jit(solution)/shard_map/ppermute | solution.py:492
  118.9 15.1 %collective-permute-start.21 = (bf16[4,96,768]{2,1,0:T(8,128)(2,1)S(1)}, bf16[4,96,768]{2,1,0:T(8,128)(2,1)S(1)}, u32[]{:S(2)}, u32[]{:S(2)}) collective-permute-start(bf16[4,96,768]{2,1,0:T(8,128)(2,1)S(1)} %get-tuple-element.206), channel_id=1, source_target_pairs={{0,16},{4,20},{8,24},{12,28},{16,0},{20,4},{24,8},{28,12},{1,17},{... | collective-permute-start | bytes 1769480 | tf_op jit(solution)/shard_map/ppermute | solution.py:492
  136.9 16.4 %collective-permute-start.23 = (bf16[2,4,104,384]{3,2,1,0:T(8,128)(2,1)S(1)}, bf16[2,4,104,384]{3,2,1,0:T(8,128)(2,1)S(1)}, u32[]{:S(2)}, u32[]{:S(2)}) collective-permute-start(bf16[2,4,104,384]{3,2,1,0:T(8,128)(2,1)S(1)} %get-tuple-element.228), channel_id=1, source_target_pairs={{0,8},{4,12},{8,0},{12,4},{16,24},{20,28},{24,16},{28,20},{1,9},{5... | collective-permute-start | bytes 1916936 | tf_op jit(solution)/shard_map/ppermute | solution.py:492
  137.9 16.1 %collective-permute-start.24 = (bf16[2,4,104,384]{3,2,1,0:T(8,128)(2,1)S(1)}, bf16[2,4,104,384]{3,2,1,0:T(8,128)(2,1)S(1)}, u32[]{:S(2)}, u32[]{:S(2)}) collective-permute-start(bf16[2,4,104,384]{3,2,1,0:T(8,128)(2,1)S(1)} %get-tuple-element.229), channel_id=1, source_target_pairs={{0,16},{4,20},{8,24},{12,28},{16,0},{20,4},{24,8},{28,12},{1,17},{... | collective-permute-start | bytes 1916936 | tf_op jit(solution)/shard_map/ppermute | solution.py:492
  139.0 13.5 %collective-permute-start.26 = (bf16[96,768]{1,0:T(8,128)(2,1)S(1)}, bf16[96,768]{1,0:T(8,128)(2,1)S(1)}, u32[]{:S(2)}, u32[]{:S(2)}) collective-permute-start(bf16[96,768]{1,0:T(8,128)(2,1)S(1)} %get-tuple-element.324), channel_id=1, source_target_pairs={{0,2},{1,3},{2,0},{3,1},{4,6},{5,7},{6,4},{7,5},{8,10},{9,11},{10,... | collective-permute-start | bytes 442376 | tf_op jit(solution)/shard_map/ppermute | solution.py:489
  165.5 20.5 %collective-permute-start.31 = (bf16[2,2,104,768]{3,2,1,0:T(8,128)(2,1)S(1)}, bf16[2,2,104,768]{3,2,1,0:T(8,128)(2,1)S(1)}, u32[]{:S(2)}, u32[]{:S(2)}) collective-permute-start(bf16[2,2,104,768]{3,2,1,0:T(8,128)(2,1)S(1)} %add_convert_fusion.5), channel_id=1, source_target_pairs={{0,8},{4,12},{8,0},{12,4},{16,24},{20,28},{24,16},{28,20},{1,9},{5... | collective-permute-start | bytes 1916936 | tf_op jit(solution)/shard_map/ppermute | solution.py:492
  166.9 19.1 %collective-permute-start.32 = (bf16[2,2,104,768]{3,2,1,0:T(8,128)(2,1)S(1)}, bf16[2,2,104,768]{3,2,1,0:T(8,128)(2,1)S(1)}, u32[]{:S(2)}, u32[]{:S(2)}) collective-permute-start(bf16[2,2,104,768]{3,2,1,0:T(8,128)(2,1)S(1)} %add_convert_fusion.4), channel_id=1, source_target_pairs={{0,16},{4,20},{8,24},{12,28},{16,0},{20,4},{24,8},{28,12},{1,17},{... | collective-permute-start | bytes 1916936 | tf_op jit(solution)/shard_map/ppermute | solution.py:492
  174.8 13.7 %collective-permute-start.41 = (bf16[96,768]{1,0:T(8,128)(2,1)S(1)}, bf16[96,768]{1,0:T(8,128)(2,1)S(1)}, u32[]{:S(2)}, u32[]{:S(2)}) collective-permute-start(bf16[96,768]{1,0:T(8,128)(2,1)S(1)} %add_convert_fusion.20), channel_id=1, source_target_pairs={{0,16},{4,20},{8,24},{12,28},{16,0},{20,4},{24,8},{28,12},{1,17},{... | collective-permute-start | bytes 442376 | tf_op jit(solution)/shard_map/ppermute | solution.py:492
  175.7 22.5 %collective-permute-start.38 = (bf16[104,768]{1,0:T(8,128)(2,1)S(1)}, bf16[104,768]{1,0:T(8,128)(2,1)S(1)}, u32[]{:S(2)}, u32[]{:S(2)}) collective-permute-start(bf16[104,768]{1,0:T(8,128)(2,1)S(1)} %get-tuple-element.317), channel_id=1, source_target_pairs={{0,1},{1,2},{2,3},{3,0},{4,5},{5,6},{6,7},{7,4},{8,9},{9,10},{10,1... | collective-permute-start | bytes 479240 | tf_op jit(solution)/shard_map/ppermute | solution.py:489
  179.5 18.7 %collective-permute-start.37 = (bf16[104,768]{1,0:T(8,128)(2,1)S(1)}, bf16[104,768]{1,0:T(8,128)(2,1)S(1)}, u32[]{:S(2)}, u32[]{:S(2)}) collective-permute-start(bf16[104,768]{1,0:T(8,128)(2,1)S(1)} %get-tuple-element.318), channel_id=1, source_target_pairs={{0,2},{1,3},{2,0},{3,1},{4,6},{5,7},{6,4},{7,5},{8,10},{9,11},{10,... | collective-permute-start | bytes 479240 | tf_op jit(solution)/shard_map/ppermute | solution.py:489
  198.3 20.6 %collective-permute-start.50 = (bf16[104,768]{1,0:T(8,128)(2,1)S(1)}, bf16[104,768]{1,0:T(8,128)(2,1)S(1)}, u32[]{:S(2)}, u32[]{:S(2)}) collective-permute-start(bf16[104,768]{1,0:T(8,128)(2,1)S(1)} %fusion.11), channel_id=1, source_target_pairs={{0,24},{4,28},{8,16},{12,20},{16,8},{20,12},{24,0},{28,4},{1,25},{... | collective-permute-start | bytes 479240 | tf_op jit(solution)/shard_map/ppermute | solution.py:492
  199.6 19.2 %collective-permute-start.49 = (bf16[104,768]{1,0:T(8,128)(2,1)S(1)}, bf16[104,768]{1,0:T(8,128)(2,1)S(1)}, u32[]{:S(2)}, u32[]{:S(2)}) collective-permute-start(bf16[104,768]{1,0:T(8,128)(2,1)S(1)} %fusion.11), channel_id=1, source_target_pairs={{0,16},{4,20},{8,24},{12,28},{16,0},{20,4},{24,8},{28,12},{1,17},{... | collective-permute-start | bytes 479240 | tf_op jit(solution)/shard_map/ppermute | solution.py:492
  200.7 18.2 %collective-permute-start.48 = (bf16[104,768]{1,0:T(8,128)(2,1)S(1)}, bf16[104,768]{1,0:T(8,128)(2,1)S(1)}, u32[]{:S(2)}, u32[]{:S(2)}) collective-permute-start(bf16[104,768]{1,0:T(8,128)(2,1)S(1)} %fusion.11), channel_id=1, source_target_pairs={{0,8},{4,12},{8,0},{12,4},{16,24},{20,28},{24,16},{28,20},{1,9},{5... | collective-permute-start | bytes 479240 | tf_op jit(solution)/shard_map/ppermute | solution.py:492
  (51 other events, 466.2 us)

commit v4 on v3

--- a/solution.py
+++ b/solution.py
@@ -19,7 +19,9 @@
     "att_forward": 7,
     "ffn_first": 5,
     "ffn_last": 10,
-    "ffn_backward": 16,
+    "ffn_slopes": 8,
+    "ffn_grads": 5,
+    "ffn_norm": 7,
     "att_backward": 11,
     "input_backward": 4,
     "finish_down": 4,
@@ -87,8 +89,9 @@
     return places[:4] + places[6:] + places[4:6]
 
 
-def place_slots(four, other, r, low, rows, places, dest, base, columns):
+def place_slots(four, other, r, down_rows, rows, places, dest, base, columns):
     for s in range(GROUP):
+        low = rows if (s < GROUP // 2) != down_rows else 0
         at = pl.multiple_of(base + places[s] * rows, rows)
         dest[pl.ds(at, rows), columns] = (other if s % 2 else four)[s // 2, r, low : low + rows]
 
@@ -285,8 +288,8 @@
             up[:, mine] = own_up[...]
             down[mine, :] = own_down[...]
         else:
-            place_slots(four, other, r - 1, 0, rows, up_places, up, 0, mine)
-            place_slots(four, other, r - 1, rows, rows, down_places, down, r * units, slice(None))
+            place_slots(four, other, r - 1, False, rows, up_places, up, 0, mine)
+            place_slots(four, other, r - 1, True, rows, down_places, down, r * units, slice(None))
         at = biases[r].shape[0] - EXTRA + 1
         hidden = nn(low, up[:, mine]) + biases[r][at : at + 1, :].astype(f32)
         activated[:, mine], slope[:, mine] = gelu_parts(hidden)
@@ -303,8 +306,8 @@
     units = up.shape[1]
     rows = four.shape[2] // 2
     index = index_ref[0]
-    place_slots(four, other, 0, 0, rows, eighths(index), up, 0, slice(None))
-    place_slots(four, other, 0, rows, rows, places_gathered(index), down, 0, slice(None))
+    place_slots(four, other, 0, False, rows, eighths(index), up, 0, slice(None))
+    place_slots(four, other, 0, True, rows, places_gathered(index), down, 0, slice(None))
     low = (normal[...] * vector(gain) + vector(shift)).astype(bf16)
     at = bias.shape[0] - EXTRA + 1
     own[...], slope[...] = gelu_parts(nn(low, up[...]) + bias[at : at + 1, :].astype(f32))
@@ -331,27 +334,32 @@
         put_slots(index, r, grad.reshape(GROUP, -1, width), 0, keep, send, True)
 
 
-def ffn_backward(
-    index_ref, grad_mixed, low_t, slope, slope_last, grad_two, normal, inverse, gain_ref, sums_two,
-    up, up_last, down, down_last,
-    grad_one, grad_attended, keep, send,
-    hidden, total,
-):
-    length, width = grad_mixed.shape
+def ffn_slopes(grad_mixed, slope, slope_last, down, down_last, hidden, sums):
     units = down_last.shape[0]
-    quarters, rows = keep.shape[1], keep.shape[2] - EXTRA
-    index = index_ref[0]
-    low_sums = []
-    for r in range(quarters):
+    sums[...] = jnp.zeros_like(sums)
+    for r in range(hidden.shape[1] // units):
         mine = slice(r * units, (r + 1) * units)
-        last = r == quarters - 1
+        last = mine.stop == hidden.shape[1]
         weight = down_last[...] if last else down[mine, :]
         factor = slope_last[...] if last else slope[:, mine]
         low = (nt(grad_mixed[...], weight) * factor.astype(f32)).astype(bf16)
         hidden[:, mine] = low
-        low_sums.append(column_sum(low.astype(f32)))
-        grad = nn(low_t[...], low).astype(bf16)
-        put_slots(index, r, grad.reshape(GROUP, rows, units), 0, keep, send)
+        sums[r : r + 1, :] = column_sum(low.astype(f32))
+
+
+def ffn_grads(index_ref, hidden, low_t, keep, send):
+    units = keep.shape[3]
+    for r in range(keep.shape[1]):
+        grad = nn(low_t[...], hidden[:, r * units : (r + 1) * units]).astype(bf16)
+        put_slots(index_ref[0], r, grad.reshape(GROUP, -1, units), 0, keep, send)
+
+
+def ffn_norm(
+    hidden, grad_two, normal, inverse, gain_ref, up, up_last,
+    grad_one, grad_attended, sums,
+    total,
+):
+    length, width = normal.shape
     inner = up.shape[1]
     total[...] = nt(hidden[:, :inner], up[...]) + grad_two[...]
     total[...] += nt(hidden[:, inner:], up_last[...])
@@ -366,17 +374,14 @@
         grad_attended[at, :] = low
         return low.astype(f32), grad_normed * n, grad_normed
 
-    shared = list(by_rows(length, norm, 3, width))
-    shared += [sums_two[i : i + 1, :] for i in range(3)] + [jnp.zeros_like(gain)]
-    for r in range(quarters):
-        extra = [
-            jnp.broadcast_to(total, (EXTRA, units)).astype(bf16) for total in [low_sums[r]] + shared
-        ]
-        put_slots(index, r, jnp.stack(extra), rows, keep, send)
+    sums[...] = jnp.zeros_like(sums)
+    for i, found in enumerate(by_rows(length, norm, 3, width)):
+        sums[i : i + 1, :] = found
 
 
 def att_backward(
-    part, index_ref, queries, keys, values, contexts, grad_attended, tokens, wo, seg_row, seg_col,
+    part, places, index_ref, queries, keys, values, contexts, grad_attended, tokens, wo,
+    seg_row, seg_col, unit_sums, sums_one, sums_two,
     grad_queries, grad_keys, grad_values, keep, send,
     grad_contexts, bias, probs_t, scores_t,
 ):
@@ -386,10 +391,10 @@
     across = quarters * w
     index = index_ref[0]
     scale = HEAD_DIM**-0.5
-    low = part * across
     fill_bias(bias, seg_row, seg_col, length)
     clear_outside(probs_t, length)
     clear_outside(scores_t, length)
+    low = part * across
     grad_contexts[...] = nt(grad_attended[...], wo[low : low + across, :]).astype(bf16)
     first = lax.broadcasted_iota(jnp.int32, (PASSAGE, LANES), 1) < HEAD_DIM
     first_all = lax.broadcasted_iota(jnp.int32, (length, LANES), 1) < HEAD_DIM
@@ -437,11 +442,14 @@
     for r in range(quarters):
         put_slots(index, r, [grads[d // 2][r, d % 2] for d in range(GROUP)], 0, keep, send)
         cols = slice(r * w, (r + 1) * w)
-        line = jnp.concatenate(
+        last = jnp.concatenate(
             [query_sum[:, cols], value_sum[:, cols], jnp.zeros((1, width - 2 * w), f32)], axis=1
         )
-        line = jnp.broadcast_to(line, (EXTRA, width)).astype(bf16)
-        put_slots(index, r, [line] * GROUP, rows, keep, send)
+        at = places[part * quarters + r]
+        lines = [unit_sums[at : at + 1, :]]
+        lines += [sums[i : i + 1, :] for sums in (sums_one, sums_two) for i in range(3)]
+        lines = [jnp.broadcast_to(line, (EXTRA, width)).astype(bf16) for line in lines + [last]]
+        put_slots(index, r, lines, rows, keep, send)
 
 
 def input_backward(q0, k0, v0, q1, k1, v1, grad_one, weights, out):
@@ -452,20 +460,11 @@
     out[...] = total.astype(bf16)
 
 
-def finish_down(index_ref, four, other, out):
+def finish_ffn(places_of, index_ref, four, other, out):
     rows = four.shape[1]
-    for s, place in enumerate(places_by_axis(index_ref[0])):
+    for s, place in enumerate(places_of(index_ref[0])):
         at = pl.multiple_of(place * rows, rows)
         out[pl.ds(at, rows), :] = (other if s % 2 else four)[s // 2].astype(f32)
-
-
-def finish_up(index_ref, four, other, out, sums):
-    rows = four.shape[1] - EXTRA
-    for s in range(GROUP):
-        owner = index_ref[0] ^ s
-        slot = (other if s % 2 else four)[s // 2].astype(f32)
-        out[pl.ds(pl.multiple_of(owner * rows, rows), rows), :] = slot[:rows]
-        sums[pl.ds(pl.multiple_of(owner * EXTRA, EXTRA), EXTRA), :] = slot[rows:]
 
 
 def finish_att(index_ref, four, other, gq, gk, gv, go, sums, whole):
@@ -590,10 +589,9 @@
         ffn_line = [rotate(piece, r) for r in order[1:]]
 
         def plane_mixed(line):
-            up_rows = slice(part, part + rows)
-            left = jnp.stack([jnp.concatenate([g[up_rows], g[:part]]) for g in line])
+            left = jnp.stack([g[: part + rows] for g in line])
             right = jnp.stack([g[part:] for g in line])
-            corner = swap(jnp.stack([g[up_rows] for g in line]), 6)
+            corner = swap(jnp.stack([g[part : part + rows] for g in line]), 6)
             return left, swap(left, 2), swap(right, 4), corner, right[:, rows:]
 
         def slots_mixed(pieces):
@@ -713,44 +711,54 @@
             [pltpu.VMEM((length, units), bf16), pltpu.VMEM((length, width), f32)],
         )
         got_down = swap(send_down, 1)
-        pieces = shape((half, n_mp, rows + EXTRA, units), bf16)
-        grad_one, grad_attended, keep_up, send_up = call(
-            ffn_backward,
-            "ffn_backward",
-            [tok_wide, tok_low, pieces, pieces],
-            [
-                index,
-                grad_mixed,
-                low_t,
-                slope,
-                slope_last,
-                grad_two,
-                normal,
-                inverse,
-                first_gain,
-                sums_two,
-                up,
-                up_last,
-                down,
-                down_last,
-            ],
-            "s" + "v" * 13,
-            [pltpu.VMEM((length, n_mp * units), bf16), pltpu.VMEM((length, width), f32)],
-        )
-        grad_attended, keep_up, send_up, got_down = tie(grad_attended, keep_up, send_up, got_down)
-        got_up = swap(send_up, 1)
+        hidden, low_sums = call(
+            ffn_slopes,
+            "ffn_slopes",
+            [shape((length, n_mp * units), bf16), shape((8, units), f32)],
+            [grad_mixed, slope, slope_last, down, down_last],
+            "v" * 5,
+        )
+        hidden, got_down = tie(hidden, got_down)
         leave_x, leave_y = add(keep_down[1], got_down[1]), add(keep_down[3], got_down[3])
         stay_x, stay_y = add(keep_down[0], got_down[0]), add(keep_down[2], got_down[2])
-        grad_attended, leave_x, leave_y = tie(grad_attended, leave_x, leave_y)
+        hidden, leave_x, leave_y = tie(hidden, leave_x, leave_y)
         come_x, come_y = swap(leave_x, 2), swap(leave_y, 4)
-
+        pieces = shape((half, n_mp, rows, units), bf16)
+        keep_up, send_up = call(
+            ffn_grads, "ffn_grads", [pieces, pieces], [index, hidden, low_t], "svv"
+        )
+        hidden, keep_up, send_up = tie(hidden, keep_up, send_up)
+        got_up = swap(send_up, 1)
+        grad_one, grad_attended, sums_one = call(
+            ffn_norm,
+            "ffn_norm",
+            [tok_wide, tok_low, shape((8, width), f32)],
+            [hidden, grad_two, normal, inverse, first_gain, up, up_last],
+            "v" * 7,
+            [pltpu.VMEM((length, width), f32)],
+        )
+        grad_attended, sums_one, got_up = tie(grad_attended, sums_one, got_up)
+        cut = units // 2
+        left, right = slice(0, cut), slice(cut, None)
+
+        def plane_halves(keep, got):
+            leaves = add(keep[1::2, ..., left], got[1::2, ..., left])
+            leaves_r = add(keep[2:, ..., right], got[2:, ..., right])
+            stays = add(keep[0::2, ..., left], got[0::2, ..., left])
+            stays_r = add(keep[:2, ..., right], got[:2, ..., right])
+            return leaves, leaves_r, stays, stays_r
+
+        leave_l, leave_r, stay_l, stay_r = plane_halves(keep_up, got_up)
+        grad_attended, leave_l, leave_r = tie(grad_attended, leave_l, leave_r)
+        come_l, come_r = swap(leave_l, 2), swap(leave_r, 4)
         halves = n_mp // 2
         across = halves * w
         pieces = shape((half, halves, rows + EXTRA, width), bf16)
+        places = [order.index(r) for r in range(n_mp)]
 
         def attention(which, grad_attended):
             return call(
-                functools.partial(att_backward, which),
+                functools.partial(att_backward, which, places),
                 "att_backward",
                 [shape((length, across), bf16)] * 3 + [pieces] * 2,
                 [
@@ -764,8 +772,11 @@
                     wo,
                     seg_row,
                     seg_col,
+                    low_sums,
+                    sums_one,
+                    sums_two,
                 ],
-                "s" + "v" * 9,
+                "s" + "v" * 12,
                 [
                     pltpu.VMEM((length, across), bf16),
                     pltpu.VMEM((blocks, 3 * PASSAGE, PASSAGE), f32),
@@ -774,33 +785,47 @@
                 ],
             )
 
-        q0, k0, v0, keep_left, send_left = attention(0, grad_attended)
-        got_up, come_x, come_y, q0, k0, v0, keep_left, send_left = tie(
-            got_up, come_x, come_y, q0, k0, v0, keep_left, send_left
-        )
-        got_left = swap(send_left, 1)
-        cut = units // 2
-        left, right = slice(0, cut), slice(cut, None)
-        leave_l = add(keep_up[1::2, ..., left], got_up[1::2, ..., left])
-        leave_r = add(keep_up[2:, ..., right], got_up[2:, ..., right])
-        stay_l = add(keep_up[0::2, ..., left], got_up[0::2, ..., left])
-        stay_r = add(keep_up[:2, ..., right], got_up[:2, ..., right])
+        q0, k0, v0, keep_0, send_0 = attention(0, grad_attended)
+        come_x, come_y, q0, k0, v0, keep_0, send_0 = tie(
+            come_x, come_y, q0, k0, v0, keep_0, send_0
+        )
+        got_0 = swap(send_0, 1)
         parts_x, parts_y = add(stay_x, come_x), add(stay_y, come_y)
-        grad_attended, leave_l, leave_r, parts_x, parts_y, got_left = tie(
-            grad_attended, leave_l, leave_r, parts_x, parts_y, got_left
-        )
-        come_l, come_r = swap(leave_l, 2), swap(leave_r, 4)
+        grad_attended, parts_x, got_0 = tie(grad_attended, parts_x, got_0)
         line_x = line_moves(parts_x, order)
-        q1, k1, v1, keep_right, send_right = attention(1, grad_attended)
-        q1, k1, v1, keep_right, send_right, come_l, come_r, line_x, parts_y = tie(
-            q1, k1, v1, keep_right, send_right, come_l, come_r, line_x, parts_y
-        )
-        got_right = swap(send_right, 1)
+        q1, k1, v1, keep_1, send_1 = attention(1, grad_attended)
+        q1, k1, v1, keep_1, send_1, come_l, come_r, line_x[1:], parts_y = tie(
+            q1, k1, v1, keep_1, send_1, come_l, come_r, line_x[1:], parts_y
+        )
+        got_1 = swap(send_1, 1)
         line_y = line_moves(parts_y, order)
         now_l, now_r = add(stay_l, come_l), add(stay_r, come_r)
         come_l, come_r = swap(now_l[1], 4), swap(now_r[1], 2)
-        leave_left, stay_left = plane_first(keep_left, got_left, 2)
-        leave_right, stay_right = plane_first(keep_right, got_right, 4)
+        keep_att = jnp.concatenate([keep_0, keep_1], axis=1)
+        got_att = jnp.concatenate([got_0, got_1], axis=1)
+        leave_left, leave_right, stay_left, stay_right = plane_halves(keep_att, got_att)
+        come_l, come_r, leave_left, leave_right = tie(come_l, come_r, leave_left, leave_right)
+        come_left, come_right = swap(leave_left, 2), swap(leave_right, 4)
+        up_parts = jnp.concatenate([add(now_l[0], come_l), add(now_r[0], come_r)], axis=-1)
+        up_parts, line_y = tie(up_parts, line_y)
+        up_line = line_moves(up_parts, order)
+        down_x, down_y = line_total(line_x), line_total(line_y)
+        come_left, come_right, up_line[1:3], down_x, down_y = tie(
+            come_left, come_right, up_line[1:3], down_x, down_y
+        )
+        left_now, right_now = add(stay_left, come_left), add(stay_right, come_right)
+        come_left, come_right = swap(left_now[1], 4), swap(right_now[1], 2)
+        come_x, come_y = swap(down_x, 4), swap(down_y, 2)
+        up_line[3:], come_left, come_right, come_x, come_y = tie(
+            up_line[3:], come_left, come_right, come_x, come_y
+        )
+        att_parts = jnp.concatenate(
+            [add(left_now[0], come_left), add(right_now[0], come_right)], axis=-1
+        )
+        att_line = line_moves(att_parts, range(n_mp))
+        down_x, down_y = add(down_x, come_x), add(down_y, come_y)
+        come_x, come_y = swap(down_x, 2), swap(down_y, 4)
+        up_total = line_total(up_line)
         (grad_tokens,) = call(
             input_backward,
             "input_backward",
@@ -808,51 +833,32 @@
             [q0, k0, v0, q1, k1, v1, grad_one, weights],
             "v" * 8,
         )
-        come_l, come_r, leave_left, leave_right, grad_tokens = tie(
-            come_l, come_r, leave_left, leave_right, grad_tokens
-        )
-        come_left, come_right = swap(leave_left, 2), swap(leave_right, 4)
-        up_parts = jnp.concatenate([add(now_l[0], come_l), add(now_r[0], come_r)], axis=-1)
-        up_parts, line_y = tie(up_parts, line_y)
-        up_line = line_moves(up_parts, order)
-        down_x, down_y = line_total(line_x), line_total(line_y)
-        come_left, come_right, up_line[1] = tie(come_left, come_right, up_line[1])
-        left_now, right_now = add(stay_left, come_left), add(stay_right, come_right)
-        come_left, come_right = swap(left_now[1], 4), swap(right_now[1], 2)
-        come_x, come_y = swap(down_x, 4), swap(down_y, 2)
-        up_line[2:], come_left, come_right, come_x, come_y = tie(
-            up_line[2:], come_left, come_right, come_x, come_y
-        )
-        left_parts, right_parts = add(left_now[0], come_left), add(right_now[0], come_right)
-        att_line = line_moves(
-            [left_parts[r] for r in range(halves)] + [right_parts[r] for r in range(halves)],
-            range(n_mp),
-        )
-        up_four = plane_swap(line_total(up_line))
-        down_x, down_y = add(down_x, come_x), add(down_y, come_y)
-        att_line[1], down_x, down_y = tie(att_line[1], down_x, down_y)
-        down_four = [down_x, swap(down_x, 2), down_y, swap(down_y, 4)]
-        att_line, down_four, up_four = tie(att_line, down_four, up_four)
+        att_line[1], come_x, come_y, up_total, grad_tokens = tie(
+            att_line[1], come_x, come_y, up_total, grad_tokens
+        )
+        up_four = plane_swap(up_total)
+        down_four = [down_x, come_x, down_y, come_y]
+        att_line[2:], up_four = tie(att_line[2:], up_four)
         att_four = plane_swap(line_total(att_line))
         down_four, up_four = jnp.stack(down_four), jnp.stack(up_four)
         (grad_down,) = call(
-            finish_down,
+            functools.partial(finish_ffn, places_by_axis),
             "finish_down",
             [shape((units, width), f32)],
             [index, down_four, swap(down_four, 1)],
             "svv",
         )
-        grad_up, sums = call(
-            finish_up,
+        (grad_up,) = call(
+            functools.partial(finish_ffn, eighths),
             "finish_up",
-            [shape((width, units), f32), shape((GROUP * EXTRA, units), f32)],
+            [shape((width, units), f32)],
             [index, up_four, swap(up_four, 1)],
             "svv",
         )
-        att_four, grad_down, grad_up, sums = tie(att_four, grad_down, grad_up, sums)
+        att_four, grad_down, grad_up = tie(att_four, grad_down, grad_up)
         att_four = jnp.stack(att_four)
         att_other = swap(att_four, 1)
-        grad_query, grad_key, grad_value, grad_output, att_sums = call(
+        grad_query, grad_key, grad_value, grad_output, sums = call(
             finish_att,
             "finish_att",
             [shape((w, width), f32)] * 4 + [shape((GROUP * EXTRA, width), f32)],
@@ -864,10 +870,10 @@
             output,
             grad_tokens,
             grad_query.T,
-            att_sums[0, :w],
+            sums[(GROUP - 1) * EXTRA, :w],
             grad_key.T,
             grad_value.T,
-            att_sums[0, w : 2 * w],
+            sums[(GROUP - 1) * EXTRA, w : 2 * w],
             grad_output,
             sums[EXTRA],
             sums[2 * EXTRA],

time: 242 us -> 234 us (0.967)
  the two profiles are of different devices: /device:TPU:0 before, /device:TPU:9 now
where the time goes in v4:
time: 234 us; the launch traced here: 231 us
  waiting for transfers between devices  82.3 us (35%)
  Pallas kernels  67.3 us (29%)
  starting transfers between devices  59.9 us (26%)
  other arithmetic  10.4 us (4%)
  local copies, waits for them, and re-layouts  9.48 us (4%)
    pallas_call x13, Pallas kernels, call(): pl.pallas_call(body, name=name, out_shape=tuple(outs), in_specs=[spec(k)...  67.3 us
    ppermute x18, waiting for transfers between devices, rotate(): lax.ppermute(array, 'mp', [(i, (i + step) % n_mp) for i in range(n_mp)])  49.5 us
    ppermute x39, starting transfers between devices, swap(): return lax.ppermute(array, 'dp', [(i, i ^ bits) for i in range(n_dp)])  41.2 us
    ppermute x39, waiting for transfers between devices, swap(): return lax.ppermute(array, 'dp', [(i, i ^ bits) for i in range(n_dp)])  32.8 us
    ppermute x18, starting transfers between devices, rotate(): lax.ppermute(array, 'mp', [(i, (i + step) % n_mp) for i in range(n_mp)])  18.7 us
  transfers between devices with their start and end apart: 57, of which 22 were waited for; matrix products, arithmetic and copies ran while one was open for 5% of the time, Pallas kernels for 21%

profile of v4, /device:TPU:9, one launch (start us, length us, event | category | flops | bytes accessed | tf_op | source)
XLA Modules:
  0.0 230.9 jit_solution(16321848187801131848)
XLA Ops:
  9.8 5.9 %collective-permute-done.1.bias_2.bias = bf16[104,768]{1,0:T(8,128)(2,1)S(1)} collective-permute-done((bf16[104,768]{1,0:T(8,128)(2,1)}, bf16[104,768]{1,0:T(8,128)(2,1)S(1)}, u32[]{:S(2)}, u32[]{:S(2)}) %collective-permute-start.1) | collective-permute-done | bytes 159776 | tf_op jit(solution)/shard_map/ppermute | solution.py:488
  15.7 3.6 %collective-permute-done.bias_1 = bf16[104,768]{1,0:T(8,128)(2,1)S(1)} collective-permute-done((bf16[104,768]{1,0:T(8,128)(2,1)}, bf16[104,768]{1,0:T(8,128)(2,1)S(1)}, u32[]{:S(2)}, u32[]{:S(2)}) %collective-permute-start) | collective-permute-done | bytes 159776 | tf_op jit(solution)/shard_map/ppermute | solution.py:488
  24.2 6.5 %collective-permute-done.7 = bf16[288,768]{1,0:T(8,128)(2,1)S(1)} collective-permute-done((bf16[288,768]{1,0:T(8,128)(2,1)S(1)}, bf16[288,768]{1,0:T(8,128)(2,1)S(1)}, u32[]{:S(2)}, u32[]{:S(2)}) %collective-permute-start.7) | collective-permute-done | bytes 442400 | tf_op jit(solution)/shard_map/ppermute | solution.py:488
  30.7 8.9 %collective-permute-done.6 = bf16[288,768]{1,0:T(8,128)(2,1)} collective-permute-done((bf16[288,768]{1,0:T(8,128)(2,1)S(1)}, bf16[288,768]{1,0:T(8,128)(2,1)}, u32[]{:S(2)}, u32[]{:S(2)}) %collective-permute-start.6) | collective-permute-done | bytes 442400 | tf_op jit(solution)/shard_map/ppermute | solution.py:488
  39.6 4.5 %collective-permute-done.4 = bf16[3,96,768]{2,1,0:T(8,128)(2,1)S(1)} collective-permute-done((bf16[3,96,768]{2,1,0:T(8,128)(2,1)S(1)}, bf16[3,96,768]{2,1,0:T(8,128)(2,1)S(1)}, u32[]{:S(2)}, u32[]{:S(2)}) %collective-permute-start.4) | collective-permute-done | bytes 442400 | tf_op jit(solution)/shard_map/ppermute | solution.py:491
  56.0 12.2 %att_forward.1 = (bf16[512,768]{1,0:T(8,128)(2,1)S(1)}, bf16[512,768]{1,0:T(8,128)(2,1)S(1)}, bf16[512,768]{1,0:T(8,128)(2,1)S(1)}, bf16[512,768]{1,0:T(8,128)(2...) custom-call(s32[1]{0:T(128)} %bitcast.index_ref, ...), custom_call_target="tpu_custom_call" | custom-call | bytes 243576 | tf_op jit(solution)/shard_map/att_forward/pallas_call | solution.py:62
  80.4 5.3 %ffn_first.1 = (bf16[512,2304]{1,0:T(8,128)(2,1)S(1)}, bf16[512,2304]{1,0:T(8,128)(2,1)S(1)}, bf16[768,512]{1,0:T(8,128)(2,1)S(1)}, f32[512,768]{1,0:T(8,128)S(1...) custom-call(s32[1]{0:T(128)} %bitcast.index_ref, f32[512,768]{1,0:T(8,128)S(1)} %get-tuple-element.168.normal, ...), custom_call_target="tpu_custom_call" | custom-call | bytes 363912 | tf_op jit(solution)/shard_map/ffn_first/pallas_call | solution.py:62
  85.7 3.5 %collective-permute-done.16 = bf16[1,96,768]{2,1,0:T(8,128)(2,1)S(1)} collective-permute-done((bf16[1,96,768]{2,1,0:T(8,128)(2,1)S(1)}, bf16[1,96,768]{2,1,0:T(8,128)(2,1)S(1)}, u32[]{:S(2)}, u32[]{:S(2)}) %collective-permute-start.16) | collective-permute-done | bytes 147488 | tf_op jit(solution)/shard_map/ppermute | solution.py:491
  93.2 9.2 %ffn_last.1 = (bf16[512,768]{1,0:T(8,128)(2,1)}, bf16[512,768]{1,0:T(8,128)(2,1)S(1)}, f32[512,768]{1,0:T(8,128)S(1)}, f32[8,768]{1,0:T(8,128)S(1)}, bf16[512,76...) custom-call(s32[1]{0:T(128)} %bitcast.index_ref, ...), custom_call_target="tpu_custom_call" | custom-call | bytes 310176 | tf_op jit(solution)/shard_map/ffn_last/pallas_call | solution.py:62
  107.3 4.7 %ffn_grads.1 = (bf16[4,4,96,768]{3,2,1,0:T(8,128)(2,1)S(1)}, bf16[4,4,96,768]{3,2,1,0:T(8,128)(2,1)S(1)}) custom-call(s32[1]{0:T(128)} %bitcast.index_ref, bf16[512,3072]{1,0:T(8,128)(2,1)S(1)} %get-tuple-element.204.hidden, bf16[768,512]{1,0:T(8,128)(2,1)S(1)} %get-tuple-element.201.low_t), custom_call_target="tpu_custom_call" | custom-call | bytes 135168 | tf_op jit(solution)/shard_map/ffn_grads/pallas_call | solution.py:62
  114.1 3.8 %ffn_norm.1 = (f32[512,768]{1,0:T(8,128)S(1)}, bf16[512,768]{1,0:T(8,128)(2,1)S(1)}, f32[8,768]{1,0:T(8,128)S(1)}) custom-call(bf16[512,3072]{1,0:T(8,128)(2,1)S(1)} %get-tuple-element.204.hidden, f32[512,768]{1,0:T(8,128)S(1)} %get-tuple-element.205.grad_two, f32[512,768]{1,0:T(8,128)S(1)} %get-tuple-element.168.normal, ...), custom_call_target="tpu_custom_call" | custom-call | bytes 209336 | tf_op jit(solution)/shard_map/ffn_norm/pallas_call | solution.py:62
  118.3 9.2 %att_backward.2 = (bf16[512,384]{1,0:T(8,128)(2,1)S(1)}, bf16[512,384]{1,0:T(8,128)(2,1)S(1)}, bf16[512,384]{1,0:T(8,128)(2,1)S(1)}, bf16[4,2,104,768]{3,2,1,0:T(8,128)(2,1)S(1)}, bf16[4,2,104,768]{3,2,1,0:T(8,128)(2,1)S(1)}) custom-call(s32[1]{0:T(128)} %bitcast.index_ref, bf16[512,768]{1,0:T(8,128)(2,1)S(1)} %get-tuple-element.196.queries, ...), custom_call_target="tpu_custom_call" | custom-call | bytes 151744 | tf_op jit(solution)/shard_map/att_backward/pallas_call | solution.py:62
  132.6 3.1 %collective-permute-start.26 = (bf16[96,768]{1,0:T(8,128)(2,1)S(1)}, bf16[96,768]{1,0:T(8,128)(2,1)S(1)}, u32[]{:S(2)}, u32[]{:S(2)}) collective-permute-start(bf16[96,768]{1,0:T(8,128)(2,1)S(1)} %get-tuple-element.329), channel_id=1, source_target_pairs={{0,2},{1,3},{2,0},{3,1},{4,6},{5,7},{6,4},{7,5},{8,10},{9,11},{10,... | collective-permute-start | bytes 442376 | tf_op jit(solution)/shard_map/ppermute | solution.py:488
  135.8 9.3 %att_backward.3 = (bf16[512,384]{1,0:T(8,128)(2,1)S(1)}, bf16[512,384]{1,0:T(8,128)(2,1)S(1)}, bf16[512,384]{1,0:T(8,128)(2,1)S(1)}, bf16[4,2,104,768]{3,2,1,0:T(8,128)(2,1)S(1)}, bf16[4,2,104,768]{3,2,1,0:T(8,128)(2,1)S(1)}) custom-call(s32[1]{0:T(128)} %bitcast.index_ref, bf16[512,768]{1,0:T(8,128)(2,1)S(1)} %get-tuple-element.196.queries, ...), custom_call_target="tpu_custom_call" | custom-call | bytes 151744 | tf_op jit(solution)/shard_map/att_backward/pallas_call | solution.py:62
  153.5 4.8 %collective-permute-done.29 = bf16[4,96,384]{2,1,0:T(8,128)(2,1)S(1)} collective-permute-done((bf16[4,96,384]{2,1,0:T(8,128)(2,1)S(1)}, bf16[4,96,384]{2,1,0:T(8,128)(2,1)S(1)}, u32[]{:S(2)}, u32[]{:S(2)}) %collective-permute-start.29) | collective-permute-done | bytes 294944 | tf_op jit(solution)/shard_map/ppermute | solution.py:491
  160.2 3.6 %collective-permute-done.34 = bf16[96,768]{1,0:T(8,128)(2,1)S(1)} collective-permute-done((bf16[96,768]{1,0:T(8,128)(2,1)S(1)}, bf16[96,768]{1,0:T(8,128)(2,1)S(1)}, u32[]{:S(2)}, u32[]{:S(2)}) %collective-permute-start.34) | collective-permute-done | bytes 147488 | tf_op jit(solution)/shard_map/ppermute | solution.py:488
  167.1 9.2 %collective-permute-done.37 = bf16[96,768]{1,0:T(8,128)(2,1)S(1)} collective-permute-done((bf16[96,768]{1,0:T(8,128)(2,1)S(1)}, bf16[96,768]{1,0:T(8,128)(2,1)S(1)}, u32[]{:S(2)}, u32[]{:S(2)}) %collective-permute-start.37) | collective-permute-done | bytes 147488 | tf_op jit(solution)/shard_map/ppermute | solution.py:488
  180.0 3.5 %input_backward.1 = bf16[512,768]{1,0:T(8,128)(2,1)} custom-call(bf16[512,384]{1,0:T(8,128)(2,1)S(1)} %get-tuple-element.267.q0, bf16[512,384]{1,0:T(8,128)(2,1)S(1)} %get-tuple-element.268.k0, bf16[512,384]{1,0:T(8,128)(2,1)S(1)} %get-tuple-element.269.v0, bf16[512,384]{1,0:T(8,128)(2,1)S(1)} %get-tuple-element.270.q1, ...), custom_call_target="tpu_custom_call" | custom-call | bytes 129024 | tf_op jit(solution)/shard_map/input_backward/pallas_call | solution.py:62
  183.5 5.3 %collective-permute-done.41 = bf16[96,768]{1,0:T(8,128)(2,1)S(1)} collective-permute-done((bf16[96,768]{1,0:T(8,128)(2,1)S(1)}, bf16[96,768]{1,0:T(8,128)(2,1)S(1)}, u32[]{:S(2)}, u32[]{:S(2)}) %collective-permute-start.41) | collective-permute-done | bytes 147488 | tf_op jit(solution)/shard_map/ppermute | solution.py:491
  192.3 3.1 %collective-permute-start.46 = (bf16[104,768]{1,0:T(8,128)(2,1)S(1)}, bf16[104,768]{1,0:T(8,128)(2,1)S(1)}, u32[]{:S(2)}, u32[]{:S(2)}) collective-permute-start(bf16[104,768]{1,0:T(8,128)(2,1)S(1)} %get-tuple-element.320), channel_id=1, source_target_pairs={{0,2},{1,3},{2,0},{3,1},{4,6},{5,7},{6,4},{7,5},{8,10},{9,11},{10,... | collective-permute-start | bytes 479240 | tf_op jit(solution)/shard_map/ppermute | solution.py:488
  195.5 6.8 %collective-permute-done.43 = bf16[104,768]{1,0:T(8,128)(2,1)S(1)} collective-permute-done((bf16[104,768]{1,0:T(8,128)(2,1)S(1)}, bf16[104,768]{1,0:T(8,128)(2,1)S(1)}, u32[]{:S(2)}, u32[]{:S(2)}) %collective-permute-start.43) | collective-permute-done | bytes 159776 | tf_op jit(solution)/shard_map/ppermute | solution.py:488
  205.1 5.5 %collective-permute-start.54 = (bf16[4,96,768]{2,1,0:T(8,128)(2,1)S(1)}, bf16[4,96,768]{2,1,0:T(8,128)(2,1)S(1)}, u32[]{:S(2)}, u32[]{:S(2)}) collective-permute-start(bf16[4,96,768]{2,1,0:T(8,128)(2,1)S(1)} %pad_maximum_fusion.7.four), channel_id=1, source_target_pairs={{0,4},{4,0},{8,12},{12,8},{16,20},{20,16},{24,28},{28,24},{1,5},{5... | collective-permute-start | bytes 1769480 | tf_op jit(solution)/shard_map/ppermute | solution.py:491
  210.7 4.2 %collective-permute-start.55 = (bf16[4,96,768]{2,1,0:T(8,128)(2,1)S(1)}, bf16[4,96,768]{2,1,0:T(8,128)(2,1)S(1)}, u32[]{:S(2)}, u32[]{:S(2)}) collective-permute-start(bf16[4,96,768]{2,1,0:T(8,128)(2,1)S(1)} %pad_maximum_fusion.8.four), channel_id=1, source_target_pairs={{0,4},{4,0},{8,12},{12,8},{16,20},{20,16},{24,28},{28,24},{1,5},{5... | collective-permute-start | bytes 1769480 | tf_op jit(solution)/shard_map/ppermute | solution.py:491
  221.8 3.7 %collective-permute-done.52 = bf16[104,768]{1,0:T(8,128)(2,1)S(1)} collective-permute-done((bf16[104,768]{1,0:T(8,128)(2,1)S(1)}, bf16[104,768]{1,0:T(8,128)(2,1)S(1)}, u32[]{:S(2)}, u32[]{:S(2)}) %collective-permute-start.52) | collective-permute-done | bytes 159776 | tf_op jit(solution)/shard_map/ppermute | solution.py:491
  (197 shorter events, 89.7 us)
Async XLA Ops:
  3.1 12.6 %collective-permute-start.1 = (bf16[104,768]{1,0:T(8,128)(2,1)}, bf16[104,768]{1,0:T(8,128)(2,1)S(1)}, u32[]{:S(2)}, u32[]{:S(2)}) collective-permute-start(bf16[104,768]{1,0:T(8,128)(2,1)} %get-tuple-element.158.bias_0), channel_id=1, source_target_pairs={{0,2},{1,3},{2,0},{3,1},{4,6},{5,7},{6,4},{7,5},{8,10},{9,11},{10,... | collective-permute-start | bytes 479240 | tf_op jit(solution)/shard_map/ppermute | solution.py:488
  5.6 13.7 %collective-permute-start = (bf16[104,768]{1,0:T(8,128)(2,1)}, bf16[104,768]{1,0:T(8,128)(2,1)S(1)}, u32[]{:S(2)}, u32[]{:S(2)}) collective-permute-start(bf16[104,768]{1,0:T(8,128)(2,1)} %get-tuple-element.158.bias_0), channel_id=1, source_target_pairs={{0,1},{1,2},{2,3},{3,0},{4,5},{5,6},{6,7},{7,4},{8,9},{9,10},{10,1... | collective-permute-start | bytes 479240 | tf_op jit(solution)/shard_map/ppermute | solution.py:488
  20.5 19.1 %collective-permute-start.6 = (bf16[288,768]{1,0:T(8,128)(2,1)S(1)}, bf16[288,768]{1,0:T(8,128)(2,1)}, u32[]{:S(2)}, u32[]{:S(2)}) collective-permute-start(bf16[288,768]{1,0:T(8,128)(2,1)S(1)} %pad_maximum_fusion.9), channel_id=1, source_target_pairs={{0,1},{1,2},{2,3},{3,0},{4,5},{5,6},{6,7},{7,4},{8,9},{9,10},{10,1... | collective-permute-start | bytes 1327112 | tf_op jit(solution)/shard_map/ppermute | solution.py:488
  21.5 18.0 %collective-permute-start.5 = (bf16[3,96,768]{2,1,0:T(8,128)(2,1)S(1)}, bf16[3,96,768]{2,1,0:T(8,128)(2,1)S(1)}, u32[]{:S(2)}, u32[]{:S(2)}) collective-permute-start(bf16[3,96,768]{2,1,0:T(8,128)(2,1)S(1)} %pad_maximum_fusion.10), channel_id=1, source_target_pairs={{0,24},{4,28},{8,16},{12,20},{16,8},{20,12},{24,0},{28,4},{1,25},{... | collective-permute-start | bytes 1327112 | tf_op jit(solution)/shard_map/ppermute | solution.py:491
  23.7 20.3 %collective-permute-start.4 = (bf16[3,96,768]{2,1,0:T(8,128)(2,1)S(1)}, bf16[3,96,768]{2,1,0:T(8,128)(2,1)S(1)}, u32[]{:S(2)}, u32[]{:S(2)}) collective-permute-start(bf16[3,96,768]{2,1,0:T(8,128)(2,1)S(1)} %pad_maximum_fusion.10), channel_id=1, source_target_pairs={{0,16},{4,20},{8,24},{12,28},{16,0},{20,4},{24,8},{28,12},{1,17},{... | collective-permute-start | bytes 1327112 | tf_op jit(solution)/shard_map/ppermute | solution.py:491
  23.9 20.1 %collective-permute-start.3 = (bf16[3,96,768]{2,1,0:T(8,128)(2,1)S(1)}, bf16[3,96,768]{2,1,0:T(8,128)(2,1)S(1)}, u32[]{:S(2)}, u32[]{:S(2)}) collective-permute-start(bf16[3,96,768]{2,1,0:T(8,128)(2,1)S(1)} %pad_maximum_fusion.10), channel_id=1, source_target_pairs={{0,8},{4,12},{8,0},{12,4},{16,24},{20,28},{24,16},{28,20},{1,9},{5... | collective-permute-start | bytes 1327112 | tf_op jit(solution)/shard_map/ppermute | solution.py:491
  44.9 23.3 %collective-permute-start.12 = (bf16[288,768]{1,0:T(8,128)(2,1)}, bf16[288,768]{1,0:T(8,128)(2,1)}, u32[]{:S(2)}, u32[]{:S(2)}) collective-permute-start(bf16[288,768]{1,0:T(8,128)(2,1)} %copy-done.17), channel_id=1, source_target_pairs={{0,2},{1,3},{2,0},{3,1},{4,6},{5,7},{6,4},{7,5},{8,10},{9,11},{10,... | collective-permute-start | bytes 1327112 | tf_op jit(solution)/shard_map/ppermute | solution.py:488
  48.1 23.0 %collective-permute-start.10 = (bf16[2,192,768]{2,1,0:T(8,128)(2,1)}, bf16[2,192,768]{2,1,0:T(8,128)(2,1)}, u32[]{:S(2)}, u32[]{:S(2)}) collective-permute-start(bf16[2,192,768]{2,1,0:T(8,128)(2,1)} %pad_maximum_fusion.3), channel_id=1, source_target_pairs={{0,16},{4,20},{8,24},{12,28},{16,0},{20,4},{24,8},{28,12},{1,17},{... | collective-permute-start | bytes 1769480 | tf_op jit(solution)/shard_map/ppermute | solution.py:491
  50.2 20.9 %collective-permute-start.9 = (bf16[2,192,768]{2,1,0:T(8,128)(2,1)}, bf16[2,192,768]{2,1,0:T(8,128)(2,1)}, u32[]{:S(2)}, u32[]{:S(2)}) collective-permute-start(bf16[2,192,768]{2,1,0:T(8,128)(2,1)} %pad_maximum_fusion.5), channel_id=1, source_target_pairs={{0,8},{4,12},{8,0},{12,4},{16,24},{20,28},{24,16},{28,20},{1,9},{5... | collective-permute-start | bytes 1769480 | tf_op jit(solution)/shard_map/ppermute | solution.py:491
  52.4 18.7 %collective-permute-start.11 = (bf16[2,96,768]{2,1,0:T(8,128)(2,1)}, bf16[2,96,768]{2,1,0:T(8,128)(2,1)}, u32[]{:S(2)}, u32[]{:S(2)}) collective-permute-start(bf16[2,96,768]{2,1,0:T(8,128)(2,1)} %pad_maximum_fusion.11), channel_id=1, source_target_pairs={{0,24},{4,28},{8,16},{12,20},{16,8},{20,12},{24,0},{28,4},{1,25},{... | collective-permute-start | bytes 884744 | tf_op jit(solution)/shard_map/ppermute | solution.py:491
  76.6 12.7 %collective-permute-start.15 = (bf16[1,192,768]{2,1,0:T(8,128)(2,1)S(1)}, bf16[1,192,768]{2,1,0:T(8,128)(2,1)S(1)}, u32[]{:S(2)}, u32[]{:S(2)}) collective-permute-start(bf16[1,192,768]{2,1,0:T(8,128)(2,1)S(1)} %get-tuple-element.331), channel_id=1, source_target_pairs={{0,16},{4,20},{8,24},{12,28},{16,0},{20,4},{24,8},{28,12},{1,17},{... | collective-permute-start | bytes 884744 | tf_op jit(solution)/shard_map/ppermute | solution.py:491
  112.5 15.0 %collective-permute-start.19 = (bf16[4,96,768]{2,1,0:T(8,128)(2,1)S(1)}, bf16[4,96,768]{2,1,0:T(8,128)(2,1)S(1)}, u32[]{:S(2)}, u32[]{:S(2)}) collective-permute-start(bf16[4,96,768]{2,1,0:T(8,128)(2,1)S(1)} %get-tuple-element.194), channel_id=1, source_target_pairs={{0,8},{4,12},{8,0},{12,4},{16,24},{20,28},{24,16},{28,20},{1,9},{5... | collective-permute-start | bytes 1769480 | tf_op jit(solution)/shard_map/ppermute | solution.py:491
  113.7 14.5 %collective-permute-start.20 = (bf16[4,96,768]{2,1,0:T(8,128)(2,1)S(1)}, bf16[4,96,768]{2,1,0:T(8,128)(2,1)S(1)}, u32[]{:S(2)}, u32[]{:S(2)}) collective-permute-start(bf16[4,96,768]{2,1,0:T(8,128)(2,1)S(1)} %get-tuple-element.195), channel_id=1, source_target_pairs={{0,16},{4,20},{8,24},{12,28},{16,0},{20,4},{24,8},{28,12},{1,17},{... | collective-permute-start | bytes 1769480 | tf_op jit(solution)/shard_map/ppermute | solution.py:491
  129.4 15.8 %collective-permute-start.23 = (bf16[2,4,96,384]{3,2,1,0:T(8,128)(2,1)S(1)}, bf16[2,4,96,384]{3,2,1,0:T(8,128)(2,1)S(1)}, u32[]{:S(2)}, u32[]{:S(2)}) collective-permute-start(bf16[2,4,96,384]{3,2,1,0:T(8,128)(2,1)S(1)} %get-tuple-element.234), channel_id=1, source_target_pairs={{0,8},{4,12},{8,0},{12,4},{16,24},{20,28},{24,16},{28,20},{1,9},{5... | collective-permute-start | bytes 1769480 | tf_op jit(solution)/shard_map/ppermute | solution.py:491
  129.7 15.5 %collective-permute-start.24 = (bf16[2,4,96,384]{3,2,1,0:T(8,128)(2,1)S(1)}, bf16[2,4,96,384]{3,2,1,0:T(8,128)(2,1)S(1)}, u32[]{:S(2)}, u32[]{:S(2)}) collective-permute-start(bf16[2,4,96,384]{3,2,1,0:T(8,128)(2,1)S(1)} %get-tuple-element.235), channel_id=1, source_target_pairs={{0,16},{4,20},{8,24},{12,28},{16,0},{20,4},{24,8},{28,12},{1,17},{... | collective-permute-start | bytes 1769480 | tf_op jit(solution)/shard_map/ppermute | solution.py:491
  132.1 13.1 %collective-permute-start.27 = (bf16[96,768]{1,0:T(8,128)(2,1)S(1)}, bf16[96,768]{1,0:T(8,128)(2,1)S(1)}, u32[]{:S(2)}, u32[]{:S(2)}) collective-permute-start(bf16[96,768]{1,0:T(8,128)(2,1)S(1)} %get-tuple-element.328), channel_id=1, source_target_pairs={{0,1},{1,2},{2,3},{3,0},{4,5},{5,6},{6,7},{7,4},{8,9},{9,10},{10,1... | collective-permute-start | bytes 442376 | tf_op jit(solution)/shard_map/ppermute | solution.py:488
  132.6 12.6 %collective-permute-start.26 = (bf16[96,768]{1,0:T(8,128)(2,1)S(1)}, bf16[96,768]{1,0:T(8,128)(2,1)S(1)}, u32[]{:S(2)}, u32[]{:S(2)}) collective-permute-start(bf16[96,768]{1,0:T(8,128)(2,1)S(1)} %get-tuple-element.329), channel_id=1, source_target_pairs={{0,2},{1,3},{2,0},{3,1},{4,6},{5,7},{6,4},{7,5},{8,10},{9,11},{10,... | collective-permute-start | bytes 442376 | tf_op jit(solution)/shard_map/ppermute | solution.py:488
  151.3 12.4 %collective-permute-start.34 = (bf16[96,768]{1,0:T(8,128)(2,1)S(1)}, bf16[96,768]{1,0:T(8,128)(2,1)S(1)}, u32[]{:S(2)}, u32[]{:S(2)}) collective-permute-start(bf16[96,768]{1,0:T(8,128)(2,1)S(1)} %get-tuple-element.325), channel_id=1, source_target_pairs={{0,2},{1,3},{2,0},{3,1},{4,6},{5,7},{6,4},{7,5},{8,10},{9,11},{10,... | collective-permute-start | bytes 442376 | tf_op jit(solution)/shard_map/ppermute | solution.py:488
  152.6 13.6 %collective-permute-start.33 = (bf16[96,768]{1,0:T(8,128)(2,1)S(1)}, bf16[96,768]{1,0:T(8,128)(2,1)S(1)}, u32[]{:S(2)}, u32[]{:S(2)}) collective-permute-start(bf16[96,768]{1,0:T(8,128)(2,1)S(1)} %get-tuple-element.326), channel_id=1, source_target_pairs={{0,3},{1,0},{2,1},{3,2},{4,7},{5,4},{6,5},{7,6},{8,11},{9,8},{10,9... | collective-permute-start | bytes 442376 | tf_op jit(solution)/shard_map/ppermute | solution.py:488
  158.7 17.6 %collective-permute-start.31 = (bf16[2,4,104,384]{3,2,1,0:T(8,128)(2,1)S(1)}, bf16[2,4,104,384]{3,2,1,0:T(8,128)(2,1)S(1)}, u32[]{:S(2)}, u32[]{:S(2)}) collective-permute-start(bf16[2,4,104,384]{3,2,1,0:T(8,128)(2,1)S(1)} %get-tuple-element.243), channel_id=1, source_target_pairs={{0,8},{4,12},{8,0},{12,4},{16,24},{20,28},{24,16},{28,20},{1,9},{5... | collective-permute-start | bytes 1916936 | tf_op jit(solution)/shard_map/ppermute | solution.py:491
  159.7 16.6 %collective-permute-start.32 = (bf16[2,4,104,384]{3,2,1,0:T(8,128)(2,1)S(1)}, bf16[2,4,104,384]{3,2,1,0:T(8,128)(2,1)S(1)}, u32[]{:S(2)}, u32[]{:S(2)}) collective-permute-start(bf16[2,4,104,384]{3,2,1,0:T(8,128)(2,1)S(1)} %get-tuple-element.244), channel_id=1, source_target_pairs={{0,16},{4,20},{8,24},{12,28},{16,0},{20,4},{24,8},{28,12},{1,17},{... | collective-permute-start | bytes 1916936 | tf_op jit(solution)/shard_map/ppermute | solution.py:491
  190.8 14.3 %collective-permute-start.47 = (bf16[104,768]{1,0:T(8,128)(2,1)S(1)}, bf16[104,768]{1,0:T(8,128)(2,1)S(1)}, u32[]{:S(2)}, u32[]{:S(2)}) collective-permute-start(bf16[104,768]{1,0:T(8,128)(2,1)S(1)} %get-tuple-element.318), channel_id=1, source_target_pairs={{0,1},{1,2},{2,3},{3,0},{4,5},{5,6},{6,7},{7,4},{8,9},{9,10},{10,1... | collective-permute-start | bytes 479240 | tf_op jit(solution)/shard_map/ppermute | solution.py:488
  192.3 18.3 %collective-permute-start.46 = (bf16[104,768]{1,0:T(8,128)(2,1)S(1)}, bf16[104,768]{1,0:T(8,128)(2,1)S(1)}, u32[]{:S(2)}, u32[]{:S(2)}) collective-permute-start(bf16[104,768]{1,0:T(8,128)(2,1)S(1)} %get-tuple-element.320), channel_id=1, source_target_pairs={{0,2},{1,3},{2,0},{3,1},{4,6},{5,7},{6,4},{7,5},{8,10},{9,11},{10,... | collective-permute-start | bytes 479240 | tf_op jit(solution)/shard_map/ppermute | solution.py:488
  205.1 12.7 %collective-permute-start.54 = (bf16[4,96,768]{2,1,0:T(8,128)(2,1)S(1)}, bf16[4,96,768]{2,1,0:T(8,128)(2,1)S(1)}, u32[]{:S(2)}, u32[]{:S(2)}) collective-permute-start(bf16[4,96,768]{2,1,0:T(8,128)(2,1)S(1)} %pad_maximum_fusion.7.four), channel_id=1, source_target_pairs={{0,4},{4,0},{8,12},{12,8},{16,20},{20,16},{24,28},{28,24},{1,5},{5... | collective-permute-start | bytes 1769480 | tf_op jit(solution)/shard_map/ppermute | solution.py:491
  (51 other events, 437.3 us)

commit v5 on v4

--- a/solution.py
+++ b/solution.py
@@ -13,7 +13,7 @@
 GROUP = 8
 EXTRA = 8
 LANES = 128
-CHUNK = 64
+CHUNK = 128
 SCOPED = {
     "first_piece": 60,
     "att_forward": 7,
@@ -140,7 +140,7 @@
         return tuple(t + folded(f) for t, f in zip(totals, found))
 
     zeros = tuple(jnp.zeros((8, width), f32) for _ in range(sums))
-    totals = lax.fori_loop(0, length // CHUNK, step, zeros, unroll=2)
+    totals = lax.fori_loop(0, length // CHUNK, step, zeros, unroll=1)
     return tuple(column_sum(t) for t in totals)
 
 
@@ -234,24 +234,24 @@
     queries[...] = (low.astype(f32) * (HEAD_DIM**-0.5)).astype(bf16)
     keys[...] = nt(tokens[...], weights[1]).astype(bf16)
     values[...] = (nt(tokens[...], weights[2]) + row[1:2, :]).astype(bf16)
-    first = lax.broadcasted_iota(jnp.int32, (PASSAGE, LANES), 1) < HEAD_DIM
-    first_all = lax.broadcasted_iota(jnp.int32, (length, LANES), 1) < HEAD_DIM
-
-    def pair(i, carry):
-        at = pl.ds(pl.multiple_of(i * LANES, LANES), LANES)
-        for half, mine in enumerate((first, jnp.logical_not(first))):
-            for b in range(length // PASSAGE):
-                lo, hi = band(b, length)
-                block = slice(b * PASSAGE, (b + 1) * PASSAGE)
-                q = queries[block, at]
-                masked = jnp.where(mine, q, jnp.zeros_like(q))
-                scores = nt(keys[lo:hi, at], masked) + bias[b, : hi - lo, :]
-                probs_t[half, lo:hi, block] = softmax_columns(scores).astype(bf16)
-        found = [tn(probs_t[half], values[:, at]) for half in range(2)]
-        contexts[:, at] = jnp.where(first_all, *found).astype(bf16)
+    lane = lax.broadcasted_iota(jnp.int32, (PASSAGE, LANES), 1) // HEAD_DIM
+    lane_all = lax.broadcasted_iota(jnp.int32, (length, LANES), 1) // HEAD_DIM
+
+    def head(i, carry):
+        half = i & 1
+        at = pl.ds(pl.multiple_of((i >> 1) * LANES, LANES), LANES)
+        for b in range(length // PASSAGE):
+            lo, hi = band(b, length)
+            block = slice(b * PASSAGE, (b + 1) * PASSAGE)
+            q = queries[block, at]
+            masked = jnp.where(lane == half, q, jnp.zeros_like(q))
+            scores = nt(keys[lo:hi, at], masked) + bias[b, : hi - lo, :]
+            probs_t[0, lo:hi, block] = softmax_columns(scores).astype(bf16)
+        found = tn(probs_t[0], values[:, at]).astype(bf16)
+        contexts[:, at] = jnp.where(lane_all == half, found, contexts[:, at])
         return carry
 
-    lax.fori_loop(0, width // LANES, pair, 0)
+    lax.fori_loop(0, width // HEAD_DIM, head, 0)
     attended[...] = nn(contexts[...], wo[...]) + vector(output_bias)
 
     def norm(rows):
@@ -263,15 +263,35 @@
     by_rows(length, norm, 0, width)
 
 
-def gelu_parts(hidden):
-    cumulative = 0.5 * (1.0 + lax.erf(hidden * 0.7071067811865476))
-    density = jnp.exp(-0.5 * hidden * hidden) * 0.3989422804014327
-    return (hidden * cumulative).astype(bf16), (cumulative + hidden * density).astype(bf16)
+def gelu_rows(hidden, activated, slope, columns):
+    def step(i, carry):
+        rows = pl.ds(pl.multiple_of(i * CHUNK, CHUNK), CHUNK)
+        value = hidden[rows, :]
+        cumulative = 0.5 * (1.0 + lax.erf(value * 0.7071067811865476))
+        density = jnp.exp(-0.5 * value * value) * 0.3989422804014327
+        activated[rows, columns] = (value * cumulative).astype(bf16)
+        slope[rows, columns] = (cumulative + value * density).astype(bf16)
+        return carry
+
+    lax.fori_loop(0, hidden.shape[0] // CHUNK, step, 0)
+
+
+def each(count, body):
+    def step(r, carry):
+        body(r)
+        return carry
+
+    lax.fori_loop(0, count, step, 0)
+
+
+def columns_of(r, size):
+    return pl.ds(pl.multiple_of(r * size, LANES), size)
 
 
 def ffn_first(
     index_ref, normal, gain, shift, down_bias, bias_0, bias_1, bias_2, own_up, own_down, four, other,
     activated, slope, low_t, mixed, up, down,
+    hidden, lines, low_rows,
 ):
     units = own_up.shape[1]
     rows = four.shape[2] // 2
@@ -281,6 +301,7 @@
     normed = normal[...] * vector(gain) + vector(shift)
     low = normed.astype(bf16)
     low_t[...] = low.T
+    low_rows[...] = low
     mixed[...] = normed + vector(down_bias)
     for r in range(quarters):
         mine = slice(r * units, (r + 1) * units)
@@ -291,8 +312,14 @@
             place_slots(four, other, r - 1, False, rows, up_places, up, 0, mine)
             place_slots(four, other, r - 1, True, rows, down_places, down, r * units, slice(None))
         at = biases[r].shape[0] - EXTRA + 1
-        hidden = nn(low, up[:, mine]) + biases[r][at : at + 1, :].astype(f32)
-        activated[:, mine], slope[:, mine] = gelu_parts(hidden)
+        lines[r, :, :] = jnp.broadcast_to(biases[r][at : at + 1, :].astype(f32), lines.shape[1:])
+
+    def quarter(r):
+        mine = columns_of(r, units)
+        hidden[...] = nn(low_rows[...], up[:, mine]) + lines[r, 0:1, :]
+        gelu_rows(hidden, activated, slope, mine)
+
+    each(quarters, quarter)
     mixed[...] += nn(activated[...], down[...])
 
 
@@ -310,7 +337,8 @@
     place_slots(four, other, 0, True, rows, places_gathered(index), down, 0, slice(None))
     low = (normal[...] * vector(gain) + vector(shift)).astype(bf16)
     at = bias.shape[0] - EXTRA + 1
-    own[...], slope[...] = gelu_parts(nn(low, up[...]) + bias[at : at + 1, :].astype(f32))
+    total[...] = nn(low, up[...]) + bias[at : at + 1, :].astype(f32)
+    gelu_rows(total, own, slope, slice(None))
     total[...] = mixed[...] + nn(own[...], down[...])
     out_gain, out_shift = vector(second_gain), vector(second_shift)
 
@@ -327,31 +355,40 @@
     sums[...] = jnp.zeros_like(sums)
     for i, found in enumerate(by_rows(length, norm, 3, width)):
         sums[i : i + 1, :] = found
-    quarters = keep.shape[1]
-    for r in range(quarters):
-        left = own[...] if r == quarters - 1 else activated[:, r * units : (r + 1) * units]
+
+    def put(r, left):
         grad = tn(left, grad_mixed[...]).astype(bf16)
         put_slots(index, r, grad.reshape(GROUP, -1, width), 0, keep, send, True)
+
+    each(keep.shape[1] - 1, lambda r: put(r, activated[:, columns_of(r, units)]))
+    put(keep.shape[1] - 1, own[...])
 
 
 def ffn_slopes(grad_mixed, slope, slope_last, down, down_last, hidden, sums):
     units = down_last.shape[0]
     sums[...] = jnp.zeros_like(sums)
-    for r in range(hidden.shape[1] // units):
-        mine = slice(r * units, (r + 1) * units)
-        last = mine.stop == hidden.shape[1]
-        weight = down_last[...] if last else down[mine, :]
-        factor = slope_last[...] if last else slope[:, mine]
+
+    def quarter(r, weight, factor):
         low = (nt(grad_mixed[...], weight) * factor.astype(f32)).astype(bf16)
-        hidden[:, mine] = low
-        sums[r : r + 1, :] = column_sum(low.astype(f32))
+        hidden[:, columns_of(r, units)] = low
+        sums[pl.ds(r, 1), :] = column_sum(low.astype(f32))
+
+    def inner(r):
+        mine = columns_of(r, units)
+        quarter(r, down[mine, :], slope[:, mine])
+
+    each(down.shape[0] // units, inner)
+    quarter(down.shape[0] // units, down_last[...], slope_last[...])
 
 
 def ffn_grads(index_ref, hidden, low_t, keep, send):
     units = keep.shape[3]
-    for r in range(keep.shape[1]):
-        grad = nn(low_t[...], hidden[:, r * units : (r + 1) * units]).astype(bf16)
+
+    def quarter(r):
+        grad = nn(low_t[...], hidden[:, columns_of(r, units)]).astype(bf16)
         put_slots(index_ref[0], r, grad.reshape(GROUP, -1, units), 0, keep, send)
+
+    each(keep.shape[1], quarter)
 
 
 def ffn_norm(
@@ -396,40 +433,36 @@
     clear_outside(scores_t, length)
     low = part * across
     grad_contexts[...] = nt(grad_attended[...], wo[low : low + across, :]).astype(bf16)
-    first = lax.broadcasted_iota(jnp.int32, (PASSAGE, LANES), 1) < HEAD_DIM
-    first_all = lax.broadcasted_iota(jnp.int32, (length, LANES), 1) < HEAD_DIM
-
-    def pair(i, carry):
-        here = pl.ds(pl.multiple_of(i * LANES, LANES), LANES)
-        at = pl.ds(pl.multiple_of(low + i * LANES, LANES), LANES)
-        found = []
-        for half, mine in enumerate((first, jnp.logical_not(first))):
-            for b in range(length // PASSAGE):
-                lo, hi = band(b, length)
-                block = slice(b * PASSAGE, (b + 1) * PASSAGE)
-                q = queries[block, at]
-                g = grad_contexts[block, here]
-                zero = jnp.zeros_like(q)
-                scores = nt(keys[lo:hi, at], jnp.where(mine, q, zero)) + bias[b, : hi - lo, :]
-                probs = softmax_columns(scores)
-                grad_probs = nt(values[lo:hi, at], jnp.where(mine, g, zero))
-                inner = jnp.sum(grad_probs * probs, axis=0, keepdims=True)
-                probs_t[half, lo:hi, block] = probs.astype(bf16)
-                scores_t[half, lo:hi, block] = (probs * (grad_probs - inner)).astype(bf16)
-            found.append(
-                (
-                    tn(scores_t[half], keys[:, at]),
-                    nn(scores_t[half], queries[:, at]),
-                    nn(probs_t[half], grad_contexts[:, here]),
-                )
-            )
-        dq, dk, dv = (jnp.where(first_all, a, b) for a, b in zip(*found))
-        grad_queries[:, here] = (dq * scale).astype(bf16)
-        grad_keys[:, here] = dk.astype(bf16)
-        grad_values[:, here] = dv.astype(bf16)
+    lane = lax.broadcasted_iota(jnp.int32, (PASSAGE, LANES), 1) // HEAD_DIM
+    lane_all = lax.broadcasted_iota(jnp.int32, (length, LANES), 1) // HEAD_DIM
+
+    def head(i, carry):
+        half = i & 1
+        here = pl.ds(pl.multiple_of((i >> 1) * LANES, LANES), LANES)
+        at = pl.ds(pl.multiple_of(low + (i >> 1) * LANES, LANES), LANES)
+        mine = lane == half
+        for b in range(length // PASSAGE):
+            lo, hi = band(b, length)
+            block = slice(b * PASSAGE, (b + 1) * PASSAGE)
+            q = queries[block, at]
+            g = grad_contexts[block, here]
+            zero = jnp.zeros_like(q)
+            scores = nt(keys[lo:hi, at], jnp.where(mine, q, zero)) + bias[b, : hi - lo, :]
+            probs = softmax_columns(scores)
+            grad_probs = nt(values[lo:hi, at], jnp.where(mine, g, zero))
+            inner = jnp.sum(grad_probs * probs, axis=0, keepdims=True)
+            probs_t[0, lo:hi, block] = probs.astype(bf16)
+            scores_t[0, lo:hi, block] = (probs * (grad_probs - inner)).astype(bf16)
+        mine = lane_all == half
+        for out, found in (
+            (grad_queries, tn(scores_t[0], keys[:, at]) * scale),
+            (grad_keys, nn(scores_t[0], queries[:, at])),
+            (grad_values, nn(probs_t[0], grad_contexts[:, here])),
+        ):
+            out[:, here] = jnp.where(mine, found.astype(bf16), out[:, here])
         return carry
 
-    lax.fori_loop(0, across // LANES, pair, 0)
+    lax.fori_loop(0, across // HEAD_DIM, head, 0)
     grads = (
         lambda: tn(grad_queries[...], tokens[...]),
         lambda: tn(grad_keys[...], tokens[...]),
@@ -629,7 +662,7 @@
             "s" + "v" * 11,
             [
                 pltpu.VMEM((blocks, 3 * PASSAGE, PASSAGE), f32),
-                pltpu.VMEM((2, length, length), bf16),
+                pltpu.VMEM((1, length, length), bf16),
                 pltpu.VMEM((8, width), f32),
                 pltpu.VMEM((length, width), f32),
             ],
@@ -664,6 +697,11 @@
                 ffn_other,
             ],
             "s" + "v" * 11,
+            [
+                pltpu.VMEM((length, units), f32),
+                pltpu.VMEM((n_mp, 8, units), f32),
+                pltpu.VMEM((length, width), bf16),
+            ],
         )
         activated, last_four = tie(activated, last_four)
         last_four = slots_mixed(last_four)
@@ -780,8 +818,8 @@
                 [
                     pltpu.VMEM((length, across), bf16),
                     pltpu.VMEM((blocks, 3 * PASSAGE, PASSAGE), f32),
-                    pltpu.VMEM((2, length, length), bf16),
-                    pltpu.VMEM((2, length, length), bf16),
+                    pltpu.VMEM((1, length, length), bf16),
+                    pltpu.VMEM((1, length, length), bf16),
                 ],
             )
 

time: 234 us -> 230 us (0.983); the launches traced: 231 us -> 230 us
  waiting for transfers between devices: 82.3 us -> 77.2 us
  Pallas kernels: 67.3 us -> 71.2 us
    ppermute x39, waiting for transfers between devices: 32.8 us -> 28 us  [swap(): return lax.ppermute(array, 'dp', [(i, i ^ bits) for i in range(n_dp)])]
    pallas_call x13, Pallas kernels: 67.3 us -> 71.2 us  [call(): pl.pallas_call(body, name=name, out_shape=tuple(outs), in_specs=[spec(k)...]
  transfers between devices with their start and end apart: 57 -> 57, of which waited for: 22 -> 22; matrix products, arithmetic and copies ran while one was open for 5% -> 6% of each run, Pallas kernels for 21% -> 24%
where the time goes in v5:
time: 230 us
  waiting for transfers between devices  77.2 us (34%)
  Pallas kernels  71.2 us (31%)
  starting transfers between devices  59.9 us (26%)
  other arithmetic  10.4 us (5%)
  local copies, waits for them, and re-layouts  9.48 us (4%)
    pallas_call x13, Pallas kernels, call(): pl.pallas_call(body, name=name, out_shape=tuple(outs), in_specs=[spec(k)...  71.2 us
    ppermute x18, waiting for transfers between devices, rotate(): lax.ppermute(array, 'mp', [(i, (i + step) % n_mp) for i in range(n_mp)])  49.2 us
    ppermute x39, starting transfers between devices, swap(): return lax.ppermute(array, 'dp', [(i, i ^ bits) for i in range(n_dp)])  41.2 us
    ppermute x39, waiting for transfers between devices, swap(): return lax.ppermute(array, 'dp', [(i, i ^ bits) for i in range(n_dp)])  28 us
    ppermute x18, starting transfers between devices, rotate(): lax.ppermute(array, 'mp', [(i, (i + step) % n_mp) for i in range(n_mp)])  18.7 us
  transfers between devices with their start and end apart: 57, of which 22 were waited for; matrix products, arithmetic and copies ran while one was open for 6% of the time, Pallas kernels for 24%

profile of v5, /device:TPU:9, one launch (start us, length us, event | category | flops | bytes accessed | tf_op | source)
XLA Modules:
  0.0 229.6 jit_solution(17055343388539306933)
XLA Ops:
  9.8 5.9 %collective-permute-done.1.bias_2.bias = bf16[104,768]{1,0:T(8,128)(2,1)S(1)} collective-permute-done((bf16[104,768]{1,0:T(8,128)(2,1)}, bf16[104,768]{1,0:T(8,128)(2,1)S(1)}, u32[]{:S(2)}, u32[]{:S(2)}) %collective-permute-start.1) | collective-permute-done | bytes 159776 | tf_op jit(solution)/shard_map/ppermute | solution.py:521
  15.7 3.6 %collective-permute-done.bias_1 = bf16[104,768]{1,0:T(8,128)(2,1)S(1)} collective-permute-done((bf16[104,768]{1,0:T(8,128)(2,1)}, bf16[104,768]{1,0:T(8,128)(2,1)S(1)}, u32[]{:S(2)}, u32[]{:S(2)}) %collective-permute-start) | collective-permute-done | bytes 159776 | tf_op jit(solution)/shard_map/ppermute | solution.py:521
  24.2 6.5 %collective-permute-done.7 = bf16[288,768]{1,0:T(8,128)(2,1)S(1)} collective-permute-done((bf16[288,768]{1,0:T(8,128)(2,1)S(1)}, bf16[288,768]{1,0:T(8,128)(2,1)S(1)}, u32[]{:S(2)}, u32[]{:S(2)}) %collective-permute-start.7) | collective-permute-done | bytes 442400 | tf_op jit(solution)/shard_map/ppermute | solution.py:521
  30.7 8.9 %collective-permute-done.6 = bf16[288,768]{1,0:T(8,128)(2,1)} collective-permute-done((bf16[288,768]{1,0:T(8,128)(2,1)S(1)}, bf16[288,768]{1,0:T(8,128)(2,1)}, u32[]{:S(2)}, u32[]{:S(2)}) %collective-permute-start.6) | collective-permute-done | bytes 442400 | tf_op jit(solution)/shard_map/ppermute | solution.py:521
  39.6 4.5 %collective-permute-done.4 = bf16[3,96,768]{2,1,0:T(8,128)(2,1)S(1)} collective-permute-done((bf16[3,96,768]{2,1,0:T(8,128)(2,1)S(1)}, bf16[3,96,768]{2,1,0:T(8,128)(2,1)S(1)}, u32[]{:S(2)}, u32[]{:S(2)}) %collective-permute-start.4) | collective-permute-done | bytes 442400 | tf_op jit(solution)/shard_map/ppermute | solution.py:524
  56.0 14.2 %att_forward.1 = (bf16[512,768]{1,0:T(8,128)(2,1)S(1)}, bf16[512,768]{1,0:T(8,128)(2,1)S(1)}, bf16[512,768]{1,0:T(8,128)(2,1)S(1)}, bf16[512,768]{1,0:T(8,128)(2...) custom-call(s32[1]{0:T(128)} %bitcast.index_ref, ...), custom_call_target="tpu_custom_call" | custom-call | bytes 243576 | tf_op jit(solution)/shard_map/att_forward/pallas_call | solution.py:62
  80.4 7.3 %ffn_first.1 = (bf16[512,2304]{1,0:T(8,128)(2,1)S(1)}, bf16[512,2304]{1,0:T(8,128)(2,1)S(1)}, bf16[768,512]{1,0:T(8,128)(2,1)S(1)}, f32[512,768]{1,0:T(8,128)S(1...) custom-call(s32[1]{0:T(128)} %bitcast.index_ref, f32[512,768]{1,0:T(8,128)S(1)} %get-tuple-element.168.normal, ...), custom_call_target="tpu_custom_call" | custom-call | bytes 363912 | tf_op jit(solution)/shard_map/ffn_first/pallas_call | solution.py:62
  93.2 9.3 %ffn_last.1 = (bf16[512,768]{1,0:T(8,128)(2,1)}, bf16[512,768]{1,0:T(8,128)(2,1)S(1)}, f32[512,768]{1,0:T(8,128)S(1)}, f32[8,768]{1,0:T(8,128)S(1)}, bf16[512,76...) custom-call(s32[1]{0:T(128)} %bitcast.index_ref, ...), custom_call_target="tpu_custom_call" | custom-call | bytes 310176 | tf_op jit(solution)/shard_map/ffn_last/pallas_call | solution.py:62
  102.9 3.5 %ffn_slopes.1 = (bf16[512,3072]{1,0:T(8,128)(2,1)S(1)}, f32[8,768]{1,0:T(8,128)S(1)}) custom-call(bf16[512,768]{1,0:T(8,128)(2,1)S(1)} %get-tuple-element.184.grad_mixed, bf16[512,2304]{1,0:T(8,128)(2,1)S(1)} %get-tuple-element.185.slope, bf16[512,768]{1,0:T(8,128)(2,1)S(1)} %get-tuple-element.186.slope_last, bf16[2304,768]{1,0:T(8,128)(2,1)S(1)} %get-tuple-element.187.down, ...), custom_call_target="tpu_custom_call" | custom-call | bytes 184704 | tf_op jit(solution)/shard_map/ffn_slopes/pallas_call | solution.py:62
  107.4 3.6 %ffn_grads.1 = (bf16[4,4,96,768]{3,2,1,0:T(8,128)(2,1)S(1)}, bf16[4,4,96,768]{3,2,1,0:T(8,128)(2,1)S(1)}) custom-call(s32[1]{0:T(128)} %bitcast.index_ref, bf16[512,3072]{1,0:T(8,128)(2,1)S(1)} %get-tuple-element.204.hidden, bf16[768,512]{1,0:T(8,128)(2,1)S(1)} %get-tuple-element.201.low_t), custom_call_target="tpu_custom_call" | custom-call | bytes 135168 | tf_op jit(solution)/shard_map/ffn_grads/pallas_call | solution.py:62
  113.1 3.9 %ffn_norm.1 = (f32[512,768]{1,0:T(8,128)S(1)}, bf16[512,768]{1,0:T(8,128)(2,1)S(1)}, f32[8,768]{1,0:T(8,128)S(1)}) custom-call(bf16[512,3072]{1,0:T(8,128)(2,1)S(1)} %get-tuple-element.204.hidden, f32[512,768]{1,0:T(8,128)S(1)} %get-tuple-element.205.grad_two, f32[512,768]{1,0:T(8,128)S(1)} %get-tuple-element.168.normal, ...), custom_call_target="tpu_custom_call" | custom-call | bytes 209336 | tf_op jit(solution)/shard_map/ffn_norm/pallas_call | solution.py:62
  117.2 9.3 %att_backward.2 = (bf16[512,384]{1,0:T(8,128)(2,1)S(1)}, bf16[512,384]{1,0:T(8,128)(2,1)S(1)}, bf16[512,384]{1,0:T(8,128)(2,1)S(1)}, bf16[4,2,104,768]{3,2,1,0:T(8,128)(2,1)S(1)}, bf16[4,2,104,768]{3,2,1,0:T(8,128)(2,1)S(1)}) custom-call(s32[1]{0:T(128)} %bitcast.index_ref, bf16[512,768]{1,0:T(8,128)(2,1)S(1)} %get-tuple-element.196.queries, ...), custom_call_target="tpu_custom_call" | custom-call | bytes 151744 | tf_op jit(solution)/shard_map/att_backward/pallas_call | solution.py:62
  131.5 3.1 %collective-permute-start.26 = (bf16[96,768]{1,0:T(8,128)(2,1)S(1)}, bf16[96,768]{1,0:T(8,128)(2,1)S(1)}, u32[]{:S(2)}, u32[]{:S(2)}) collective-permute-start(bf16[96,768]{1,0:T(8,128)(2,1)S(1)} %get-tuple-element.329), channel_id=1, source_target_pairs={{0,2},{1,3},{2,0},{3,1},{4,6},{5,7},{6,4},{7,5},{8,10},{9,11},{10,... | collective-permute-start | bytes 442376 | tf_op jit(solution)/shard_map/ppermute | solution.py:521
  134.7 9.6 %att_backward.3 = (bf16[512,384]{1,0:T(8,128)(2,1)S(1)}, bf16[512,384]{1,0:T(8,128)(2,1)S(1)}, bf16[512,384]{1,0:T(8,128)(2,1)S(1)}, bf16[4,2,104,768]{3,2,1,0:T(8,128)(2,1)S(1)}, bf16[4,2,104,768]{3,2,1,0:T(8,128)(2,1)S(1)}) custom-call(s32[1]{0:T(128)} %bitcast.index_ref, bf16[512,768]{1,0:T(8,128)(2,1)S(1)} %get-tuple-element.196.queries, ...), custom_call_target="tpu_custom_call" | custom-call | bytes 151744 | tf_op jit(solution)/shard_map/att_backward/pallas_call | solution.py:62
  152.5 4.8 %collective-permute-done.29 = bf16[4,96,384]{2,1,0:T(8,128)(2,1)S(1)} collective-permute-done((bf16[4,96,384]{2,1,0:T(8,128)(2,1)S(1)}, bf16[4,96,384]{2,1,0:T(8,128)(2,1)S(1)}, u32[]{:S(2)}, u32[]{:S(2)}) %collective-permute-start.29) | collective-permute-done | bytes 294944 | tf_op jit(solution)/shard_map/ppermute | solution.py:524
  159.1 3.6 %collective-permute-done.34 = bf16[96,768]{1,0:T(8,128)(2,1)S(1)} collective-permute-done((bf16[96,768]{1,0:T(8,128)(2,1)S(1)}, bf16[96,768]{1,0:T(8,128)(2,1)S(1)}, u32[]{:S(2)}, u32[]{:S(2)}) %collective-permute-start.34) | collective-permute-done | bytes 147488 | tf_op jit(solution)/shard_map/ppermute | solution.py:521
  166.0 9.2 %collective-permute-done.37 = bf16[96,768]{1,0:T(8,128)(2,1)S(1)} collective-permute-done((bf16[96,768]{1,0:T(8,128)(2,1)S(1)}, bf16[96,768]{1,0:T(8,128)(2,1)S(1)}, u32[]{:S(2)}, u32[]{:S(2)}) %collective-permute-start.37) | collective-permute-done | bytes 147488 | tf_op jit(solution)/shard_map/ppermute | solution.py:521
  178.9 3.5 %input_backward.1 = bf16[512,768]{1,0:T(8,128)(2,1)} custom-call(bf16[512,384]{1,0:T(8,128)(2,1)S(1)} %get-tuple-element.267.q0, bf16[512,384]{1,0:T(8,128)(2,1)S(1)} %get-tuple-element.268.k0, bf16[512,384]{1,0:T(8,128)(2,1)S(1)} %get-tuple-element.269.v0, bf16[512,384]{1,0:T(8,128)(2,1)S(1)} %get-tuple-element.270.q1, ...), custom_call_target="tpu_custom_call" | custom-call | bytes 129024 | tf_op jit(solution)/shard_map/input_backward/pallas_call | solution.py:62
  182.4 5.3 %collective-permute-done.41 = bf16[96,768]{1,0:T(8,128)(2,1)S(1)} collective-permute-done((bf16[96,768]{1,0:T(8,128)(2,1)S(1)}, bf16[96,768]{1,0:T(8,128)(2,1)S(1)}, u32[]{:S(2)}, u32[]{:S(2)}) %collective-permute-start.41) | collective-permute-done | bytes 147488 | tf_op jit(solution)/shard_map/ppermute | solution.py:524
  191.3 3.1 %collective-permute-start.46 = (bf16[104,768]{1,0:T(8,128)(2,1)S(1)}, bf16[104,768]{1,0:T(8,128)(2,1)S(1)}, u32[]{:S(2)}, u32[]{:S(2)}) collective-permute-start(bf16[104,768]{1,0:T(8,128)(2,1)S(1)} %get-tuple-element.320), channel_id=1, source_target_pairs={{0,2},{1,3},{2,0},{3,1},{4,6},{5,7},{6,4},{7,5},{8,10},{9,11},{10,... | collective-permute-start | bytes 479240 | tf_op jit(solution)/shard_map/ppermute | solution.py:521
  194.5 6.8 %collective-permute-done.43 = bf16[104,768]{1,0:T(8,128)(2,1)S(1)} collective-permute-done((bf16[104,768]{1,0:T(8,128)(2,1)S(1)}, bf16[104,768]{1,0:T(8,128)(2,1)S(1)}, u32[]{:S(2)}, u32[]{:S(2)}) %collective-permute-start.43) | collective-permute-done | bytes 159776 | tf_op jit(solution)/shard_map/ppermute | solution.py:521
  204.0 5.5 %collective-permute-start.54 = (bf16[4,96,768]{2,1,0:T(8,128)(2,1)S(1)}, bf16[4,96,768]{2,1,0:T(8,128)(2,1)S(1)}, u32[]{:S(2)}, u32[]{:S(2)}) collective-permute-start(bf16[4,96,768]{2,1,0:T(8,128)(2,1)S(1)} %pad_maximum_fusion.7.four), channel_id=1, source_target_pairs={{0,4},{4,0},{8,12},{12,8},{16,20},{20,16},{24,28},{28,24},{1,5},{5... | collective-permute-start | bytes 1769480 | tf_op jit(solution)/shard_map/ppermute | solution.py:524
  209.6 4.2 %collective-permute-start.55 = (bf16[4,96,768]{2,1,0:T(8,128)(2,1)S(1)}, bf16[4,96,768]{2,1,0:T(8,128)(2,1)S(1)}, u32[]{:S(2)}, u32[]{:S(2)}) collective-permute-start(bf16[4,96,768]{2,1,0:T(8,128)(2,1)S(1)} %pad_maximum_fusion.8.four), channel_id=1, source_target_pairs={{0,4},{4,0},{8,12},{12,8},{16,20},{20,16},{24,28},{28,24},{1,5},{5... | collective-permute-start | bytes 1769480 | tf_op jit(solution)/shard_map/ppermute | solution.py:524
  220.7 3.7 %collective-permute-done.52 = bf16[104,768]{1,0:T(8,128)(2,1)S(1)} collective-permute-done((bf16[104,768]{1,0:T(8,128)(2,1)S(1)}, bf16[104,768]{1,0:T(8,128)(2,1)S(1)}, u32[]{:S(2)}, u32[]{:S(2)}) %collective-permute-start.52) | collective-permute-done | bytes 159776 | tf_op jit(solution)/shard_map/ppermute | solution.py:524
  (197 shorter events, 85.4 us)
Async XLA Ops:
  3.1 12.6 %collective-permute-start.1 = (bf16[104,768]{1,0:T(8,128)(2,1)}, bf16[104,768]{1,0:T(8,128)(2,1)S(1)}, u32[]{:S(2)}, u32[]{:S(2)}) collective-permute-start(bf16[104,768]{1,0:T(8,128)(2,1)} %get-tuple-element.158.bias_0), channel_id=1, source_target_pairs={{0,2},{1,3},{2,0},{3,1},{4,6},{5,7},{6,4},{7,5},{8,10},{9,11},{10,... | collective-permute-start | bytes 479240 | tf_op jit(solution)/shard_map/ppermute | solution.py:521
  5.6 13.7 %collective-permute-start = (bf16[104,768]{1,0:T(8,128)(2,1)}, bf16[104,768]{1,0:T(8,128)(2,1)S(1)}, u32[]{:S(2)}, u32[]{:S(2)}) collective-permute-start(bf16[104,768]{1,0:T(8,128)(2,1)} %get-tuple-element.158.bias_0), channel_id=1, source_target_pairs={{0,1},{1,2},{2,3},{3,0},{4,5},{5,6},{6,7},{7,4},{8,9},{9,10},{10,1... | collective-permute-start | bytes 479240 | tf_op jit(solution)/shard_map/ppermute | solution.py:521
  20.5 19.1 %collective-permute-start.6 = (bf16[288,768]{1,0:T(8,128)(2,1)S(1)}, bf16[288,768]{1,0:T(8,128)(2,1)}, u32[]{:S(2)}, u32[]{:S(2)}) collective-permute-start(bf16[288,768]{1,0:T(8,128)(2,1)S(1)} %pad_maximum_fusion.9), channel_id=1, source_target_pairs={{0,1},{1,2},{2,3},{3,0},{4,5},{5,6},{6,7},{7,4},{8,9},{9,10},{10,1... | collective-permute-start | bytes 1327112 | tf_op jit(solution)/shard_map/ppermute | solution.py:521
  21.5 18.0 %collective-permute-start.5 = (bf16[3,96,768]{2,1,0:T(8,128)(2,1)S(1)}, bf16[3,96,768]{2,1,0:T(8,128)(2,1)S(1)}, u32[]{:S(2)}, u32[]{:S(2)}) collective-permute-start(bf16[3,96,768]{2,1,0:T(8,128)(2,1)S(1)} %pad_maximum_fusion.10), channel_id=1, source_target_pairs={{0,24},{4,28},{8,16},{12,20},{16,8},{20,12},{24,0},{28,4},{1,25},{... | collective-permute-start | bytes 1327112 | tf_op jit(solution)/shard_map/ppermute | solution.py:524
  23.7 20.3 %collective-permute-start.4 = (bf16[3,96,768]{2,1,0:T(8,128)(2,1)S(1)}, bf16[3,96,768]{2,1,0:T(8,128)(2,1)S(1)}, u32[]{:S(2)}, u32[]{:S(2)}) collective-permute-start(bf16[3,96,768]{2,1,0:T(8,128)(2,1)S(1)} %pad_maximum_fusion.10), channel_id=1, source_target_pairs={{0,16},{4,20},{8,24},{12,28},{16,0},{20,4},{24,8},{28,12},{1,17},{... | collective-permute-start | bytes 1327112 | tf_op jit(solution)/shard_map/ppermute | solution.py:524
  23.9 20.1 %collective-permute-start.3 = (bf16[3,96,768]{2,1,0:T(8,128)(2,1)S(1)}, bf16[3,96,768]{2,1,0:T(8,128)(2,1)S(1)}, u32[]{:S(2)}, u32[]{:S(2)}) collective-permute-start(bf16[3,96,768]{2,1,0:T(8,128)(2,1)S(1)} %pad_maximum_fusion.10), channel_id=1, source_target_pairs={{0,8},{4,12},{8,0},{12,4},{16,24},{20,28},{24,16},{28,20},{1,9},{5... | collective-permute-start | bytes 1327112 | tf_op jit(solution)/shard_map/ppermute | solution.py:524
  44.9 25.2 %collective-permute-start.12 = (bf16[288,768]{1,0:T(8,128)(2,1)}, bf16[288,768]{1,0:T(8,128)(2,1)}, u32[]{:S(2)}, u32[]{:S(2)}) collective-permute-start(bf16[288,768]{1,0:T(8,128)(2,1)} %copy-done.17), channel_id=1, source_target_pairs={{0,2},{1,3},{2,0},{3,1},{4,6},{5,7},{6,4},{7,5},{8,10},{9,11},{10,... | collective-permute-start | bytes 1327112 | tf_op jit(solution)/shard_map/ppermute | solution.py:521
  48.1 23.0 %collective-permute-start.10 = (bf16[2,192,768]{2,1,0:T(8,128)(2,1)}, bf16[2,192,768]{2,1,0:T(8,128)(2,1)}, u32[]{:S(2)}, u32[]{:S(2)}) collective-permute-start(bf16[2,192,768]{2,1,0:T(8,128)(2,1)} %pad_maximum_fusion.3), channel_id=1, source_target_pairs={{0,16},{4,20},{8,24},{12,28},{16,0},{20,4},{24,8},{28,12},{1,17},{... | collective-permute-start | bytes 1769480 | tf_op jit(solution)/shard_map/ppermute | solution.py:524
  50.2 20.9 %collective-permute-start.9 = (bf16[2,192,768]{2,1,0:T(8,128)(2,1)}, bf16[2,192,768]{2,1,0:T(8,128)(2,1)}, u32[]{:S(2)}, u32[]{:S(2)}) collective-permute-start(bf16[2,192,768]{2,1,0:T(8,128)(2,1)} %pad_maximum_fusion.5), channel_id=1, source_target_pairs={{0,8},{4,12},{8,0},{12,4},{16,24},{20,28},{24,16},{28,20},{1,9},{5... | collective-permute-start | bytes 1769480 | tf_op jit(solution)/shard_map/ppermute | solution.py:524
  52.4 18.7 %collective-permute-start.11 = (bf16[2,96,768]{2,1,0:T(8,128)(2,1)}, bf16[2,96,768]{2,1,0:T(8,128)(2,1)}, u32[]{:S(2)}, u32[]{:S(2)}) collective-permute-start(bf16[2,96,768]{2,1,0:T(8,128)(2,1)} %pad_maximum_fusion.11), channel_id=1, source_target_pairs={{0,24},{4,28},{8,16},{12,20},{16,8},{20,12},{24,0},{28,4},{1,25},{... | collective-permute-start | bytes 884744 | tf_op jit(solution)/shard_map/ppermute | solution.py:524
  76.6 12.7 %collective-permute-start.15 = (bf16[1,192,768]{2,1,0:T(8,128)(2,1)S(1)}, bf16[1,192,768]{2,1,0:T(8,128)(2,1)S(1)}, u32[]{:S(2)}, u32[]{:S(2)}) collective-permute-start(bf16[1,192,768]{2,1,0:T(8,128)(2,1)S(1)} %get-tuple-element.331), channel_id=1, source_target_pairs={{0,16},{4,20},{8,24},{12,28},{16,0},{20,4},{24,8},{28,12},{1,17},{... | collective-permute-start | bytes 884744 | tf_op jit(solution)/shard_map/ppermute | solution.py:524
  111.4 15.2 %collective-permute-start.19 = (bf16[4,96,768]{2,1,0:T(8,128)(2,1)S(1)}, bf16[4,96,768]{2,1,0:T(8,128)(2,1)S(1)}, u32[]{:S(2)}, u32[]{:S(2)}) collective-permute-start(bf16[4,96,768]{2,1,0:T(8,128)(2,1)S(1)} %get-tuple-element.194), channel_id=1, source_target_pairs={{0,8},{4,12},{8,0},{12,4},{16,24},{20,28},{24,16},{28,20},{1,9},{5... | collective-permute-start | bytes 1769480 | tf_op jit(solution)/shard_map/ppermute | solution.py:524
  112.6 14.5 %collective-permute-start.20 = (bf16[4,96,768]{2,1,0:T(8,128)(2,1)S(1)}, bf16[4,96,768]{2,1,0:T(8,128)(2,1)S(1)}, u32[]{:S(2)}, u32[]{:S(2)}) collective-permute-start(bf16[4,96,768]{2,1,0:T(8,128)(2,1)S(1)} %get-tuple-element.195), channel_id=1, source_target_pairs={{0,16},{4,20},{8,24},{12,28},{16,0},{20,4},{24,8},{28,12},{1,17},{... | collective-permute-start | bytes 1769480 | tf_op jit(solution)/shard_map/ppermute | solution.py:524
  128.4 16.0 %collective-permute-start.23 = (bf16[2,4,96,384]{3,2,1,0:T(8,128)(2,1)S(1)}, bf16[2,4,96,384]{3,2,1,0:T(8,128)(2,1)S(1)}, u32[]{:S(2)}, u32[]{:S(2)}) collective-permute-start(bf16[2,4,96,384]{3,2,1,0:T(8,128)(2,1)S(1)} %get-tuple-element.234), channel_id=1, source_target_pairs={{0,8},{4,12},{8,0},{12,4},{16,24},{20,28},{24,16},{28,20},{1,9},{5... | collective-permute-start | bytes 1769480 | tf_op jit(solution)/shard_map/ppermute | solution.py:524
  128.6 15.8 %collective-permute-start.24 = (bf16[2,4,96,384]{3,2,1,0:T(8,128)(2,1)S(1)}, bf16[2,4,96,384]{3,2,1,0:T(8,128)(2,1)S(1)}, u32[]{:S(2)}, u32[]{:S(2)}) collective-permute-start(bf16[2,4,96,384]{3,2,1,0:T(8,128)(2,1)S(1)} %get-tuple-element.235), channel_id=1, source_target_pairs={{0,16},{4,20},{8,24},{12,28},{16,0},{20,4},{24,8},{28,12},{1,17},{... | collective-permute-start | bytes 1769480 | tf_op jit(solution)/shard_map/ppermute | solution.py:524
  131.0 13.4 %collective-permute-start.27 = (bf16[96,768]{1,0:T(8,128)(2,1)S(1)}, bf16[96,768]{1,0:T(8,128)(2,1)S(1)}, u32[]{:S(2)}, u32[]{:S(2)}) collective-permute-start(bf16[96,768]{1,0:T(8,128)(2,1)S(1)} %get-tuple-element.328), channel_id=1, source_target_pairs={{0,1},{1,2},{2,3},{3,0},{4,5},{5,6},{6,7},{7,4},{8,9},{9,10},{10,1... | collective-permute-start | bytes 442376 | tf_op jit(solution)/shard_map/ppermute | solution.py:521
  131.5 12.9 %collective-permute-start.26 = (bf16[96,768]{1,0:T(8,128)(2,1)S(1)}, bf16[96,768]{1,0:T(8,128)(2,1)S(1)}, u32[]{:S(2)}, u32[]{:S(2)}) collective-permute-start(bf16[96,768]{1,0:T(8,128)(2,1)S(1)} %get-tuple-element.329), channel_id=1, source_target_pairs={{0,2},{1,3},{2,0},{3,1},{4,6},{5,7},{6,4},{7,5},{8,10},{9,11},{10,... | collective-permute-start | bytes 442376 | tf_op jit(solution)/shard_map/ppermute | solution.py:521
  150.3 12.4 %collective-permute-start.34 = (bf16[96,768]{1,0:T(8,128)(2,1)S(1)}, bf16[96,768]{1,0:T(8,128)(2,1)S(1)}, u32[]{:S(2)}, u32[]{:S(2)}) collective-permute-start(bf16[96,768]{1,0:T(8,128)(2,1)S(1)} %get-tuple-element.325), channel_id=1, source_target_pairs={{0,2},{1,3},{2,0},{3,1},{4,6},{5,7},{6,4},{7,5},{8,10},{9,11},{10,... | collective-permute-start | bytes 442376 | tf_op jit(solution)/shard_map/ppermute | solution.py:521
  151.5 13.6 %collective-permute-start.33 = (bf16[96,768]{1,0:T(8,128)(2,1)S(1)}, bf16[96,768]{1,0:T(8,128)(2,1)S(1)}, u32[]{:S(2)}, u32[]{:S(2)}) collective-permute-start(bf16[96,768]{1,0:T(8,128)(2,1)S(1)} %get-tuple-element.326), channel_id=1, source_target_pairs={{0,3},{1,0},{2,1},{3,2},{4,7},{5,4},{6,5},{7,6},{8,11},{9,8},{10,9... | collective-permute-start | bytes 442376 | tf_op jit(solution)/shard_map/ppermute | solution.py:521
  157.6 17.6 %collective-permute-start.31 = (bf16[2,4,104,384]{3,2,1,0:T(8,128)(2,1)S(1)}, bf16[2,4,104,384]{3,2,1,0:T(8,128)(2,1)S(1)}, u32[]{:S(2)}, u32[]{:S(2)}) collective-permute-start(bf16[2,4,104,384]{3,2,1,0:T(8,128)(2,1)S(1)} %get-tuple-element.243), channel_id=1, source_target_pairs={{0,8},{4,12},{8,0},{12,4},{16,24},{20,28},{24,16},{28,20},{1,9},{5... | collective-permute-start | bytes 1916936 | tf_op jit(solution)/shard_map/ppermute | solution.py:524
  158.6 16.6 %collective-permute-start.32 = (bf16[2,4,104,384]{3,2,1,0:T(8,128)(2,1)S(1)}, bf16[2,4,104,384]{3,2,1,0:T(8,128)(2,1)S(1)}, u32[]{:S(2)}, u32[]{:S(2)}) collective-permute-start(bf16[2,4,104,384]{3,2,1,0:T(8,128)(2,1)S(1)} %get-tuple-element.244), channel_id=1, source_target_pairs={{0,16},{4,20},{8,24},{12,28},{16,0},{20,4},{24,8},{28,12},{1,17},{... | collective-permute-start | bytes 1916936 | tf_op jit(solution)/shard_map/ppermute | solution.py:524
  189.7 14.3 %collective-permute-start.47 = (bf16[104,768]{1,0:T(8,128)(2,1)S(1)}, bf16[104,768]{1,0:T(8,128)(2,1)S(1)}, u32[]{:S(2)}, u32[]{:S(2)}) collective-permute-start(bf16[104,768]{1,0:T(8,128)(2,1)S(1)} %get-tuple-element.318), channel_id=1, source_target_pairs={{0,1},{1,2},{2,3},{3,0},{4,5},{5,6},{6,7},{7,4},{8,9},{9,10},{10,1... | collective-permute-start | bytes 479240 | tf_op jit(solution)/shard_map/ppermute | solution.py:521
  191.3 18.3 %collective-permute-start.46 = (bf16[104,768]{1,0:T(8,128)(2,1)S(1)}, bf16[104,768]{1,0:T(8,128)(2,1)S(1)}, u32[]{:S(2)}, u32[]{:S(2)}) collective-permute-start(bf16[104,768]{1,0:T(8,128)(2,1)S(1)} %get-tuple-element.320), channel_id=1, source_target_pairs={{0,2},{1,3},{2,0},{3,1},{4,6},{5,7},{6,4},{7,5},{8,10},{9,11},{10,... | collective-permute-start | bytes 479240 | tf_op jit(solution)/shard_map/ppermute | solution.py:521
  204.0 12.7 %collective-permute-start.54 = (bf16[4,96,768]{2,1,0:T(8,128)(2,1)S(1)}, bf16[4,96,768]{2,1,0:T(8,128)(2,1)S(1)}, u32[]{:S(2)}, u32[]{:S(2)}) collective-permute-start(bf16[4,96,768]{2,1,0:T(8,128)(2,1)S(1)} %pad_maximum_fusion.7.four), channel_id=1, source_target_pairs={{0,4},{4,0},{8,12},{12,8},{16,20},{20,16},{24,28},{28,24},{1,5},{5... | collective-permute-start | bytes 1769480 | tf_op jit(solution)/shard_map/ppermute | solution.py:524
  (51 other events, 437.3 us)

commit v6 on v5

--- a/solution.py
+++ b/solution.py
@@ -89,11 +89,15 @@
     return places[:4] + places[6:] + places[4:6]
 
 
-def place_slots(four, other, r, down_rows, rows, places, dest, base, columns):
+def place_slots(pieces, others, r, down_rows, rows, places, dest, base, columns):
+    upper, lower = slice(0, rows), slice(rows, 2 * rows)
+    sources = ((0, upper), (1, upper), (2, lower), (4, lower))
+    if not down_rows:
+        sources = ((0, lower), (1, lower), (2, upper), (3, upper))
     for s in range(GROUP):
-        low = rows if (s < GROUP // 2) != down_rows else 0
+        piece, part = sources[s // 2]
         at = pl.multiple_of(base + places[s] * rows, rows)
-        dest[pl.ds(at, rows), columns] = (other if s % 2 else four)[s // 2, r, low : low + rows]
+        dest[pl.ds(at, rows), columns] = (others if s % 2 else pieces)[piece][r, part]
 
 
 def put_slots(index, r, rows, low, keep, send, by_axis=False):
@@ -234,24 +238,24 @@
     queries[...] = (low.astype(f32) * (HEAD_DIM**-0.5)).astype(bf16)
     keys[...] = nt(tokens[...], weights[1]).astype(bf16)
     values[...] = (nt(tokens[...], weights[2]) + row[1:2, :]).astype(bf16)
-    lane = lax.broadcasted_iota(jnp.int32, (PASSAGE, LANES), 1) // HEAD_DIM
-    lane_all = lax.broadcasted_iota(jnp.int32, (length, LANES), 1) // HEAD_DIM
-
-    def head(i, carry):
-        half = i & 1
-        at = pl.ds(pl.multiple_of((i >> 1) * LANES, LANES), LANES)
-        for b in range(length // PASSAGE):
-            lo, hi = band(b, length)
-            block = slice(b * PASSAGE, (b + 1) * PASSAGE)
-            q = queries[block, at]
-            masked = jnp.where(lane == half, q, jnp.zeros_like(q))
-            scores = nt(keys[lo:hi, at], masked) + bias[b, : hi - lo, :]
-            probs_t[0, lo:hi, block] = softmax_columns(scores).astype(bf16)
-        found = tn(probs_t[0], values[:, at]).astype(bf16)
-        contexts[:, at] = jnp.where(lane_all == half, found, contexts[:, at])
+    first = lax.broadcasted_iota(jnp.int32, (PASSAGE, LANES), 1) < HEAD_DIM
+    first_all = lax.broadcasted_iota(jnp.int32, (length, LANES), 1) < HEAD_DIM
+
+    def pair(i, carry):
+        at = pl.ds(pl.multiple_of(i * LANES, LANES), LANES)
+        for half, mine in enumerate((first, jnp.logical_not(first))):
+            for b in range(length // PASSAGE):
+                lo, hi = band(b, length)
+                block = slice(b * PASSAGE, (b + 1) * PASSAGE)
+                q = queries[block, at]
+                masked = jnp.where(mine, q, jnp.zeros_like(q))
+                scores = nt(keys[lo:hi, at], masked) + bias[b, : hi - lo, :]
+                probs_t[half, lo:hi, block] = softmax_columns(scores).astype(bf16)
+        found = [tn(probs_t[half], values[:, at]) for half in range(2)]
+        contexts[:, at] = jnp.where(first_all, *found).astype(bf16)
         return carry
 
-    lax.fori_loop(0, width // HEAD_DIM, head, 0)
+    lax.fori_loop(0, width // LANES, pair, 0)
     attended[...] = nn(contexts[...], wo[...]) + vector(output_bias)
 
     def norm(rows):
@@ -289,13 +293,16 @@
 
 
 def ffn_first(
-    index_ref, normal, gain, shift, down_bias, bias_0, bias_1, bias_2, own_up, own_down, four, other,
+    index_ref, normal, gain, shift, down_bias, bias_0, bias_1, bias_2, own_up, own_down,
+    left, from_x, from_y, corner, right, left_o, from_x_o, from_y_o, corner_o, right_o,
     activated, slope, low_t, mixed, up, down,
     hidden, lines, low_rows,
 ):
     units = own_up.shape[1]
-    rows = four.shape[2] // 2
-    quarters = four.shape[1] + 1
+    four = (left, from_x, from_y, corner, right)
+    other = (left_o, from_x_o, from_y_o, corner_o, right_o)
+    rows = corner.shape[1]
+    quarters = corner.shape[0] + 1
     biases = (bias_0, bias_1, bias_2)
     up_places, down_places = eighths(index_ref[0]), places_gathered(index_ref[0])
     normed = normal[...] * vector(gain) + vector(shift)
@@ -325,13 +332,15 @@
 
 def ffn_last(
     index_ref, normal, cotangent, gain, shift, second_gain, second_shift, bias, activated, mixed,
-    four, other,
+    left, from_x, from_y, corner, right, left_o, from_x_o, from_y_o, corner_o, right_o,
     output, grad_mixed, grad_two, sums, slope, up, down, keep, send,
     own, total,
 ):
     length, width = normal.shape
     units = up.shape[1]
-    rows = four.shape[2] // 2
+    four = (left, from_x, from_y, corner, right)
+    other = (left_o, from_x_o, from_y_o, corner_o, right_o)
+    rows = corner.shape[1]
     index = index_ref[0]
     place_slots(four, other, 0, False, rows, eighths(index), up, 0, slice(None))
     place_slots(four, other, 0, True, rows, places_gathered(index), down, 0, slice(None))
@@ -625,11 +634,7 @@
             left = jnp.stack([g[: part + rows] for g in line])
             right = jnp.stack([g[part:] for g in line])
             corner = swap(jnp.stack([g[part : part + rows] for g in line]), 6)
-            return left, swap(left, 2), swap(right, 4), corner, right[:, rows:]
-
-        def slots_mixed(pieces):
-            left, from_x, from_y, corner, own = pieces
-            return jnp.stack([left, from_x, from_y, jnp.concatenate([corner, own], axis=1)])
+            return left, swap(left, 2), swap(right, 4), corner, right
 
         att_four = [att_line] + [swap(att_line, b) for b in (2, 4, 6)]
         att_four, ffn_line[:-1] = tie(att_four, ffn_line[:-1])
@@ -662,14 +667,13 @@
             "s" + "v" * 11,
             [
                 pltpu.VMEM((blocks, 3 * PASSAGE, PASSAGE), f32),
-                pltpu.VMEM((1, length, length), bf16),
+                pltpu.VMEM((2, length, length), bf16),
                 pltpu.VMEM((8, width), f32),
                 pltpu.VMEM((length, width), f32),
             ],
         )
         normal, ffn_four, ffn_line[-1] = tie(normal, ffn_four, ffn_line[-1])
-        ffn_four = slots_mixed(ffn_four)
-        ffn_other = swap(ffn_four, 1)
+        ffn_other = [swap(array, 1) for array in ffn_four]
         last_four = plane_mixed(ffn_line[-1:])
         inner = (n_mp - 1) * units
         hidden_low = shape((length, inner), bf16)
@@ -693,10 +697,10 @@
                 *ffn_biases[:-1],
                 up_weight,
                 down_weight,
-                ffn_four,
-                ffn_other,
+                *ffn_four,
+                *ffn_other,
             ],
-            "s" + "v" * 11,
+            "s" + "v" * 19,
             [
                 pltpu.VMEM((length, units), f32),
                 pltpu.VMEM((n_mp, 8, units), f32),
@@ -704,8 +708,7 @@
             ],
         )
         activated, last_four = tie(activated, last_four)
-        last_four = slots_mixed(last_four)
-        last_other = swap(last_four, 1)
+        last_other = [swap(array, 1) for array in last_four]
         pieces = shape((half, n_mp, part, width), bf16)
         (
             output,
@@ -742,10 +745,10 @@
                 ffn_biases[-1],
                 activated,
                 mixed,
-                last_four,
-                last_other,
+                *last_four,
+                *last_other,
             ],
-            "s" + "v" * 11,
+            "s" + "v" * 19,
             [pltpu.VMEM((length, units), bf16), pltpu.VMEM((length, width), f32)],
         )
         got_down = swap(send_down, 1)
@@ -853,10 +856,10 @@
         )
         left_now, right_now = add(stay_left, come_left), add(stay_right, come_right)
         come_left, come_right = swap(left_now[1], 4), swap(right_now[1], 2)
+        up_line[3:], come_left, come_right, down_x, down_y = tie(
+            up_line[3:], come_left, come_right, down_x, down_y
+        )
         come_x, come_y = swap(down_x, 4), swap(down_y, 2)
-        up_line[3:], come_left, come_right, come_x, come_y = tie(
-            up_line[3:], come_left, come_right, come_x, come_y
-        )
         att_parts = jnp.concatenate(
             [add(left_now[0], come_left), add(right_now[0], come_right)], axis=-1
         )

time: 230 us -> 224 us (0.974)
  waiting for transfers between devices: 77.2 us -> 71.4 us
  other arithmetic: 10.4 us -> 6.13 us
  starting transfers between devices: 59.9 us -> 62.3 us
    ppermute x39 -> x47, waiting for transfers between devices: 28 us -> 24.2 us  [swap(): return lax.ppermute(array, 'dp', [(i, i ^ bits) for i in range(n_dp)])]
    unnamed x38 -> x50, local copies, waits for them, and re-layouts: 1.53 us -> 5.19 us
    another operation x4 -> x0, other arithmetic: 2.98 us -> none  [slots_mixed(): jnp.stack([left, from_x, from_y, jnp.concatenate([corner, own], axis=1)])]
    ppermute x39 -> x47, starting transfers between devices: 41.2 us -> 43.1 us  [swap(): return lax.ppermute(array, 'dp', [(i, i ^ bits) for i in range(n_dp)])]
  transfers between devices with their start and end apart: 57 -> 65, of which waited for: 22 -> 24; matrix products, arithmetic and copies ran while one was open for 6% -> 4% of each run, Pallas kernels for 24% -> 24%
where the time goes in v6:
time: 224 us; the launch traced here: 223 us
  waiting for transfers between devices  71.4 us (32%)
  Pallas kernels  71 us (32%)
  starting transfers between devices  62.3 us (28%)
  local copies, waits for them, and re-layouts  11.1 us (5%)
  other arithmetic  6.13 us (3%)
    pallas_call x13, Pallas kernels, call(): pl.pallas_call(body, name=name, out_shape=tuple(outs), in_specs=[spec(k)...  71 us
    ppermute x18, waiting for transfers between devices, rotate(): lax.ppermute(array, 'mp', [(i, (i + step) % n_mp) for i in range(n_mp)])  47.1 us
    ppermute x47, starting transfers between devices, swap(): return lax.ppermute(array, 'dp', [(i, i ^ bits) for i in range(n_dp)])  43.1 us
    ppermute x47, waiting for transfers between devices, swap(): return lax.ppermute(array, 'dp', [(i, i ^ bits) for i in range(n_dp)])  24.2 us
    ppermute x18, starting transfers between devices, rotate(): lax.ppermute(array, 'mp', [(i, (i + step) % n_mp) for i in range(n_mp)])  19.2 us
    unnamed x50, local copies, waits for them, and re-layouts  5.19 us
  transfers between devices with their start and end apart: 65, of which 24 were waited for; matrix products, arithmetic and copies ran while one was open for 4% of the time, Pallas kernels for 24%

profile of v6, /device:TPU:9, one launch (start us, length us, event | category | flops | bytes accessed | tf_op | source)
XLA Modules:
  0.0 223.2 jit_solution(1907274654867624002)
XLA Ops:
  10.5 5.2 %collective-permute-done.1.bias_2.bias = bf16[104,768]{1,0:T(8,128)(2,1)S(1)} collective-permute-done((bf16[104,768]{1,0:T(8,128)(2,1)}, bf16[104,768]{1,0:T(8,128)(2,1)S(1)}, u32[]{:S(2)}, u32[]{:S(2)}) %collective-permute-start.1) | collective-permute-done | bytes 159776 | tf_op jit(solution)/shard_map/ppermute | solution.py:530
  15.7 3.5 %collective-permute-done.bias_1 = bf16[104,768]{1,0:T(8,128)(2,1)S(1)} collective-permute-done((bf16[104,768]{1,0:T(8,128)(2,1)}, bf16[104,768]{1,0:T(8,128)(2,1)S(1)}, u32[]{:S(2)}, u32[]{:S(2)}) %collective-permute-start) | collective-permute-done | bytes 159776 | tf_op jit(solution)/shard_map/ppermute | solution.py:530
  24.2 6.7 %collective-permute-done.7 = bf16[288,768]{1,0:T(8,128)(2,1)S(1)} collective-permute-done((bf16[288,768]{1,0:T(8,128)(2,1)}, bf16[288,768]{1,0:T(8,128)(2,1)S(1)}, u32[]{:S(2)}, u32[]{:S(2)}) %collective-permute-start.7) | collective-permute-done | bytes 442400 | tf_op jit(solution)/shard_map/ppermute | solution.py:530
  30.9 9.0 %collective-permute-done.6 = bf16[288,768]{1,0:T(8,128)(2,1)S(1)} collective-permute-done((bf16[288,768]{1,0:T(8,128)(2,1)}, bf16[288,768]{1,0:T(8,128)(2,1)S(1)}, u32[]{:S(2)}, u32[]{:S(2)}) %collective-permute-start.6) | collective-permute-done | bytes 442400 | tf_op jit(solution)/shard_map/ppermute | solution.py:530
  39.9 4.1 %collective-permute-done.4 = bf16[3,96,768]{2,1,0:T(8,128)(2,1)S(1)} collective-permute-done((bf16[3,96,768]{2,1,0:T(8,128)(2,1)S(1)}, bf16[3,96,768]{2,1,0:T(8,128)(2,1)S(1)}, u32[]{:S(2)}, u32[]{:S(2)}) %collective-permute-start.4) | collective-permute-done | bytes 442400 | tf_op jit(solution)/shard_map/ppermute | solution.py:533
  55.7 12.3 %att_forward.1 = (bf16[512,768]{1,0:T(8,128)(2,1)S(1)}, bf16[512,768]{1,0:T(8,128)(2,1)S(1)}, bf16[512,768]{1,0:T(8,128)(2,1)S(1)}, bf16[512,768]{1,0:T(8,128)(2...) custom-call(s32[1]{0:T(128)} %bitcast.index_ref, ...), custom_call_target="tpu_custom_call" | custom-call | bytes 243576 | tf_op jit(solution)/shard_map/att_forward/pallas_call | solution.py:62
  77.6 8.8 %ffn_first.1 = (bf16[512,2304]{1,0:T(8,128)(2,1)S(1)}, bf16[512,2304]{1,0:T(8,128)(2,1)S(1)}, bf16[768,512]{1,0:T(8,128)(2,1)S(1)}, f32[512,768]{1,0:T(8,128)S(1...) custom-call(s32[1]{0:T(128)} %bitcast.index_ref, f32[512,768]{1,0:T(8,128)S(1)} %get-tuple-element.168.normal, ...), custom_call_target="tpu_custom_call" | custom-call | bytes 373128 | tf_op jit(solution)/shard_map/ffn_first/pallas_call | solution.py:62
  90.5 9.3 %ffn_last.1 = (bf16[512,768]{1,0:T(8,128)(2,1)}, bf16[512,768]{1,0:T(8,128)(2,1)S(1)}, f32[512,768]{1,0:T(8,128)S(1)}, f32[8,768]{1,0:T(8,128)S(1)}, bf16[512,76...) custom-call(s32[1]{0:T(128)} %bitcast.index_ref, ...), custom_call_target="tpu_custom_call" | custom-call | bytes 314784 | tf_op jit(solution)/shard_map/ffn_last/pallas_call | solution.py:62
  100.2 3.5 %ffn_slopes.1 = (bf16[512,3072]{1,0:T(8,128)(2,1)S(1)}, f32[8,768]{1,0:T(8,128)S(1)}) custom-call(bf16[512,768]{1,0:T(8,128)(2,1)S(1)} %get-tuple-element.184.grad_mixed, bf16[512,2304]{1,0:T(8,128)(2,1)S(1)} %get-tuple-element.185.slope, bf16[512,768]{1,0:T(8,128)(2,1)S(1)} %get-tuple-element.186.slope_last, bf16[2304,768]{1,0:T(8,128)(2,1)S(1)} %get-tuple-element.187.down, ...), custom_call_target="tpu_custom_call" | custom-call | bytes 184704 | tf_op jit(solution)/shard_map/ffn_slopes/pallas_call | solution.py:62
  104.7 3.6 %ffn_grads.1 = (bf16[4,4,96,768]{3,2,1,0:T(8,128)(2,1)S(1)}, bf16[4,4,96,768]{3,2,1,0:T(8,128)(2,1)S(1)}) custom-call(s32[1]{0:T(128)} %bitcast.index_ref, bf16[512,3072]{1,0:T(8,128)(2,1)S(1)} %get-tuple-element.204.hidden, bf16[768,512]{1,0:T(8,128)(2,1)S(1)} %get-tuple-element.201.low_t), custom_call_target="tpu_custom_call" | custom-call | bytes 135168 | tf_op jit(solution)/shard_map/ffn_grads/pallas_call | solution.py:62
  110.1 3.9 %ffn_norm.1 = (f32[512,768]{1,0:T(8,128)S(1)}, bf16[512,768]{1,0:T(8,128)(2,1)S(1)}, f32[8,768]{1,0:T(8,128)S(1)}) custom-call(bf16[512,3072]{1,0:T(8,128)(2,1)S(1)} %get-tuple-element.204.hidden, f32[512,768]{1,0:T(8,128)S(1)} %get-tuple-element.205.grad_two, f32[512,768]{1,0:T(8,128)S(1)} %get-tuple-element.168.normal, ...), custom_call_target="tpu_custom_call" | custom-call | bytes 209336 | tf_op jit(solution)/shard_map/ffn_norm/pallas_call | solution.py:62
  114.3 9.4 %att_backward.2 = (bf16[512,384]{1,0:T(8,128)(2,1)S(1)}, bf16[512,384]{1,0:T(8,128)(2,1)S(1)}, bf16[512,384]{1,0:T(8,128)(2,1)S(1)}, bf16[4,2,104,768]{3,2,1,0:T(8,128)(2,1)S(1)}, bf16[4,2,104,768]{3,2,1,0:T(8,128)(2,1)S(1)}) custom-call(s32[1]{0:T(128)} %bitcast.index_ref, bf16[512,768]{1,0:T(8,128)(2,1)S(1)} %get-tuple-element.196.queries, ...), custom_call_target="tpu_custom_call" | custom-call | bytes 151744 | tf_op jit(solution)/shard_map/att_backward/pallas_call | solution.py:62
  127.9 3.1 %collective-permute-start.34 = (bf16[96,768]{1,0:T(8,128)(2,1)S(1)}, bf16[96,768]{1,0:T(8,128)(2,1)S(1)}, u32[]{:S(2)}, u32[]{:S(2)}) collective-permute-start(bf16[96,768]{1,0:T(8,128)(2,1)S(1)} %get-tuple-element.329), channel_id=1, source_target_pairs={{0,2},{1,3},{2,0},{3,1},{4,6},{5,7},{6,4},{7,5},{8,10},{9,11},{10,... | collective-permute-start | bytes 442376 | tf_op jit(solution)/shard_map/ppermute | solution.py:530
  131.1 9.6 %att_backward.3 = (bf16[512,384]{1,0:T(8,128)(2,1)S(1)}, bf16[512,384]{1,0:T(8,128)(2,1)S(1)}, bf16[512,384]{1,0:T(8,128)(2,1)S(1)}, bf16[4,2,104,768]{3,2,1,0:T(8,128)(2,1)S(1)}, bf16[4,2,104,768]{3,2,1,0:T(8,128)(2,1)S(1)}) custom-call(s32[1]{0:T(128)} %bitcast.index_ref, bf16[512,768]{1,0:T(8,128)(2,1)S(1)} %get-tuple-element.196.queries, ...), custom_call_target="tpu_custom_call" | custom-call | bytes 151744 | tf_op jit(solution)/shard_map/att_backward/pallas_call | solution.py:62
  149.5 4.1 %collective-permute-done.37 = bf16[4,96,384]{2,1,0:T(8,128)(2,1)S(1)} collective-permute-done((bf16[4,96,384]{2,1,0:T(8,128)(2,1)S(1)}, bf16[4,96,384]{2,1,0:T(8,128)(2,1)S(1)}, u32[]{:S(2)}, u32[]{:S(2)}) %collective-permute-start.37) | collective-permute-done | bytes 294944 | tf_op jit(solution)/shard_map/ppermute | solution.py:533
  156.4 2.9 %collective-permute-done.42 = bf16[96,768]{1,0:T(8,128)(2,1)S(1)} collective-permute-done((bf16[96,768]{1,0:T(8,128)(2,1)S(1)}, bf16[96,768]{1,0:T(8,128)(2,1)S(1)}, u32[]{:S(2)}, u32[]{:S(2)}) %collective-permute-start.42) | collective-permute-done | bytes 147488 | tf_op jit(solution)/shard_map/ppermute | solution.py:530
  162.6 9.2 %collective-permute-done.45 = bf16[96,768]{1,0:T(8,128)(2,1)S(1)} collective-permute-done((bf16[96,768]{1,0:T(8,128)(2,1)S(1)}, bf16[96,768]{1,0:T(8,128)(2,1)S(1)}, u32[]{:S(2)}, u32[]{:S(2)}) %collective-permute-start.45) | collective-permute-done | bytes 147488 | tf_op jit(solution)/shard_map/ppermute | solution.py:530
  173.8 3.5 %input_backward.1 = bf16[512,768]{1,0:T(8,128)(2,1)} custom-call(bf16[512,384]{1,0:T(8,128)(2,1)S(1)} %get-tuple-element.267.q0, bf16[512,384]{1,0:T(8,128)(2,1)S(1)} %get-tuple-element.268.k0, bf16[512,384]{1,0:T(8,128)(2,1)S(1)} %get-tuple-element.269.v0, bf16[512,384]{1,0:T(8,128)(2,1)S(1)} %get-tuple-element.270.q1, ...), custom_call_target="tpu_custom_call" | custom-call | bytes 129024 | tf_op jit(solution)/shard_map/input_backward/pallas_call | solution.py:62
  178.1 3.1 %collective-permute-done.47 = bf16[4,104,384]{2,1,0:T(8,128)(2,1)S(1)} collective-permute-done((bf16[4,104,384]{2,1,0:T(8,128)(2,1)S(1)}, bf16[4,104,384]{2,1,0:T(8,128)(2,1)S(1)}, u32[]{:S(2)}, u32[]{:S(2)}) %collective-permute-start.47) | collective-permute-done | bytes 319520 | tf_op jit(solution)/shard_map/ppermute | solution.py:533
  185.1 3.1 %collective-permute-start.54 = (bf16[104,768]{1,0:T(8,128)(2,1)S(1)}, bf16[104,768]{1,0:T(8,128)(2,1)S(1)}, u32[]{:S(2)}, u32[]{:S(2)}) collective-permute-start(bf16[104,768]{1,0:T(8,128)(2,1)S(1)} %get-tuple-element.320), channel_id=1, source_target_pairs={{0,2},{1,3},{2,0},{3,1},{4,6},{5,7},{6,4},{7,5},{8,10},{9,11},{10,... | collective-permute-start | bytes 479240 | tf_op jit(solution)/shard_map/ppermute | solution.py:530
  190.0 5.1 %collective-permute-done.49 = bf16[104,768]{1,0:T(8,128)(2,1)S(1)} collective-permute-done((bf16[104,768]{1,0:T(8,128)(2,1)S(1)}, bf16[104,768]{1,0:T(8,128)(2,1)S(1)}, u32[]{:S(2)}, u32[]{:S(2)}) %collective-permute-start.49) | collective-permute-done | bytes 159776 | tf_op jit(solution)/shard_map/ppermute | solution.py:530
  197.8 5.5 %collective-permute-start.62 = (bf16[4,96,768]{2,1,0:T(8,128)(2,1)S(1)}, bf16[4,96,768]{2,1,0:T(8,128)(2,1)S(1)}, u32[]{:S(2)}, u32[]{:S(2)}) collective-permute-start(bf16[4,96,768]{2,1,0:T(8,128)(2,1)S(1)} %pad_maximum_fusion.5.four), channel_id=1, source_target_pairs={{0,4},{4,0},{8,12},{12,8},{16,20},{20,16},{24,28},{28,24},{1,5},{5... | collective-permute-start | bytes 1769480 | tf_op jit(solution)/shard_map/ppermute | solution.py:533
  203.4 4.0 %collective-permute-start.63 = (bf16[4,96,768]{2,1,0:T(8,128)(2,1)S(1)}, bf16[4,96,768]{2,1,0:T(8,128)(2,1)S(1)}, u32[]{:S(2)}, u32[]{:S(2)}) collective-permute-start(bf16[4,96,768]{2,1,0:T(8,128)(2,1)S(1)} %pad_maximum_fusion.6.four), channel_id=1, source_target_pairs={{0,4},{4,0},{8,12},{12,8},{16,20},{20,16},{24,28},{28,24},{1,5},{5... | collective-permute-start | bytes 1769480 | tf_op jit(solution)/shard_map/ppermute | solution.py:533
  214.3 3.7 %collective-permute-done.60 = bf16[104,768]{1,0:T(8,128)(2,1)S(1)} collective-permute-done((bf16[104,768]{1,0:T(8,128)(2,1)S(1)}, bf16[104,768]{1,0:T(8,128)(2,1)S(1)}, u32[]{:S(2)}, u32[]{:S(2)}) %collective-permute-start.60) | collective-permute-done | bytes 159776 | tf_op jit(solution)/shard_map/ppermute | solution.py:533
  (219 shorter events, 85.6 us)
Async XLA Ops:
  3.1 12.6 %collective-permute-start.1 = (bf16[104,768]{1,0:T(8,128)(2,1)}, bf16[104,768]{1,0:T(8,128)(2,1)S(1)}, u32[]{:S(2)}, u32[]{:S(2)}) collective-permute-start(bf16[104,768]{1,0:T(8,128)(2,1)} %get-tuple-element.158.bias_0), channel_id=1, source_target_pairs={{0,2},{1,3},{2,0},{3,1},{4,6},{5,7},{6,4},{7,5},{8,10},{9,11},{10,... | collective-permute-start | bytes 479240 | tf_op jit(solution)/shard_map/ppermute | solution.py:530
  5.6 13.7 %collective-permute-start = (bf16[104,768]{1,0:T(8,128)(2,1)}, bf16[104,768]{1,0:T(8,128)(2,1)S(1)}, u32[]{:S(2)}, u32[]{:S(2)}) collective-permute-start(bf16[104,768]{1,0:T(8,128)(2,1)} %get-tuple-element.158.bias_0), channel_id=1, source_target_pairs={{0,1},{1,2},{2,3},{3,0},{4,5},{5,6},{6,7},{7,4},{8,9},{9,10},{10,1... | collective-permute-start | bytes 479240 | tf_op jit(solution)/shard_map/ppermute | solution.py:530
  20.5 19.4 %collective-permute-start.6 = (bf16[288,768]{1,0:T(8,128)(2,1)}, bf16[288,768]{1,0:T(8,128)(2,1)S(1)}, u32[]{:S(2)}, u32[]{:S(2)}) collective-permute-start(bf16[288,768]{1,0:T(8,128)(2,1)} %pad_maximum_fusion.7), channel_id=1, source_target_pairs={{0,1},{1,2},{2,3},{3,0},{4,5},{5,6},{6,7},{7,4},{8,9},{9,10},{10,1... | collective-permute-start | bytes 1327112 | tf_op jit(solution)/shard_map/ppermute | solution.py:530
  21.5 18.3 %collective-permute-start.5 = (bf16[3,96,768]{2,1,0:T(8,128)(2,1)S(1)}, bf16[3,96,768]{2,1,0:T(8,128)(2,1)S(1)}, u32[]{:S(2)}, u32[]{:S(2)}) collective-permute-start(bf16[3,96,768]{2,1,0:T(8,128)(2,1)S(1)} %pad_maximum_fusion.8), channel_id=1, source_target_pairs={{0,24},{4,28},{8,16},{12,20},{16,8},{20,12},{24,0},{28,4},{1,25},{... | collective-permute-start | bytes 1327112 | tf_op jit(solution)/shard_map/ppermute | solution.py:533
  23.7 20.3 %collective-permute-start.4 = (bf16[3,96,768]{2,1,0:T(8,128)(2,1)S(1)}, bf16[3,96,768]{2,1,0:T(8,128)(2,1)S(1)}, u32[]{:S(2)}, u32[]{:S(2)}) collective-permute-start(bf16[3,96,768]{2,1,0:T(8,128)(2,1)S(1)} %pad_maximum_fusion.8), channel_id=1, source_target_pairs={{0,16},{4,20},{8,24},{12,28},{16,0},{20,4},{24,8},{28,12},{1,17},{... | collective-permute-start | bytes 1327112 | tf_op jit(solution)/shard_map/ppermute | solution.py:533
  23.9 20.1 %collective-permute-start.3 = (bf16[3,96,768]{2,1,0:T(8,128)(2,1)S(1)}, bf16[3,96,768]{2,1,0:T(8,128)(2,1)S(1)}, u32[]{:S(2)}, u32[]{:S(2)}) collective-permute-start(bf16[3,96,768]{2,1,0:T(8,128)(2,1)S(1)} %pad_maximum_fusion.8), channel_id=1, source_target_pairs={{0,8},{4,12},{8,0},{12,4},{16,24},{20,28},{24,16},{28,20},{1,9},{5... | collective-permute-start | bytes 1327112 | tf_op jit(solution)/shard_map/ppermute | solution.py:533
  44.9 23.2 %collective-permute-start.12 = (bf16[288,768]{1,0:T(8,128)(2,1)}, bf16[288,768]{1,0:T(8,128)(2,1)}, u32[]{:S(2)}, u32[]{:S(2)}) collective-permute-start(bf16[288,768]{1,0:T(8,128)(2,1)} %pad_maximum_fusion.7), channel_id=1, source_target_pairs={{0,2},{1,3},{2,0},{3,1},{4,6},{5,7},{6,4},{7,5},{8,10},{9,11},{10,... | collective-permute-start | bytes 1327112 | tf_op jit(solution)/shard_map/ppermute | solution.py:530
  46.2 22.0 %collective-permute-start.9 = (bf16[2,192,768]{2,1,0:T(8,128)(2,1)S(1)}, bf16[2,192,768]{2,1,0:T(8,128)(2,1)}, u32[]{:S(2)}, u32[]{:S(2)}) collective-permute-start(bf16[2,192,768]{2,1,0:T(8,128)(2,1)S(1)} %pad_maximum_fusion.2.left), channel_id=1, source_target_pairs={{0,8},{4,12},{8,0},{12,4},{16,24},{20,28},{24,16},{28,20},{1,9},{5... | collective-permute-start | bytes 1769480 | tf_op jit(solution)/shard_map/ppermute | solution.py:533
  48.3 20.9 %collective-permute-start.10 = (bf16[2,192,768]{2,1,0:T(8,128)(2,1)}, bf16[2,192,768]{2,1,0:T(8,128)(2,1)}, u32[]{:S(2)}, u32[]{:S(2)}) collective-permute-start(bf16[2,192,768]{2,1,0:T(8,128)(2,1)} %pad_maximum_fusion.3.right), channel_id=1, source_target_pairs={{0,16},{4,20},{8,24},{12,28},{16,0},{20,4},{24,8},{28,12},{1,17},{... | collective-permute-start | bytes 1769480 | tf_op jit(solution)/shard_map/ppermute | solution.py:533
  49.6 18.6 %collective-permute-start.11 = (bf16[2,96,768]{2,1,0:T(8,128)(2,1)}, bf16[2,96,768]{2,1,0:T(8,128)(2,1)}, u32[]{:S(2)}, u32[]{:S(2)}) collective-permute-start(bf16[2,96,768]{2,1,0:T(8,128)(2,1)} %pad_maximum_fusion.9), channel_id=1, source_target_pairs={{0,24},{4,28},{8,16},{12,20},{16,8},{20,12},{24,0},{28,4},{1,25},{... | collective-permute-start | bytes 884744 | tf_op jit(solution)/shard_map/ppermute | solution.py:533
  73.8 12.6 %collective-permute-start.19 = (bf16[1,192,768]{2,1,0:T(8,128)(2,1)S(1)}, bf16[1,192,768]{2,1,0:T(8,128)(2,1)S(1)}, u32[]{:S(2)}, u32[]{:S(2)}) collective-permute-start(bf16[1,192,768]{2,1,0:T(8,128)(2,1)S(1)} %get-tuple-element.182.right), channel_id=1, source_target_pairs={{0,16},{4,20},{8,24},{12,28},{16,0},{20,4},{24,8},{28,12},{1,17},{... | collective-permute-start | bytes 884744 | tf_op jit(solution)/shard_map/ppermute | solution.py:533
  108.7 14.9 %collective-permute-start.27 = (bf16[4,96,768]{2,1,0:T(8,128)(2,1)S(1)}, bf16[4,96,768]{2,1,0:T(8,128)(2,1)S(1)}, u32[]{:S(2)}, u32[]{:S(2)}) collective-permute-start(bf16[4,96,768]{2,1,0:T(8,128)(2,1)S(1)} %get-tuple-element.194), channel_id=1, source_target_pairs={{0,8},{4,12},{8,0},{12,4},{16,24},{20,28},{24,16},{28,20},{1,9},{5... | collective-permute-start | bytes 1769480 | tf_op jit(solution)/shard_map/ppermute | solution.py:533
  109.0 14.7 %collective-permute-start.28 = (bf16[4,96,768]{2,1,0:T(8,128)(2,1)S(1)}, bf16[4,96,768]{2,1,0:T(8,128)(2,1)S(1)}, u32[]{:S(2)}, u32[]{:S(2)}) collective-permute-start(bf16[4,96,768]{2,1,0:T(8,128)(2,1)S(1)} %get-tuple-element.195), channel_id=1, source_target_pairs={{0,16},{4,20},{8,24},{12,28},{16,0},{20,4},{24,8},{28,12},{1,17},{... | collective-permute-start | bytes 1769480 | tf_op jit(solution)/shard_map/ppermute | solution.py:533
  124.7 16.0 %collective-permute-start.31 = (bf16[2,4,96,384]{3,2,1,0:T(8,128)(2,1)S(1)}, bf16[2,4,96,384]{3,2,1,0:T(8,128)(2,1)S(1)}, u32[]{:S(2)}, u32[]{:S(2)}) collective-permute-start(bf16[2,4,96,384]{3,2,1,0:T(8,128)(2,1)S(1)} %get-tuple-element.234), channel_id=1, source_target_pairs={{0,8},{4,12},{8,0},{12,4},{16,24},{20,28},{24,16},{28,20},{1,9},{5... | collective-permute-start | bytes 1769480 | tf_op jit(solution)/shard_map/ppermute | solution.py:533
  125.9 14.8 %collective-permute-start.32 = (bf16[2,4,96,384]{3,2,1,0:T(8,128)(2,1)S(1)}, bf16[2,4,96,384]{3,2,1,0:T(8,128)(2,1)S(1)}, u32[]{:S(2)}, u32[]{:S(2)}) collective-permute-start(bf16[2,4,96,384]{3,2,1,0:T(8,128)(2,1)S(1)} %get-tuple-element.235), channel_id=1, source_target_pairs={{0,16},{4,20},{8,24},{12,28},{16,0},{20,4},{24,8},{28,12},{1,17},{... | collective-permute-start | bytes 1769480 | tf_op jit(solution)/shard_map/ppermute | solution.py:533
  127.4 13.4 %collective-permute-start.35 = (bf16[96,768]{1,0:T(8,128)(2,1)S(1)}, bf16[96,768]{1,0:T(8,128)(2,1)S(1)}, u32[]{:S(2)}, u32[]{:S(2)}) collective-permute-start(bf16[96,768]{1,0:T(8,128)(2,1)S(1)} %get-tuple-element.328), channel_id=1, source_target_pairs={{0,1},{1,2},{2,3},{3,0},{4,5},{5,6},{6,7},{7,4},{8,9},{9,10},{10,1... | collective-permute-start | bytes 442376 | tf_op jit(solution)/shard_map/ppermute | solution.py:530
  127.9 12.9 %collective-permute-start.34 = (bf16[96,768]{1,0:T(8,128)(2,1)S(1)}, bf16[96,768]{1,0:T(8,128)(2,1)S(1)}, u32[]{:S(2)}, u32[]{:S(2)}) collective-permute-start(bf16[96,768]{1,0:T(8,128)(2,1)S(1)} %get-tuple-element.329), channel_id=1, source_target_pairs={{0,2},{1,3},{2,0},{3,1},{4,6},{5,7},{6,4},{7,5},{8,10},{9,11},{10,... | collective-permute-start | bytes 442376 | tf_op jit(solution)/shard_map/ppermute | solution.py:530
  146.9 12.4 %collective-permute-start.42 = (bf16[96,768]{1,0:T(8,128)(2,1)S(1)}, bf16[96,768]{1,0:T(8,128)(2,1)S(1)}, u32[]{:S(2)}, u32[]{:S(2)}) collective-permute-start(bf16[96,768]{1,0:T(8,128)(2,1)S(1)} %get-tuple-element.325), channel_id=1, source_target_pairs={{0,2},{1,3},{2,0},{3,1},{4,6},{5,7},{6,4},{7,5},{8,10},{9,11},{10,... | collective-permute-start | bytes 442376 | tf_op jit(solution)/shard_map/ppermute | solution.py:530
  148.1 13.6 %collective-permute-start.41 = (bf16[96,768]{1,0:T(8,128)(2,1)S(1)}, bf16[96,768]{1,0:T(8,128)(2,1)S(1)}, u32[]{:S(2)}, u32[]{:S(2)}) collective-permute-start(bf16[96,768]{1,0:T(8,128)(2,1)S(1)} %get-tuple-element.326), channel_id=1, source_target_pairs={{0,3},{1,0},{2,1},{3,2},{4,7},{5,4},{6,5},{7,6},{8,11},{9,8},{10,9... | collective-permute-start | bytes 442376 | tf_op jit(solution)/shard_map/ppermute | solution.py:530
  154.7 17.2 %collective-permute-start.39 = (bf16[2,4,104,384]{3,2,1,0:T(8,128)(2,1)S(1)}, bf16[2,4,104,384]{3,2,1,0:T(8,128)(2,1)S(1)}, u32[]{:S(2)}, u32[]{:S(2)}) collective-permute-start(bf16[2,4,104,384]{3,2,1,0:T(8,128)(2,1)S(1)} %get-tuple-element.243), channel_id=1, source_target_pairs={{0,8},{4,12},{8,0},{12,4},{16,24},{20,28},{24,16},{28,20},{1,9},{5... | collective-permute-start | bytes 1916936 | tf_op jit(solution)/shard_map/ppermute | solution.py:533
  155.3 16.6 %collective-permute-start.40 = (bf16[2,4,104,384]{3,2,1,0:T(8,128)(2,1)S(1)}, bf16[2,4,104,384]{3,2,1,0:T(8,128)(2,1)S(1)}, u32[]{:S(2)}, u32[]{:S(2)}) collective-permute-start(bf16[2,4,104,384]{3,2,1,0:T(8,128)(2,1)S(1)} %get-tuple-element.244), channel_id=1, source_target_pairs={{0,16},{4,20},{8,24},{12,28},{16,0},{20,4},{24,8},{28,12},{1,17},{... | collective-permute-start | bytes 1916936 | tf_op jit(solution)/shard_map/ppermute | solution.py:533
  183.5 14.3 %collective-permute-start.55 = (bf16[104,768]{1,0:T(8,128)(2,1)S(1)}, bf16[104,768]{1,0:T(8,128)(2,1)S(1)}, u32[]{:S(2)}, u32[]{:S(2)}) collective-permute-start(bf16[104,768]{1,0:T(8,128)(2,1)S(1)} %get-tuple-element.318), channel_id=1, source_target_pairs={{0,1},{1,2},{2,3},{3,0},{4,5},{5,6},{6,7},{7,4},{8,9},{9,10},{10,1... | collective-permute-start | bytes 479240 | tf_op jit(solution)/shard_map/ppermute | solution.py:530
  185.1 18.3 %collective-permute-start.54 = (bf16[104,768]{1,0:T(8,128)(2,1)S(1)}, bf16[104,768]{1,0:T(8,128)(2,1)S(1)}, u32[]{:S(2)}, u32[]{:S(2)}) collective-permute-start(bf16[104,768]{1,0:T(8,128)(2,1)S(1)} %get-tuple-element.320), channel_id=1, source_target_pairs={{0,2},{1,3},{2,0},{3,1},{4,6},{5,7},{6,4},{7,5},{8,10},{9,11},{10,... | collective-permute-start | bytes 479240 | tf_op jit(solution)/shard_map/ppermute | solution.py:530
  197.8 12.4 %collective-permute-start.62 = (bf16[4,96,768]{2,1,0:T(8,128)(2,1)S(1)}, bf16[4,96,768]{2,1,0:T(8,128)(2,1)S(1)}, u32[]{:S(2)}, u32[]{:S(2)}) collective-permute-start(bf16[4,96,768]{2,1,0:T(8,128)(2,1)S(1)} %pad_maximum_fusion.5.four), channel_id=1, source_target_pairs={{0,4},{4,0},{8,12},{12,8},{16,20},{20,16},{24,28},{28,24},{1,5},{5... | collective-permute-start | bytes 1769480 | tf_op jit(solution)/shard_map/ppermute | solution.py:533
  (65 other events, 603.7 us)

commit v7 on v6

--- a/solution.py
+++ b/solution.py
@@ -509,16 +509,23 @@
         out[pl.ds(at, rows), :] = (other if s % 2 else four)[s // 2].astype(f32)
 
 
-def finish_att(index_ref, four, other, gq, gk, gv, go, sums, whole):
+def finish_att(index_ref, four, other, gq, gk, gv, go, query_sum, value_sum, *rest):
+    sums, whole = rest[:-2], rest[-1]
+    lines = rest[-2]
     rows = four.shape[1] - EXTRA
     w = 2 * rows
     for s in range(GROUP):
         slot = (other if s % 2 else four)[s // 2].astype(f32)
         owner = index_ref[0] ^ s
         whole[pl.ds(pl.multiple_of(owner * rows, rows), rows), :] = slot[:rows]
-        sums[pl.ds(pl.multiple_of(owner * EXTRA, EXTRA), EXTRA), :] = slot[rows:]
+        lines[pl.ds(pl.multiple_of(owner * EXTRA, EXTRA), EXTRA), :] = slot[rows:]
     for m, out in enumerate((gq, gk, gv, go)):
         out[...] = whole[m * w : (m + 1) * w, :]
+    for j, out in enumerate(sums):
+        out[...] = lines[j * EXTRA, :]
+    last = len(sums) * EXTRA
+    query_sum[...] = lines[last, :w]
+    value_sum[...] = lines[last, w : 2 * w]
 
 
 def solution(mesh):
@@ -899,32 +906,34 @@
         att_four, grad_down, grad_up = tie(att_four, grad_down, grad_up)
         att_four = jnp.stack(att_four)
         att_other = swap(att_four, 1)
-        grad_query, grad_key, grad_value, grad_output, sums = call(
+        grad_query, grad_key, grad_value, grad_output, query_sum, value_sum, *sums = call(
             finish_att,
             "finish_att",
-            [shape((w, width), f32)] * 4 + [shape((GROUP * EXTRA, width), f32)],
+            [shape((w, width), f32)] * 4
+            + [shape((w,), f32)] * 2
+            + [shape((width,), f32)] * (GROUP - 1),
             [index, att_four, att_other],
             "svv",
-            [pltpu.VMEM((4 * w, width), f32)],
+            [pltpu.VMEM((GROUP * EXTRA, width), f32), pltpu.VMEM((4 * w, width), f32)],
         )
         return (
             output,
             grad_tokens,
             grad_query.T,
-            sums[(GROUP - 1) * EXTRA, :w],
+            query_sum,
             grad_key.T,
             grad_value.T,
-            sums[(GROUP - 1) * EXTRA, w : 2 * w],
+            value_sum,
             grad_output,
-            sums[EXTRA],
-            sums[2 * EXTRA],
-            sums[3 * EXTRA],
+            sums[1],
+            sums[2],
+            sums[3],
             grad_up,
             sums[0],
             grad_down,
-            sums[4 * EXTRA],
-            sums[5 * EXTRA],
-            sums[6 * EXTRA],
+            sums[4],
+            sums[5],
+            sums[6],
         )
 
     everywhere, rows, columns, units = P(), P(("dp", "mp"), None), P(None, "mp"), P("mp")

time: 224 us -> 223 us (level)
  no operation moved by 1% of the time
where the time goes in v7:
time: 223 us; the launch traced here: 222 us
  waiting for transfers between devices  71.4 us (32%)
  Pallas kernels  71 us (32%)
  starting transfers between devices  62.3 us (28%)
  local copies, waits for them, and re-layouts  9.81 us (4%)
  other arithmetic  6.13 us (3%)
    pallas_call x13, Pallas kernels, call(): pl.pallas_call(body, name=name, out_shape=tuple(outs), in_specs=[spec(k)...  71 us
    ppermute x18, waiting for transfers between devices, rotate(): lax.ppermute(array, 'mp', [(i, (i + step) % n_mp) for i in range(n_mp)])  47.1 us
    ppermute x47, starting transfers between devices, swap(): return lax.ppermute(array, 'dp', [(i, i ^ bits) for i in range(n_dp)])  43.1 us
    ppermute x47, waiting for transfers between devices, swap(): return lax.ppermute(array, 'dp', [(i, i ^ bits) for i in range(n_dp)])  24.2 us
    ppermute x18, starting transfers between devices, rotate(): lax.ppermute(array, 'mp', [(i, (i + step) % n_mp) for i in range(n_mp)])  19.2 us
    unnamed x50, local copies, waits for them, and re-layouts  5.19 us
  transfers between devices with their start and end apart: 65, of which 24 were waited for; matrix products, arithmetic and copies ran while one was open for 4% of the time, Pallas kernels for 24%

profile of v7, /device:TPU:9, one launch (start us, length us, event | category | flops | bytes accessed | tf_op | source)
XLA Modules:
  0.0 222.2 jit_solution(16022785128840865672)
XLA Ops:
  10.5 5.2 %collective-permute-done.1.bias_2.bias = bf16[104,768]{1,0:T(8,128)(2,1)S(1)} collective-permute-done((bf16[104,768]{1,0:T(8,128)(2,1)}, bf16[104,768]{1,0:T(8,128)(2,1)S(1)}, u32[]{:S(2)}, u32[]{:S(2)}) %collective-permute-start.1) | collective-permute-done | bytes 159776 | tf_op jit(solution)/shard_map/ppermute | solution.py:537
  15.7 3.5 %collective-permute-done.bias_1 = bf16[104,768]{1,0:T(8,128)(2,1)S(1)} collective-permute-done((bf16[104,768]{1,0:T(8,128)(2,1)}, bf16[104,768]{1,0:T(8,128)(2,1)S(1)}, u32[]{:S(2)}, u32[]{:S(2)}) %collective-permute-start) | collective-permute-done | bytes 159776 | tf_op jit(solution)/shard_map/ppermute | solution.py:537
  24.2 6.7 %collective-permute-done.7 = bf16[288,768]{1,0:T(8,128)(2,1)S(1)} collective-permute-done((bf16[288,768]{1,0:T(8,128)(2,1)}, bf16[288,768]{1,0:T(8,128)(2,1)S(1)}, u32[]{:S(2)}, u32[]{:S(2)}) %collective-permute-start.7) | collective-permute-done | bytes 442400 | tf_op jit(solution)/shard_map/ppermute | solution.py:537
  30.9 9.0 %collective-permute-done.6 = bf16[288,768]{1,0:T(8,128)(2,1)S(1)} collective-permute-done((bf16[288,768]{1,0:T(8,128)(2,1)}, bf16[288,768]{1,0:T(8,128)(2,1)S(1)}, u32[]{:S(2)}, u32[]{:S(2)}) %collective-permute-start.6) | collective-permute-done | bytes 442400 | tf_op jit(solution)/shard_map/ppermute | solution.py:537
  39.9 4.1 %collective-permute-done.4 = bf16[3,96,768]{2,1,0:T(8,128)(2,1)S(1)} collective-permute-done((bf16[3,96,768]{2,1,0:T(8,128)(2,1)S(1)}, bf16[3,96,768]{2,1,0:T(8,128)(2,1)S(1)}, u32[]{:S(2)}, u32[]{:S(2)}) %collective-permute-start.4) | collective-permute-done | bytes 442400 | tf_op jit(solution)/shard_map/ppermute | solution.py:540
  55.7 12.3 %att_forward.1 = (bf16[512,768]{1,0:T(8,128)(2,1)S(1)}, bf16[512,768]{1,0:T(8,128)(2,1)S(1)}, bf16[512,768]{1,0:T(8,128)(2,1)S(1)}, bf16[512,768]{1,0:T(8,128)(2...) custom-call(s32[1]{0:T(128)} %bitcast.index_ref, ...), custom_call_target="tpu_custom_call" | custom-call | bytes 243576 | tf_op jit(solution)/shard_map/att_forward/pallas_call | solution.py:62
  77.6 8.8 %ffn_first.1 = (bf16[512,2304]{1,0:T(8,128)(2,1)S(1)}, bf16[512,2304]{1,0:T(8,128)(2,1)S(1)}, bf16[768,512]{1,0:T(8,128)(2,1)S(1)}, f32[512,768]{1,0:T(8,128)S(1...) custom-call(s32[1]{0:T(128)} %bitcast.index_ref, f32[512,768]{1,0:T(8,128)S(1)} %get-tuple-element.176.normal, ...), custom_call_target="tpu_custom_call" | custom-call | bytes 373128 | tf_op jit(solution)/shard_map/ffn_first/pallas_call | solution.py:62
  90.5 9.3 %ffn_last.1 = (bf16[512,768]{1,0:T(8,128)(2,1)}, bf16[512,768]{1,0:T(8,128)(2,1)S(1)}, f32[512,768]{1,0:T(8,128)S(1)}, f32[8,768]{1,0:T(8,128)S(1)}, bf16[512,76...) custom-call(s32[1]{0:T(128)} %bitcast.index_ref, ...), custom_call_target="tpu_custom_call" | custom-call | bytes 314784 | tf_op jit(solution)/shard_map/ffn_last/pallas_call | solution.py:62
  100.2 3.5 %ffn_slopes.1 = (bf16[512,3072]{1,0:T(8,128)(2,1)S(1)}, f32[8,768]{1,0:T(8,128)S(1)}) custom-call(bf16[512,768]{1,0:T(8,128)(2,1)S(1)} %get-tuple-element.192.grad_mixed, bf16[512,2304]{1,0:T(8,128)(2,1)S(1)} %get-tuple-element.193.slope, bf16[512,768]{1,0:T(8,128)(2,1)S(1)} %get-tuple-element.194.slope_last, bf16[2304,768]{1,0:T(8,128)(2,1)S(1)} %get-tuple-element.195.down, ...), custom_call_target="tpu_custom_call" | custom-call | bytes 184704 | tf_op jit(solution)/shard_map/ffn_slopes/pallas_call | solution.py:62
  104.7 3.6 %ffn_grads.1 = (bf16[4,4,96,768]{3,2,1,0:T(8,128)(2,1)S(1)}, bf16[4,4,96,768]{3,2,1,0:T(8,128)(2,1)S(1)}) custom-call(s32[1]{0:T(128)} %bitcast.index_ref, bf16[512,3072]{1,0:T(8,128)(2,1)S(1)} %get-tuple-element.212.hidden, bf16[768,512]{1,0:T(8,128)(2,1)S(1)} %get-tuple-element.209.low_t), custom_call_target="tpu_custom_call" | custom-call | bytes 135168 | tf_op jit(solution)/shard_map/ffn_grads/pallas_call | solution.py:62
  110.1 3.9 %ffn_norm.1 = (f32[512,768]{1,0:T(8,128)S(1)}, bf16[512,768]{1,0:T(8,128)(2,1)S(1)}, f32[8,768]{1,0:T(8,128)S(1)}) custom-call(bf16[512,3072]{1,0:T(8,128)(2,1)S(1)} %get-tuple-element.212.hidden, f32[512,768]{1,0:T(8,128)S(1)} %get-tuple-element.213.grad_two, f32[512,768]{1,0:T(8,128)S(1)} %get-tuple-element.176.normal, ...), custom_call_target="tpu_custom_call" | custom-call | bytes 209336 | tf_op jit(solution)/shard_map/ffn_norm/pallas_call | solution.py:62
  114.3 9.4 %att_backward.2 = (bf16[512,384]{1,0:T(8,128)(2,1)S(1)}, bf16[512,384]{1,0:T(8,128)(2,1)S(1)}, bf16[512,384]{1,0:T(8,128)(2,1)S(1)}, bf16[4,2,104,768]{3,2,1,0:T(8,128)(2,1)S(1)}, bf16[4,2,104,768]{3,2,1,0:T(8,128)(2,1)S(1)}) custom-call(s32[1]{0:T(128)} %bitcast.index_ref, bf16[512,768]{1,0:T(8,128)(2,1)S(1)} %get-tuple-element.204.queries, ...), custom_call_target="tpu_custom_call" | custom-call | bytes 151744 | tf_op jit(solution)/shard_map/att_backward/pallas_call | solution.py:62
  127.9 3.1 %collective-permute-start.34 = (bf16[96,768]{1,0:T(8,128)(2,1)S(1)}, bf16[96,768]{1,0:T(8,128)(2,1)S(1)}, u32[]{:S(2)}, u32[]{:S(2)}) collective-permute-start(bf16[96,768]{1,0:T(8,128)(2,1)S(1)} %get-tuple-element.338), channel_id=1, source_target_pairs={{0,2},{1,3},{2,0},{3,1},{4,6},{5,7},{6,4},{7,5},{8,10},{9,11},{10,... | collective-permute-start | bytes 442376 | tf_op jit(solution)/shard_map/ppermute | solution.py:537
  131.1 9.6 %att_backward.3 = (bf16[512,384]{1,0:T(8,128)(2,1)S(1)}, bf16[512,384]{1,0:T(8,128)(2,1)S(1)}, bf16[512,384]{1,0:T(8,128)(2,1)S(1)}, bf16[4,2,104,768]{3,2,1,0:T(8,128)(2,1)S(1)}, bf16[4,2,104,768]{3,2,1,0:T(8,128)(2,1)S(1)}) custom-call(s32[1]{0:T(128)} %bitcast.index_ref, bf16[512,768]{1,0:T(8,128)(2,1)S(1)} %get-tuple-element.204.queries, ...), custom_call_target="tpu_custom_call" | custom-call | bytes 151744 | tf_op jit(solution)/shard_map/att_backward/pallas_call | solution.py:62
  149.5 4.1 %collective-permute-done.37 = bf16[4,96,384]{2,1,0:T(8,128)(2,1)S(1)} collective-permute-done((bf16[4,96,384]{2,1,0:T(8,128)(2,1)S(1)}, bf16[4,96,384]{2,1,0:T(8,128)(2,1)S(1)}, u32[]{:S(2)}, u32[]{:S(2)}) %collective-permute-start.37) | collective-permute-done | bytes 294944 | tf_op jit(solution)/shard_map/ppermute | solution.py:540
  156.4 2.9 %collective-permute-done.42 = bf16[96,768]{1,0:T(8,128)(2,1)S(1)} collective-permute-done((bf16[96,768]{1,0:T(8,128)(2,1)S(1)}, bf16[96,768]{1,0:T(8,128)(2,1)S(1)}, u32[]{:S(2)}, u32[]{:S(2)}) %collective-permute-start.42) | collective-permute-done | bytes 147488 | tf_op jit(solution)/shard_map/ppermute | solution.py:537
  162.6 9.2 %collective-permute-done.45 = bf16[96,768]{1,0:T(8,128)(2,1)S(1)} collective-permute-done((bf16[96,768]{1,0:T(8,128)(2,1)S(1)}, bf16[96,768]{1,0:T(8,128)(2,1)S(1)}, u32[]{:S(2)}, u32[]{:S(2)}) %collective-permute-start.45) | collective-permute-done | bytes 147488 | tf_op jit(solution)/shard_map/ppermute | solution.py:537
  173.8 3.5 %input_backward.1 = bf16[512,768]{1,0:T(8,128)(2,1)} custom-call(bf16[512,384]{1,0:T(8,128)(2,1)S(1)} %get-tuple-element.275.q0, bf16[512,384]{1,0:T(8,128)(2,1)S(1)} %get-tuple-element.276.k0, bf16[512,384]{1,0:T(8,128)(2,1)S(1)} %get-tuple-element.277.v0, bf16[512,384]{1,0:T(8,128)(2,1)S(1)} %get-tuple-element.278.q1, ...), custom_call_target="tpu_custom_call" | custom-call | bytes 129024 | tf_op jit(solution)/shard_map/input_backward/pallas_call | solution.py:62
  178.1 3.1 %collective-permute-done.47 = bf16[4,104,384]{2,1,0:T(8,128)(2,1)S(1)} collective-permute-done((bf16[4,104,384]{2,1,0:T(8,128)(2,1)S(1)}, bf16[4,104,384]{2,1,0:T(8,128)(2,1)S(1)}, u32[]{:S(2)}, u32[]{:S(2)}) %collective-permute-start.47) | collective-permute-done | bytes 319520 | tf_op jit(solution)/shard_map/ppermute | solution.py:540
  185.1 3.1 %collective-permute-start.54 = (bf16[104,768]{1,0:T(8,128)(2,1)S(1)}, bf16[104,768]{1,0:T(8,128)(2,1)S(1)}, u32[]{:S(2)}, u32[]{:S(2)}) collective-permute-start(bf16[104,768]{1,0:T(8,128)(2,1)S(1)} %get-tuple-element.329), channel_id=1, source_target_pairs={{0,2},{1,3},{2,0},{3,1},{4,6},{5,7},{6,4},{7,5},{8,10},{9,11},{10,... | collective-permute-start | bytes 479240 | tf_op jit(solution)/shard_map/ppermute | solution.py:537
  190.0 5.1 %collective-permute-done.49 = bf16[104,768]{1,0:T(8,128)(2,1)S(1)} collective-permute-done((bf16[104,768]{1,0:T(8,128)(2,1)S(1)}, bf16[104,768]{1,0:T(8,128)(2,1)S(1)}, u32[]{:S(2)}, u32[]{:S(2)}) %collective-permute-start.49) | collective-permute-done | bytes 159776 | tf_op jit(solution)/shard_map/ppermute | solution.py:537
  197.8 5.5 %collective-permute-start.62 = (bf16[4,96,768]{2,1,0:T(8,128)(2,1)S(1)}, bf16[4,96,768]{2,1,0:T(8,128)(2,1)S(1)}, u32[]{:S(2)}, u32[]{:S(2)}) collective-permute-start(bf16[4,96,768]{2,1,0:T(8,128)(2,1)S(1)} %pad_maximum_fusion.5.four), channel_id=1, source_target_pairs={{0,4},{4,0},{8,12},{12,8},{16,20},{20,16},{24,28},{28,24},{1,5},{5... | collective-permute-start | bytes 1769480 | tf_op jit(solution)/shard_map/ppermute | solution.py:540
  203.4 4.0 %collective-permute-start.63 = (bf16[4,96,768]{2,1,0:T(8,128)(2,1)S(1)}, bf16[4,96,768]{2,1,0:T(8,128)(2,1)S(1)}, u32[]{:S(2)}, u32[]{:S(2)}) collective-permute-start(bf16[4,96,768]{2,1,0:T(8,128)(2,1)S(1)} %pad_maximum_fusion.6.four), channel_id=1, source_target_pairs={{0,4},{4,0},{8,12},{12,8},{16,20},{20,16},{24,28},{28,24},{1,5},{5... | collective-permute-start | bytes 1769480 | tf_op jit(solution)/shard_map/ppermute | solution.py:540
  214.3 3.7 %collective-permute-done.60 = bf16[104,768]{1,0:T(8,128)(2,1)S(1)} collective-permute-done((bf16[104,768]{1,0:T(8,128)(2,1)S(1)}, bf16[104,768]{1,0:T(8,128)(2,1)S(1)}, u32[]{:S(2)}, u32[]{:S(2)}) %collective-permute-start.60) | collective-permute-done | bytes 159776 | tf_op jit(solution)/shard_map/ppermute | solution.py:540
  (217 shorter events, 84.4 us)
Async XLA Ops:
  3.1 12.6 %collective-permute-start.1 = (bf16[104,768]{1,0:T(8,128)(2,1)}, bf16[104,768]{1,0:T(8,128)(2,1)S(1)}, u32[]{:S(2)}, u32[]{:S(2)}) collective-permute-start(bf16[104,768]{1,0:T(8,128)(2,1)} %get-tuple-element.166.bias_0), channel_id=1, source_target_pairs={{0,2},{1,3},{2,0},{3,1},{4,6},{5,7},{6,4},{7,5},{8,10},{9,11},{10,... | collective-permute-start | bytes 479240 | tf_op jit(solution)/shard_map/ppermute | solution.py:537
  5.6 13.7 %collective-permute-start = (bf16[104,768]{1,0:T(8,128)(2,1)}, bf16[104,768]{1,0:T(8,128)(2,1)S(1)}, u32[]{:S(2)}, u32[]{:S(2)}) collective-permute-start(bf16[104,768]{1,0:T(8,128)(2,1)} %get-tuple-element.166.bias_0), channel_id=1, source_target_pairs={{0,1},{1,2},{2,3},{3,0},{4,5},{5,6},{6,7},{7,4},{8,9},{9,10},{10,1... | collective-permute-start | bytes 479240 | tf_op jit(solution)/shard_map/ppermute | solution.py:537
  20.5 19.4 %collective-permute-start.6 = (bf16[288,768]{1,0:T(8,128)(2,1)}, bf16[288,768]{1,0:T(8,128)(2,1)S(1)}, u32[]{:S(2)}, u32[]{:S(2)}) collective-permute-start(bf16[288,768]{1,0:T(8,128)(2,1)} %pad_maximum_fusion.7), channel_id=1, source_target_pairs={{0,1},{1,2},{2,3},{3,0},{4,5},{5,6},{6,7},{7,4},{8,9},{9,10},{10,1... | collective-permute-start | bytes 1327112 | tf_op jit(solution)/shard_map/ppermute | solution.py:537
  21.5 18.3 %collective-permute-start.5 = (bf16[3,96,768]{2,1,0:T(8,128)(2,1)S(1)}, bf16[3,96,768]{2,1,0:T(8,128)(2,1)S(1)}, u32[]{:S(2)}, u32[]{:S(2)}) collective-permute-start(bf16[3,96,768]{2,1,0:T(8,128)(2,1)S(1)} %pad_maximum_fusion.8), channel_id=1, source_target_pairs={{0,24},{4,28},{8,16},{12,20},{16,8},{20,12},{24,0},{28,4},{1,25},{... | collective-permute-start | bytes 1327112 | tf_op jit(solution)/shard_map/ppermute | solution.py:540
  23.7 20.3 %collective-permute-start.4 = (bf16[3,96,768]{2,1,0:T(8,128)(2,1)S(1)}, bf16[3,96,768]{2,1,0:T(8,128)(2,1)S(1)}, u32[]{:S(2)}, u32[]{:S(2)}) collective-permute-start(bf16[3,96,768]{2,1,0:T(8,128)(2,1)S(1)} %pad_maximum_fusion.8), channel_id=1, source_target_pairs={{0,16},{4,20},{8,24},{12,28},{16,0},{20,4},{24,8},{28,12},{1,17},{... | collective-permute-start | bytes 1327112 | tf_op jit(solution)/shard_map/ppermute | solution.py:540
  23.9 20.1 %collective-permute-start.3 = (bf16[3,96,768]{2,1,0:T(8,128)(2,1)S(1)}, bf16[3,96,768]{2,1,0:T(8,128)(2,1)S(1)}, u32[]{:S(2)}, u32[]{:S(2)}) collective-permute-start(bf16[3,96,768]{2,1,0:T(8,128)(2,1)S(1)} %pad_maximum_fusion.8), channel_id=1, source_target_pairs={{0,8},{4,12},{8,0},{12,4},{16,24},{20,28},{24,16},{28,20},{1,9},{5... | collective-permute-start | bytes 1327112 | tf_op jit(solution)/shard_map/ppermute | solution.py:540
  44.9 23.2 %collective-permute-start.12 = (bf16[288,768]{1,0:T(8,128)(2,1)}, bf16[288,768]{1,0:T(8,128)(2,1)}, u32[]{:S(2)}, u32[]{:S(2)}) collective-permute-start(bf16[288,768]{1,0:T(8,128)(2,1)} %pad_maximum_fusion.7), channel_id=1, source_target_pairs={{0,2},{1,3},{2,0},{3,1},{4,6},{5,7},{6,4},{7,5},{8,10},{9,11},{10,... | collective-permute-start | bytes 1327112 | tf_op jit(solution)/shard_map/ppermute | solution.py:537
  46.2 22.0 %collective-permute-start.9 = (bf16[2,192,768]{2,1,0:T(8,128)(2,1)S(1)}, bf16[2,192,768]{2,1,0:T(8,128)(2,1)}, u32[]{:S(2)}, u32[]{:S(2)}) collective-permute-start(bf16[2,192,768]{2,1,0:T(8,128)(2,1)S(1)} %pad_maximum_fusion.2.left), channel_id=1, source_target_pairs={{0,8},{4,12},{8,0},{12,4},{16,24},{20,28},{24,16},{28,20},{1,9},{5... | collective-permute-start | bytes 1769480 | tf_op jit(solution)/shard_map/ppermute | solution.py:540
  48.3 20.9 %collective-permute-start.10 = (bf16[2,192,768]{2,1,0:T(8,128)(2,1)}, bf16[2,192,768]{2,1,0:T(8,128)(2,1)}, u32[]{:S(2)}, u32[]{:S(2)}) collective-permute-start(bf16[2,192,768]{2,1,0:T(8,128)(2,1)} %pad_maximum_fusion.3.right), channel_id=1, source_target_pairs={{0,16},{4,20},{8,24},{12,28},{16,0},{20,4},{24,8},{28,12},{1,17},{... | collective-permute-start | bytes 1769480 | tf_op jit(solution)/shard_map/ppermute | solution.py:540
  49.6 18.6 %collective-permute-start.11 = (bf16[2,96,768]{2,1,0:T(8,128)(2,1)}, bf16[2,96,768]{2,1,0:T(8,128)(2,1)}, u32[]{:S(2)}, u32[]{:S(2)}) collective-permute-start(bf16[2,96,768]{2,1,0:T(8,128)(2,1)} %pad_maximum_fusion.9), channel_id=1, source_target_pairs={{0,24},{4,28},{8,16},{12,20},{16,8},{20,12},{24,0},{28,4},{1,25},{... | collective-permute-start | bytes 884744 | tf_op jit(solution)/shard_map/ppermute | solution.py:540
  73.8 12.6 %collective-permute-start.19 = (bf16[1,192,768]{2,1,0:T(8,128)(2,1)S(1)}, bf16[1,192,768]{2,1,0:T(8,128)(2,1)S(1)}, u32[]{:S(2)}, u32[]{:S(2)}) collective-permute-start(bf16[1,192,768]{2,1,0:T(8,128)(2,1)S(1)} %get-tuple-element.190.right), channel_id=1, source_target_pairs={{0,16},{4,20},{8,24},{12,28},{16,0},{20,4},{24,8},{28,12},{1,17},{... | collective-permute-start | bytes 884744 | tf_op jit(solution)/shard_map/ppermute | solution.py:540
  108.7 14.9 %collective-permute-start.27 = (bf16[4,96,768]{2,1,0:T(8,128)(2,1)S(1)}, bf16[4,96,768]{2,1,0:T(8,128)(2,1)S(1)}, u32[]{:S(2)}, u32[]{:S(2)}) collective-permute-start(bf16[4,96,768]{2,1,0:T(8,128)(2,1)S(1)} %get-tuple-element.202), channel_id=1, source_target_pairs={{0,8},{4,12},{8,0},{12,4},{16,24},{20,28},{24,16},{28,20},{1,9},{5... | collective-permute-start | bytes 1769480 | tf_op jit(solution)/shard_map/ppermute | solution.py:540
  109.0 14.7 %collective-permute-start.28 = (bf16[4,96,768]{2,1,0:T(8,128)(2,1)S(1)}, bf16[4,96,768]{2,1,0:T(8,128)(2,1)S(1)}, u32[]{:S(2)}, u32[]{:S(2)}) collective-permute-start(bf16[4,96,768]{2,1,0:T(8,128)(2,1)S(1)} %get-tuple-element.203), channel_id=1, source_target_pairs={{0,16},{4,20},{8,24},{12,28},{16,0},{20,4},{24,8},{28,12},{1,17},{... | collective-permute-start | bytes 1769480 | tf_op jit(solution)/shard_map/ppermute | solution.py:540
  124.7 16.0 %collective-permute-start.31 = (bf16[2,4,96,384]{3,2,1,0:T(8,128)(2,1)S(1)}, bf16[2,4,96,384]{3,2,1,0:T(8,128)(2,1)S(1)}, u32[]{:S(2)}, u32[]{:S(2)}) collective-permute-start(bf16[2,4,96,384]{3,2,1,0:T(8,128)(2,1)S(1)} %get-tuple-element.242), channel_id=1, source_target_pairs={{0,8},{4,12},{8,0},{12,4},{16,24},{20,28},{24,16},{28,20},{1,9},{5... | collective-permute-start | bytes 1769480 | tf_op jit(solution)/shard_map/ppermute | solution.py:540
  125.9 14.8 %collective-permute-start.32 = (bf16[2,4,96,384]{3,2,1,0:T(8,128)(2,1)S(1)}, bf16[2,4,96,384]{3,2,1,0:T(8,128)(2,1)S(1)}, u32[]{:S(2)}, u32[]{:S(2)}) collective-permute-start(bf16[2,4,96,384]{3,2,1,0:T(8,128)(2,1)S(1)} %get-tuple-element.243), channel_id=1, source_target_pairs={{0,16},{4,20},{8,24},{12,28},{16,0},{20,4},{24,8},{28,12},{1,17},{... | collective-permute-start | bytes 1769480 | tf_op jit(solution)/shard_map/ppermute | solution.py:540
  127.4 13.4 %collective-permute-start.35 = (bf16[96,768]{1,0:T(8,128)(2,1)S(1)}, bf16[96,768]{1,0:T(8,128)(2,1)S(1)}, u32[]{:S(2)}, u32[]{:S(2)}) collective-permute-start(bf16[96,768]{1,0:T(8,128)(2,1)S(1)} %get-tuple-element.337), channel_id=1, source_target_pairs={{0,1},{1,2},{2,3},{3,0},{4,5},{5,6},{6,7},{7,4},{8,9},{9,10},{10,1... | collective-permute-start | bytes 442376 | tf_op jit(solution)/shard_map/ppermute | solution.py:537
  127.9 12.9 %collective-permute-start.34 = (bf16[96,768]{1,0:T(8,128)(2,1)S(1)}, bf16[96,768]{1,0:T(8,128)(2,1)S(1)}, u32[]{:S(2)}, u32[]{:S(2)}) collective-permute-start(bf16[96,768]{1,0:T(8,128)(2,1)S(1)} %get-tuple-element.338), channel_id=1, source_target_pairs={{0,2},{1,3},{2,0},{3,1},{4,6},{5,7},{6,4},{7,5},{8,10},{9,11},{10,... | collective-permute-start | bytes 442376 | tf_op jit(solution)/shard_map/ppermute | solution.py:537
  146.9 12.4 %collective-permute-start.42 = (bf16[96,768]{1,0:T(8,128)(2,1)S(1)}, bf16[96,768]{1,0:T(8,128)(2,1)S(1)}, u32[]{:S(2)}, u32[]{:S(2)}) collective-permute-start(bf16[96,768]{1,0:T(8,128)(2,1)S(1)} %get-tuple-element.334), channel_id=1, source_target_pairs={{0,2},{1,3},{2,0},{3,1},{4,6},{5,7},{6,4},{7,5},{8,10},{9,11},{10,... | collective-permute-start | bytes 442376 | tf_op jit(solution)/shard_map/ppermute | solution.py:537
  148.1 13.6 %collective-permute-start.41 = (bf16[96,768]{1,0:T(8,128)(2,1)S(1)}, bf16[96,768]{1,0:T(8,128)(2,1)S(1)}, u32[]{:S(2)}, u32[]{:S(2)}) collective-permute-start(bf16[96,768]{1,0:T(8,128)(2,1)S(1)} %get-tuple-element.335), channel_id=1, source_target_pairs={{0,3},{1,0},{2,1},{3,2},{4,7},{5,4},{6,5},{7,6},{8,11},{9,8},{10,9... | collective-permute-start | bytes 442376 | tf_op jit(solution)/shard_map/ppermute | solution.py:537
  154.7 17.2 %collective-permute-start.39 = (bf16[2,4,104,384]{3,2,1,0:T(8,128)(2,1)S(1)}, bf16[2,4,104,384]{3,2,1,0:T(8,128)(2,1)S(1)}, u32[]{:S(2)}, u32[]{:S(2)}) collective-permute-start(bf16[2,4,104,384]{3,2,1,0:T(8,128)(2,1)S(1)} %get-tuple-element.251), channel_id=1, source_target_pairs={{0,8},{4,12},{8,0},{12,4},{16,24},{20,28},{24,16},{28,20},{1,9},{5... | collective-permute-start | bytes 1916936 | tf_op jit(solution)/shard_map/ppermute | solution.py:540
  155.3 16.6 %collective-permute-start.40 = (bf16[2,4,104,384]{3,2,1,0:T(8,128)(2,1)S(1)}, bf16[2,4,104,384]{3,2,1,0:T(8,128)(2,1)S(1)}, u32[]{:S(2)}, u32[]{:S(2)}) collective-permute-start(bf16[2,4,104,384]{3,2,1,0:T(8,128)(2,1)S(1)} %get-tuple-element.252), channel_id=1, source_target_pairs={{0,16},{4,20},{8,24},{12,28},{16,0},{20,4},{24,8},{28,12},{1,17},{... | collective-permute-start | bytes 1916936 | tf_op jit(solution)/shard_map/ppermute | solution.py:540
  183.5 14.3 %collective-permute-start.55 = (bf16[104,768]{1,0:T(8,128)(2,1)S(1)}, bf16[104,768]{1,0:T(8,128)(2,1)S(1)}, u32[]{:S(2)}, u32[]{:S(2)}) collective-permute-start(bf16[104,768]{1,0:T(8,128)(2,1)S(1)} %get-tuple-element.327), channel_id=1, source_target_pairs={{0,1},{1,2},{2,3},{3,0},{4,5},{5,6},{6,7},{7,4},{8,9},{9,10},{10,1... | collective-permute-start | bytes 479240 | tf_op jit(solution)/shard_map/ppermute | solution.py:537
  185.1 18.3 %collective-permute-start.54 = (bf16[104,768]{1,0:T(8,128)(2,1)S(1)}, bf16[104,768]{1,0:T(8,128)(2,1)S(1)}, u32[]{:S(2)}, u32[]{:S(2)}) collective-permute-start(bf16[104,768]{1,0:T(8,128)(2,1)S(1)} %get-tuple-element.329), channel_id=1, source_target_pairs={{0,2},{1,3},{2,0},{3,1},{4,6},{5,7},{6,4},{7,5},{8,10},{9,11},{10,... | collective-permute-start | bytes 479240 | tf_op jit(solution)/shard_map/ppermute | solution.py:537
  197.8 12.4 %collective-permute-start.62 = (bf16[4,96,768]{2,1,0:T(8,128)(2,1)S(1)}, bf16[4,96,768]{2,1,0:T(8,128)(2,1)S(1)}, u32[]{:S(2)}, u32[]{:S(2)}) collective-permute-start(bf16[4,96,768]{2,1,0:T(8,128)(2,1)S(1)} %pad_maximum_fusion.5.four), channel_id=1, source_target_pairs={{0,4},{4,0},{8,12},{12,8},{16,20},{20,16},{24,28},{28,24},{1,5},{5... | collective-permute-start | bytes 1769480 | tf_op jit(solution)/shard_map/ppermute | solution.py:540
  (65 other events, 602.5 us)

commit v8 on v7

--- a/solution.py
+++ b/solution.py
@@ -386,7 +386,8 @@
         mine = columns_of(r, units)
         quarter(r, down[mine, :], slope[:, mine])
 
-    each(down.shape[0] // units, inner)
+    for r in range(down.shape[0] // units):
+        inner(r)
     quarter(down.shape[0] // units, down_last[...], slope_last[...])
 
 
@@ -863,9 +864,7 @@
         )
         left_now, right_now = add(stay_left, come_left), add(stay_right, come_right)
         come_left, come_right = swap(left_now[1], 4), swap(right_now[1], 2)
-        up_line[3:], come_left, come_right, down_x, down_y = tie(
-            up_line[3:], come_left, come_right, down_x, down_y
-        )
+        come_left, come_right, down_x, down_y = tie(come_left, come_right, down_x, down_y)
         come_x, come_y = swap(down_x, 4), swap(down_y, 2)
         att_parts = jnp.concatenate(
             [add(left_now[0], come_left), add(right_now[0], come_right)], axis=-1

time: 223 us -> 223 us (level)
    ppermute x47, waiting for transfers between devices: 24.2 us -> 26.6 us  [swap(): return lax.ppermute(array, 'dp', [(i, i ^ bits) for i in range(n_dp)])]
  transfers between devices with their start and end apart: 65 -> 65, of which waited for: 24 -> 25; matrix products, arithmetic and copies ran while one was open for 4% -> 4% of each run, Pallas kernels for 24% -> 24%
where the time goes in v8:
time: 223 us; the launch traced here: 222 us
  waiting for transfers between devices  72.4 us (32%)
  Pallas kernels  70.1 us (31%)
  starting transfers between devices  62.1 us (28%)
  local copies, waits for them, and re-layouts  9.81 us (4%)
  other arithmetic  6.13 us (3%)
    pallas_call x13, Pallas kernels, call(): pl.pallas_call(body, name=name, out_shape=tuple(outs), in_specs=[spec(k)...  70.1 us
    ppermute x18, waiting for transfers between devices, rotate(): lax.ppermute(array, 'mp', [(i, (i + step) % n_mp) for i in range(n_mp)])  45.8 us
    ppermute x47, starting transfers between devices, swap(): return lax.ppermute(array, 'dp', [(i, i ^ bits) for i in range(n_dp)])  42.9 us
    ppermute x47, waiting for transfers between devices, swap(): return lax.ppermute(array, 'dp', [(i, i ^ bits) for i in range(n_dp)])  26.6 us
    ppermute x18, starting transfers between devices, rotate(): lax.ppermute(array, 'mp', [(i, (i + step) % n_mp) for i in range(n_mp)])  19.2 us
    unnamed x50, local copies, waits for them, and re-layouts  5.19 us
  transfers between devices with their start and end apart: 65, of which 25 were waited for; matrix products, arithmetic and copies ran while one was open for 4% of the time, Pallas kernels for 24%

profile of v8, /device:TPU:9, one launch (start us, length us, event | category | flops | bytes accessed | tf_op | source)
XLA Modules:
  0.0 222.2 jit_solution(13517133022118131951)
XLA Ops:
  10.5 5.2 %collective-permute-done.1.bias_2.bias = bf16[104,768]{1,0:T(8,128)(2,1)S(1)} collective-permute-done((bf16[104,768]{1,0:T(8,128)(2,1)}, bf16[104,768]{1,0:T(8,128)(2,1)S(1)}, u32[]{:S(2)}, u32[]{:S(2)}) %collective-permute-start.1) | collective-permute-done | bytes 159776 | tf_op jit(solution)/shard_map/ppermute | solution.py:538
  15.7 3.5 %collective-permute-done.bias_1 = bf16[104,768]{1,0:T(8,128)(2,1)S(1)} collective-permute-done((bf16[104,768]{1,0:T(8,128)(2,1)}, bf16[104,768]{1,0:T(8,128)(2,1)S(1)}, u32[]{:S(2)}, u32[]{:S(2)}) %collective-permute-start) | collective-permute-done | bytes 159776 | tf_op jit(solution)/shard_map/ppermute | solution.py:538
  24.2 6.7 %collective-permute-done.7 = bf16[288,768]{1,0:T(8,128)(2,1)S(1)} collective-permute-done((bf16[288,768]{1,0:T(8,128)(2,1)}, bf16[288,768]{1,0:T(8,128)(2,1)S(1)}, u32[]{:S(2)}, u32[]{:S(2)}) %collective-permute-start.7) | collective-permute-done | bytes 442400 | tf_op jit(solution)/shard_map/ppermute | solution.py:538
  30.9 9.0 %collective-permute-done.6 = bf16[288,768]{1,0:T(8,128)(2,1)S(1)} collective-permute-done((bf16[288,768]{1,0:T(8,128)(2,1)}, bf16[288,768]{1,0:T(8,128)(2,1)S(1)}, u32[]{:S(2)}, u32[]{:S(2)}) %collective-permute-start.6) | collective-permute-done | bytes 442400 | tf_op jit(solution)/shard_map/ppermute | solution.py:538
  39.9 4.1 %collective-permute-done.4 = bf16[3,96,768]{2,1,0:T(8,128)(2,1)S(1)} collective-permute-done((bf16[3,96,768]{2,1,0:T(8,128)(2,1)S(1)}, bf16[3,96,768]{2,1,0:T(8,128)(2,1)S(1)}, u32[]{:S(2)}, u32[]{:S(2)}) %collective-permute-start.4) | collective-permute-done | bytes 442400 | tf_op jit(solution)/shard_map/ppermute | solution.py:541
  55.7 12.3 %att_forward.1 = (bf16[512,768]{1,0:T(8,128)(2,1)S(1)}, bf16[512,768]{1,0:T(8,128)(2,1)S(1)}, bf16[512,768]{1,0:T(8,128)(2,1)S(1)}, bf16[512,768]{1,0:T(8,128)(2...) custom-call(s32[1]{0:T(128)} %bitcast.index_ref, ...), custom_call_target="tpu_custom_call" | custom-call | bytes 243576 | tf_op jit(solution)/shard_map/att_forward/pallas_call | solution.py:62
  77.6 8.8 %ffn_first.1 = (bf16[512,2304]{1,0:T(8,128)(2,1)S(1)}, bf16[512,2304]{1,0:T(8,128)(2,1)S(1)}, bf16[768,512]{1,0:T(8,128)(2,1)S(1)}, f32[512,768]{1,0:T(8,128)S(1...) custom-call(s32[1]{0:T(128)} %bitcast.index_ref, f32[512,768]{1,0:T(8,128)S(1)} %get-tuple-element.175.normal, ...), custom_call_target="tpu_custom_call" | custom-call | bytes 373128 | tf_op jit(solution)/shard_map/ffn_first/pallas_call | solution.py:62
  90.5 9.3 %ffn_last.1 = (bf16[512,768]{1,0:T(8,128)(2,1)}, bf16[512,768]{1,0:T(8,128)(2,1)S(1)}, f32[512,768]{1,0:T(8,128)S(1)}, f32[8,768]{1,0:T(8,128)S(1)}, bf16[512,76...) custom-call(s32[1]{0:T(128)} %bitcast.index_ref, ...), custom_call_target="tpu_custom_call" | custom-call | bytes 314784 | tf_op jit(solution)/shard_map/ffn_last/pallas_call | solution.py:62
  100.2 2.8 %ffn_slopes.1 = (bf16[512,3072]{1,0:T(8,128)(2,1)S(1)}, f32[8,768]{1,0:T(8,128)S(1)}) custom-call(bf16[512,768]{1,0:T(8,128)(2,1)S(1)} %get-tuple-element.191.grad_mixed, bf16[512,2304]{1,0:T(8,128)(2,1)S(1)} %get-tuple-element.192.slope, bf16[512,768]{1,0:T(8,128)(2,1)S(1)} %get-tuple-element.193.slope_last, bf16[2304,768]{1,0:T(8,128)(2,1)S(1)} %get-tuple-element.194.down, ...), custom_call_target="tpu_custom_call" | custom-call | bytes 184704 | tf_op jit(solution)/shard_map/ffn_slopes/pallas_call | solution.py:62
  104.7 3.6 %ffn_grads.1 = (bf16[4,4,96,768]{3,2,1,0:T(8,128)(2,1)S(1)}, bf16[4,4,96,768]{3,2,1,0:T(8,128)(2,1)S(1)}) custom-call(s32[1]{0:T(128)} %bitcast.index_ref, bf16[512,3072]{1,0:T(8,128)(2,1)S(1)} %get-tuple-element.211.hidden, bf16[768,512]{1,0:T(8,128)(2,1)S(1)} %get-tuple-element.208.low_t), custom_call_target="tpu_custom_call" | custom-call | bytes 135168 | tf_op jit(solution)/shard_map/ffn_grads/pallas_call | solution.py:62
  110.1 3.9 %ffn_norm.1 = (f32[512,768]{1,0:T(8,128)S(1)}, bf16[512,768]{1,0:T(8,128)(2,1)S(1)}, f32[8,768]{1,0:T(8,128)S(1)}) custom-call(bf16[512,3072]{1,0:T(8,128)(2,1)S(1)} %get-tuple-element.211.hidden, f32[512,768]{1,0:T(8,128)S(1)} %get-tuple-element.212.grad_two, f32[512,768]{1,0:T(8,128)S(1)} %get-tuple-element.175.normal, ...), custom_call_target="tpu_custom_call" | custom-call | bytes 209336 | tf_op jit(solution)/shard_map/ffn_norm/pallas_call | solution.py:62
  114.3 9.4 %att_backward.2 = (bf16[512,384]{1,0:T(8,128)(2,1)S(1)}, bf16[512,384]{1,0:T(8,128)(2,1)S(1)}, bf16[512,384]{1,0:T(8,128)(2,1)S(1)}, bf16[4,2,104,768]{3,2,1,0:T(8,128)(2,1)S(1)}, bf16[4,2,104,768]{3,2,1,0:T(8,128)(2,1)S(1)}) custom-call(s32[1]{0:T(128)} %bitcast.index_ref, bf16[512,768]{1,0:T(8,128)(2,1)S(1)} %get-tuple-element.203.queries, ...), custom_call_target="tpu_custom_call" | custom-call | bytes 151744 | tf_op jit(solution)/shard_map/att_backward/pallas_call | solution.py:62
  127.9 3.1 %collective-permute-start.34 = (bf16[96,768]{1,0:T(8,128)(2,1)S(1)}, bf16[96,768]{1,0:T(8,128)(2,1)S(1)}, u32[]{:S(2)}, u32[]{:S(2)}) collective-permute-start(bf16[96,768]{1,0:T(8,128)(2,1)S(1)} %get-tuple-element.336), channel_id=1, source_target_pairs={{0,2},{1,3},{2,0},{3,1},{4,6},{5,7},{6,4},{7,5},{8,10},{9,11},{10,... | collective-permute-start | bytes 442376 | tf_op jit(solution)/shard_map/ppermute | solution.py:538
  131.1 9.3 %att_backward.3 = (bf16[512,384]{1,0:T(8,128)(2,1)S(1)}, bf16[512,384]{1,0:T(8,128)(2,1)S(1)}, bf16[512,384]{1,0:T(8,128)(2,1)S(1)}, bf16[4,2,104,768]{3,2,1,0:T(8,128)(2,1)S(1)}, bf16[4,2,104,768]{3,2,1,0:T(8,128)(2,1)S(1)}) custom-call(s32[1]{0:T(128)} %bitcast.index_ref, bf16[512,768]{1,0:T(8,128)(2,1)S(1)} %get-tuple-element.203.queries, ...), custom_call_target="tpu_custom_call" | custom-call | bytes 151744 | tf_op jit(solution)/shard_map/att_backward/pallas_call | solution.py:62
  149.5 4.1 %collective-permute-done.37 = bf16[4,96,384]{2,1,0:T(8,128)(2,1)S(1)} collective-permute-done((bf16[4,96,384]{2,1,0:T(8,128)(2,1)S(1)}, bf16[4,96,384]{2,1,0:T(8,128)(2,1)S(1)}, u32[]{:S(2)}, u32[]{:S(2)}) %collective-permute-start.37) | collective-permute-done | bytes 294944 | tf_op jit(solution)/shard_map/ppermute | solution.py:541
  156.4 2.9 %collective-permute-done.42 = bf16[96,768]{1,0:T(8,128)(2,1)S(1)} collective-permute-done((bf16[96,768]{1,0:T(8,128)(2,1)S(1)}, bf16[96,768]{1,0:T(8,128)(2,1)S(1)}, u32[]{:S(2)}, u32[]{:S(2)}) %collective-permute-start.42) | collective-permute-done | bytes 147488 | tf_op jit(solution)/shard_map/ppermute | solution.py:538
  162.6 9.2 %collective-permute-done.45 = bf16[96,768]{1,0:T(8,128)(2,1)S(1)} collective-permute-done((bf16[96,768]{1,0:T(8,128)(2,1)S(1)}, bf16[96,768]{1,0:T(8,128)(2,1)S(1)}, u32[]{:S(2)}, u32[]{:S(2)}) %collective-permute-start.45) | collective-permute-done | bytes 147488 | tf_op jit(solution)/shard_map/ppermute | solution.py:538
  173.8 3.5 %input_backward.1 = bf16[512,768]{1,0:T(8,128)(2,1)} custom-call(bf16[512,384]{1,0:T(8,128)(2,1)S(1)} %get-tuple-element.273.q0, bf16[512,384]{1,0:T(8,128)(2,1)S(1)} %get-tuple-element.274.k0, bf16[512,384]{1,0:T(8,128)(2,1)S(1)} %get-tuple-element.275.v0, bf16[512,384]{1,0:T(8,128)(2,1)S(1)} %get-tuple-element.276.q1, ...), custom_call_target="tpu_custom_call" | custom-call | bytes 129024 | tf_op jit(solution)/shard_map/input_backward/pallas_call | solution.py:62
  177.3 3.8 %collective-permute-done.46 = bf16[4,104,384]{2,1,0:T(8,128)(2,1)S(1)} collective-permute-done((bf16[4,104,384]{2,1,0:T(8,128)(2,1)S(1)}, bf16[4,104,384]{2,1,0:T(8,128)(2,1)S(1)}, u32[]{:S(2)}, u32[]{:S(2)}) %collective-permute-start.46) | collective-permute-done | bytes 319520 | tf_op jit(solution)/shard_map/ppermute | solution.py:541
  185.9 3.1 %collective-permute-start.54 = (bf16[104,768]{1,0:T(8,128)(2,1)S(1)}, bf16[104,768]{1,0:T(8,128)(2,1)S(1)}, u32[]{:S(2)}, u32[]{:S(2)}) collective-permute-start(bf16[104,768]{1,0:T(8,128)(2,1)S(1)} %get-tuple-element.327), channel_id=1, source_target_pairs={{0,2},{1,3},{2,0},{3,1},{4,6},{5,7},{6,4},{7,5},{8,10},{9,11},{10,... | collective-permute-start | bytes 479240 | tf_op jit(solution)/shard_map/ppermute | solution.py:538
  190.8 4.3 %collective-permute-done.48 = bf16[104,768]{1,0:T(8,128)(2,1)S(1)} collective-permute-done((bf16[104,768]{1,0:T(8,128)(2,1)S(1)}, bf16[104,768]{1,0:T(8,128)(2,1)S(1)}, u32[]{:S(2)}, u32[]{:S(2)}) %collective-permute-start.48) | collective-permute-done | bytes 159776 | tf_op jit(solution)/shard_map/ppermute | solution.py:538
  197.8 5.5 %collective-permute-start.62 = (bf16[4,96,768]{2,1,0:T(8,128)(2,1)S(1)}, bf16[4,96,768]{2,1,0:T(8,128)(2,1)S(1)}, u32[]{:S(2)}, u32[]{:S(2)}) collective-permute-start(bf16[4,96,768]{2,1,0:T(8,128)(2,1)S(1)} %pad_maximum_fusion.5.four), channel_id=1, source_target_pairs={{0,4},{4,0},{8,12},{12,8},{16,20},{20,16},{24,28},{28,24},{1,5},{5... | collective-permute-start | bytes 1769480 | tf_op jit(solution)/shard_map/ppermute | solution.py:541
  203.4 4.0 %collective-permute-start.63 = (bf16[4,96,768]{2,1,0:T(8,128)(2,1)S(1)}, bf16[4,96,768]{2,1,0:T(8,128)(2,1)S(1)}, u32[]{:S(2)}, u32[]{:S(2)}) collective-permute-start(bf16[4,96,768]{2,1,0:T(8,128)(2,1)S(1)} %pad_maximum_fusion.6.four), channel_id=1, source_target_pairs={{0,4},{4,0},{8,12},{12,8},{16,20},{20,16},{24,28},{28,24},{1,5},{5... | collective-permute-start | bytes 1769480 | tf_op jit(solution)/shard_map/ppermute | solution.py:541
  214.3 3.7 %collective-permute-done.60 = bf16[104,768]{1,0:T(8,128)(2,1)S(1)} collective-permute-done((bf16[104,768]{1,0:T(8,128)(2,1)S(1)}, bf16[104,768]{1,0:T(8,128)(2,1)S(1)}, u32[]{:S(2)}, u32[]{:S(2)}) %collective-permute-start.60) | collective-permute-done | bytes 159776 | tf_op jit(solution)/shard_map/ppermute | solution.py:541
  (217 shorter events, 85.3 us)
Async XLA Ops:
  3.1 12.6 %collective-permute-start.1 = (bf16[104,768]{1,0:T(8,128)(2,1)}, bf16[104,768]{1,0:T(8,128)(2,1)S(1)}, u32[]{:S(2)}, u32[]{:S(2)}) collective-permute-start(bf16[104,768]{1,0:T(8,128)(2,1)} %get-tuple-element.165.bias_0), channel_id=1, source_target_pairs={{0,2},{1,3},{2,0},{3,1},{4,6},{5,7},{6,4},{7,5},{8,10},{9,11},{10,... | collective-permute-start | bytes 479240 | tf_op jit(solution)/shard_map/ppermute | solution.py:538
  5.6 13.7 %collective-permute-start = (bf16[104,768]{1,0:T(8,128)(2,1)}, bf16[104,768]{1,0:T(8,128)(2,1)S(1)}, u32[]{:S(2)}, u32[]{:S(2)}) collective-permute-start(bf16[104,768]{1,0:T(8,128)(2,1)} %get-tuple-element.165.bias_0), channel_id=1, source_target_pairs={{0,1},{1,2},{2,3},{3,0},{4,5},{5,6},{6,7},{7,4},{8,9},{9,10},{10,1... | collective-permute-start | bytes 479240 | tf_op jit(solution)/shard_map/ppermute | solution.py:538
  20.5 19.4 %collective-permute-start.6 = (bf16[288,768]{1,0:T(8,128)(2,1)}, bf16[288,768]{1,0:T(8,128)(2,1)S(1)}, u32[]{:S(2)}, u32[]{:S(2)}) collective-permute-start(bf16[288,768]{1,0:T(8,128)(2,1)} %pad_maximum_fusion.7), channel_id=1, source_target_pairs={{0,1},{1,2},{2,3},{3,0},{4,5},{5,6},{6,7},{7,4},{8,9},{9,10},{10,1... | collective-permute-start | bytes 1327112 | tf_op jit(solution)/shard_map/ppermute | solution.py:538
  21.5 18.3 %collective-permute-start.5 = (bf16[3,96,768]{2,1,0:T(8,128)(2,1)S(1)}, bf16[3,96,768]{2,1,0:T(8,128)(2,1)S(1)}, u32[]{:S(2)}, u32[]{:S(2)}) collective-permute-start(bf16[3,96,768]{2,1,0:T(8,128)(2,1)S(1)} %pad_maximum_fusion.8), channel_id=1, source_target_pairs={{0,24},{4,28},{8,16},{12,20},{16,8},{20,12},{24,0},{28,4},{1,25},{... | collective-permute-start | bytes 1327112 | tf_op jit(solution)/shard_map/ppermute | solution.py:541
  23.7 20.3 %collective-permute-start.4 = (bf16[3,96,768]{2,1,0:T(8,128)(2,1)S(1)}, bf16[3,96,768]{2,1,0:T(8,128)(2,1)S(1)}, u32[]{:S(2)}, u32[]{:S(2)}) collective-permute-start(bf16[3,96,768]{2,1,0:T(8,128)(2,1)S(1)} %pad_maximum_fusion.8), channel_id=1, source_target_pairs={{0,16},{4,20},{8,24},{12,28},{16,0},{20,4},{24,8},{28,12},{1,17},{... | collective-permute-start | bytes 1327112 | tf_op jit(solution)/shard_map/ppermute | solution.py:541
  23.9 20.1 %collective-permute-start.3 = (bf16[3,96,768]{2,1,0:T(8,128)(2,1)S(1)}, bf16[3,96,768]{2,1,0:T(8,128)(2,1)S(1)}, u32[]{:S(2)}, u32[]{:S(2)}) collective-permute-start(bf16[3,96,768]{2,1,0:T(8,128)(2,1)S(1)} %pad_maximum_fusion.8), channel_id=1, source_target_pairs={{0,8},{4,12},{8,0},{12,4},{16,24},{20,28},{24,16},{28,20},{1,9},{5... | collective-permute-start | bytes 1327112 | tf_op jit(solution)/shard_map/ppermute | solution.py:541
  44.9 23.2 %collective-permute-start.12 = (bf16[288,768]{1,0:T(8,128)(2,1)}, bf16[288,768]{1,0:T(8,128)(2,1)}, u32[]{:S(2)}, u32[]{:S(2)}) collective-permute-start(bf16[288,768]{1,0:T(8,128)(2,1)} %pad_maximum_fusion.7), channel_id=1, source_target_pairs={{0,2},{1,3},{2,0},{3,1},{4,6},{5,7},{6,4},{7,5},{8,10},{9,11},{10,... | collective-permute-start | bytes 1327112 | tf_op jit(solution)/shard_map/ppermute | solution.py:538
  46.2 22.0 %collective-permute-start.9 = (bf16[2,192,768]{2,1,0:T(8,128)(2,1)S(1)}, bf16[2,192,768]{2,1,0:T(8,128)(2,1)}, u32[]{:S(2)}, u32[]{:S(2)}) collective-permute-start(bf16[2,192,768]{2,1,0:T(8,128)(2,1)S(1)} %pad_maximum_fusion.2.left), channel_id=1, source_target_pairs={{0,8},{4,12},{8,0},{12,4},{16,24},{20,28},{24,16},{28,20},{1,9},{5... | collective-permute-start | bytes 1769480 | tf_op jit(solution)/shard_map/ppermute | solution.py:541
  48.3 20.9 %collective-permute-start.10 = (bf16[2,192,768]{2,1,0:T(8,128)(2,1)}, bf16[2,192,768]{2,1,0:T(8,128)(2,1)}, u32[]{:S(2)}, u32[]{:S(2)}) collective-permute-start(bf16[2,192,768]{2,1,0:T(8,128)(2,1)} %pad_maximum_fusion.3.right), channel_id=1, source_target_pairs={{0,16},{4,20},{8,24},{12,28},{16,0},{20,4},{24,8},{28,12},{1,17},{... | collective-permute-start | bytes 1769480 | tf_op jit(solution)/shard_map/ppermute | solution.py:541
  49.6 18.6 %collective-permute-start.11 = (bf16[2,96,768]{2,1,0:T(8,128)(2,1)}, bf16[2,96,768]{2,1,0:T(8,128)(2,1)}, u32[]{:S(2)}, u32[]{:S(2)}) collective-permute-start(bf16[2,96,768]{2,1,0:T(8,128)(2,1)} %pad_maximum_fusion.9), channel_id=1, source_target_pairs={{0,24},{4,28},{8,16},{12,20},{16,8},{20,12},{24,0},{28,4},{1,25},{... | collective-permute-start | bytes 884744 | tf_op jit(solution)/shard_map/ppermute | solution.py:541
  73.8 12.6 %collective-permute-start.19 = (bf16[1,192,768]{2,1,0:T(8,128)(2,1)S(1)}, bf16[1,192,768]{2,1,0:T(8,128)(2,1)S(1)}, u32[]{:S(2)}, u32[]{:S(2)}) collective-permute-start(bf16[1,192,768]{2,1,0:T(8,128)(2,1)S(1)} %get-tuple-element.189.right), channel_id=1, source_target_pairs={{0,16},{4,20},{8,24},{12,28},{16,0},{20,4},{24,8},{28,12},{1,17},{... | collective-permute-start | bytes 884744 | tf_op jit(solution)/shard_map/ppermute | solution.py:541
  108.7 14.9 %collective-permute-start.27 = (bf16[4,96,768]{2,1,0:T(8,128)(2,1)S(1)}, bf16[4,96,768]{2,1,0:T(8,128)(2,1)S(1)}, u32[]{:S(2)}, u32[]{:S(2)}) collective-permute-start(bf16[4,96,768]{2,1,0:T(8,128)(2,1)S(1)} %get-tuple-element.201), channel_id=1, source_target_pairs={{0,8},{4,12},{8,0},{12,4},{16,24},{20,28},{24,16},{28,20},{1,9},{5... | collective-permute-start | bytes 1769480 | tf_op jit(solution)/shard_map/ppermute | solution.py:541
  109.0 14.7 %collective-permute-start.28 = (bf16[4,96,768]{2,1,0:T(8,128)(2,1)S(1)}, bf16[4,96,768]{2,1,0:T(8,128)(2,1)S(1)}, u32[]{:S(2)}, u32[]{:S(2)}) collective-permute-start(bf16[4,96,768]{2,1,0:T(8,128)(2,1)S(1)} %get-tuple-element.202), channel_id=1, source_target_pairs={{0,16},{4,20},{8,24},{12,28},{16,0},{20,4},{24,8},{28,12},{1,17},{... | collective-permute-start | bytes 1769480 | tf_op jit(solution)/shard_map/ppermute | solution.py:541
  124.7 15.8 %collective-permute-start.31 = (bf16[2,4,96,384]{3,2,1,0:T(8,128)(2,1)S(1)}, bf16[2,4,96,384]{3,2,1,0:T(8,128)(2,1)S(1)}, u32[]{:S(2)}, u32[]{:S(2)}) collective-permute-start(bf16[2,4,96,384]{3,2,1,0:T(8,128)(2,1)S(1)} %get-tuple-element.241), channel_id=1, source_target_pairs={{0,8},{4,12},{8,0},{12,4},{16,24},{20,28},{24,16},{28,20},{1,9},{5... | collective-permute-start | bytes 1769480 | tf_op jit(solution)/shard_map/ppermute | solution.py:541
  125.9 14.6 %collective-permute-start.32 = (bf16[2,4,96,384]{3,2,1,0:T(8,128)(2,1)S(1)}, bf16[2,4,96,384]{3,2,1,0:T(8,128)(2,1)S(1)}, u32[]{:S(2)}, u32[]{:S(2)}) collective-permute-start(bf16[2,4,96,384]{3,2,1,0:T(8,128)(2,1)S(1)} %get-tuple-element.242), channel_id=1, source_target_pairs={{0,16},{4,20},{8,24},{12,28},{16,0},{20,4},{24,8},{28,12},{1,17},{... | collective-permute-start | bytes 1769480 | tf_op jit(solution)/shard_map/ppermute | solution.py:541
  127.4 13.2 %collective-permute-start.35 = (bf16[96,768]{1,0:T(8,128)(2,1)S(1)}, bf16[96,768]{1,0:T(8,128)(2,1)S(1)}, u32[]{:S(2)}, u32[]{:S(2)}) collective-permute-start(bf16[96,768]{1,0:T(8,128)(2,1)S(1)} %get-tuple-element.335), channel_id=1, source_target_pairs={{0,1},{1,2},{2,3},{3,0},{4,5},{5,6},{6,7},{7,4},{8,9},{9,10},{10,1... | collective-permute-start | bytes 442376 | tf_op jit(solution)/shard_map/ppermute | solution.py:538
  127.9 12.7 %collective-permute-start.34 = (bf16[96,768]{1,0:T(8,128)(2,1)S(1)}, bf16[96,768]{1,0:T(8,128)(2,1)S(1)}, u32[]{:S(2)}, u32[]{:S(2)}) collective-permute-start(bf16[96,768]{1,0:T(8,128)(2,1)S(1)} %get-tuple-element.336), channel_id=1, source_target_pairs={{0,2},{1,3},{2,0},{3,1},{4,6},{5,7},{6,4},{7,5},{8,10},{9,11},{10,... | collective-permute-start | bytes 442376 | tf_op jit(solution)/shard_map/ppermute | solution.py:538
  146.9 12.4 %collective-permute-start.42 = (bf16[96,768]{1,0:T(8,128)(2,1)S(1)}, bf16[96,768]{1,0:T(8,128)(2,1)S(1)}, u32[]{:S(2)}, u32[]{:S(2)}) collective-permute-start(bf16[96,768]{1,0:T(8,128)(2,1)S(1)} %get-tuple-element.332), channel_id=1, source_target_pairs={{0,2},{1,3},{2,0},{3,1},{4,6},{5,7},{6,4},{7,5},{8,10},{9,11},{10,... | collective-permute-start | bytes 442376 | tf_op jit(solution)/shard_map/ppermute | solution.py:538
  148.1 13.6 %collective-permute-start.41 = (bf16[96,768]{1,0:T(8,128)(2,1)S(1)}, bf16[96,768]{1,0:T(8,128)(2,1)S(1)}, u32[]{:S(2)}, u32[]{:S(2)}) collective-permute-start(bf16[96,768]{1,0:T(8,128)(2,1)S(1)} %get-tuple-element.333), channel_id=1, source_target_pairs={{0,3},{1,0},{2,1},{3,2},{4,7},{5,4},{6,5},{7,6},{8,11},{9,8},{10,9... | collective-permute-start | bytes 442376 | tf_op jit(solution)/shard_map/ppermute | solution.py:538
  154.7 17.2 %collective-permute-start.39 = (bf16[2,4,104,384]{3,2,1,0:T(8,128)(2,1)S(1)}, bf16[2,4,104,384]{3,2,1,0:T(8,128)(2,1)S(1)}, u32[]{:S(2)}, u32[]{:S(2)}) collective-permute-start(bf16[2,4,104,384]{3,2,1,0:T(8,128)(2,1)S(1)} %get-tuple-element.250), channel_id=1, source_target_pairs={{0,8},{4,12},{8,0},{12,4},{16,24},{20,28},{24,16},{28,20},{1,9},{5... | collective-permute-start | bytes 1916936 | tf_op jit(solution)/shard_map/ppermute | solution.py:541
  155.3 16.6 %collective-permute-start.40 = (bf16[2,4,104,384]{3,2,1,0:T(8,128)(2,1)S(1)}, bf16[2,4,104,384]{3,2,1,0:T(8,128)(2,1)S(1)}, u32[]{:S(2)}, u32[]{:S(2)}) collective-permute-start(bf16[2,4,104,384]{3,2,1,0:T(8,128)(2,1)S(1)} %get-tuple-element.251), channel_id=1, source_target_pairs={{0,16},{4,20},{8,24},{12,28},{16,0},{20,4},{24,8},{28,12},{1,17},{... | collective-permute-start | bytes 1916936 | tf_op jit(solution)/shard_map/ppermute | solution.py:541
  183.5 14.3 %collective-permute-start.55 = (bf16[104,768]{1,0:T(8,128)(2,1)S(1)}, bf16[104,768]{1,0:T(8,128)(2,1)S(1)}, u32[]{:S(2)}, u32[]{:S(2)}) collective-permute-start(bf16[104,768]{1,0:T(8,128)(2,1)S(1)} %get-tuple-element.325), channel_id=1, source_target_pairs={{0,1},{1,2},{2,3},{3,0},{4,5},{5,6},{6,7},{7,4},{8,9},{9,10},{10,1... | collective-permute-start | bytes 479240 | tf_op jit(solution)/shard_map/ppermute | solution.py:538
  185.9 17.4 %collective-permute-start.54 = (bf16[104,768]{1,0:T(8,128)(2,1)S(1)}, bf16[104,768]{1,0:T(8,128)(2,1)S(1)}, u32[]{:S(2)}, u32[]{:S(2)}) collective-permute-start(bf16[104,768]{1,0:T(8,128)(2,1)S(1)} %get-tuple-element.327), channel_id=1, source_target_pairs={{0,2},{1,3},{2,0},{3,1},{4,6},{5,7},{6,4},{7,5},{8,10},{9,11},{10,... | collective-permute-start | bytes 479240 | tf_op jit(solution)/shard_map/ppermute | solution.py:538
  197.8 12.4 %collective-permute-start.62 = (bf16[4,96,768]{2,1,0:T(8,128)(2,1)S(1)}, bf16[4,96,768]{2,1,0:T(8,128)(2,1)S(1)}, u32[]{:S(2)}, u32[]{:S(2)}) collective-permute-start(bf16[4,96,768]{2,1,0:T(8,128)(2,1)S(1)} %pad_maximum_fusion.5.four), channel_id=1, source_target_pairs={{0,4},{4,0},{8,12},{12,8},{16,20},{20,16},{24,28},{28,24},{1,5},{5... | collective-permute-start | bytes 1769480 | tf_op jit(solution)/shard_map/ppermute | solution.py:541
  (65 other events, 606.9 us)
